TPU v7x, 32 devices: a whole 2x2x4 slice. The times are simulated.
32 devices in a mesh: dp: 8 (over y, x, core), seq: 4 (over z).
Axes of the slice: x: 2, y: 2, z: 4, core: 2. Of those that a mesh axis runs over, the one named last changes fastest.
Arguments:
- tokens: bfloat16 [8, 1024, 1024], P('dp', 'seq'), may hold values from -6 to 6
- encoded: bfloat16 [8, 512, 1024], P('dp', 'seq'), may hold values from -6 to 6
- cotangent: bfloat16 [8, 1024, 1024], P('dp', 'seq'), may hold values from -6 to 6
- doc_ids: int32 [8, 1024], P('dp'), may hold values from 0 to 2, as said below
- block_ids: int32 [8, 1024], P('dp'), may hold values from 0 to 7, never falling along the last dimension, each value on 1 to 256 neighbouring positions
- query_weight: float32 [1024, 1024], P(('dp', 'seq')), may hold values from -0.1875 to 0.1875
- key_weight: float32 [1024, 1024], P(('dp', 'seq')), may hold values from -0.1875 to 0.1875
- value_weight: float32 [1024, 1024], P(('dp', 'seq')), may hold values from -0.1875 to 0.1875
- out_weight: float32 [1024, 1024], P(('dp', 'seq')), may hold values from -0.75 to 0.75
- query_bias: float32 [1024], P(('dp', 'seq')), may hold values from -3 to 3
- value_bias: float32 [1024], P(('dp', 'seq')), may hold values from -3 to 3
- out_bias: float32 [1024], P(('dp', 'seq')), may hold values from -3 to 3
- first_gain: float32 [1024], P(('dp', 'seq')), may hold values from 0.1 to 1.9
- first_shift: float32 [1024], P(('dp', 'seq')), may hold values from -3 to 3
- probe_weight: float32 [1024, 1024], P(('dp', 'seq')), may hold values from -0.1875 to 0.1875
- lookup_weight: float32 [1024, 1024], P(('dp', 'seq')), may hold values from -0.1875 to 0.1875
- content_weight: float32 [1024, 1024], P(('dp', 'seq')), may hold values from -0.1875 to 0.1875
- merge_weight: float32 [1024, 1024], P(('dp', 'seq')), may hold values from -0.75 to 0.75
- probe_bias: float32 [1024], P(('dp', 'seq')), may hold values from -3 to 3
- content_bias: float32 [1024], P(('dp', 'seq')), may hold values from -3 to 3
- merge_bias: float32 [1024], P(('dp', 'seq')), may hold values from -3 to 3
- second_gain: float32 [1024], P(('dp', 'seq')), may hold values from 0.1 to 1.9
- second_shift: float32 [1024], P(('dp', 'seq')), may hold values from -3 to 3
- expand_weight: float32 [1024, 4096], P(('dp', 'seq')), may hold values from -0.1875 to 0.1875
- expand_bias: float32 [4096], P(('dp', 'seq')), may hold values from -3 to 3
- reduce_weight: float32 [4096, 1024], P(('dp', 'seq')), may hold values from -0.09375 to 0.09375
- reduce_bias: float32 [1024], P(('dp', 'seq')), may hold values from -3 to 3
- third_gain: float32 [1024], P(('dp', 'seq')), may hold values from 0.1 to 1.9
- third_shift: float32 [1024], P(('dp', 'seq')), may hold values from -3 to 3
Outputs:
- output: bfloat16 [8, 1024, 1024], P('dp', 'seq')
- tokens_grad: float32 [8, 1024, 1024], P('dp', 'seq')
- encoded_grad: float32 [8, 512, 1024], P('dp', 'seq')
- query_weight_grad: float32 [1024, 1024], P(('dp', 'seq'))
- key_weight_grad: float32 [1024, 1024], P(('dp', 'seq'))
- value_weight_grad: float32 [1024, 1024], P(('dp', 'seq'))
- out_weight_grad: float32 [1024, 1024], P(('dp', 'seq'))
- query_bias_grad: float32 [1024], P(('dp', 'seq'))
- value_bias_grad: float32 [1024], P(('dp', 'seq'))
- out_bias_grad: float32 [1024], P(('dp', 'seq'))
- first_gain_grad: float32 [1024], P(('dp', 'seq'))
- first_shift_grad: float32 [1024], P(('dp', 'seq'))
- probe_weight_grad: float32 [1024, 1024], P(('dp', 'seq'))
- lookup_weight_grad: float32 [1024, 1024], P(('dp', 'seq'))
- content_weight_grad: float32 [1024, 1024], P(('dp', 'seq'))
- merge_weight_grad: float32 [1024, 1024], P(('dp', 'seq'))
- probe_bias_grad: float32 [1024], P(('dp', 'seq'))
- content_bias_grad: float32 [1024], P(('dp', 'seq'))
- merge_bias_grad: float32 [1024], P(('dp', 'seq'))
- second_gain_grad: float32 [1024], P(('dp', 'seq'))
- second_shift_grad: float32 [1024], P(('dp', 'seq'))
- expand_weight_grad: float32 [1024, 4096], P(('dp', 'seq'))
- expand_bias_grad: float32 [4096], P(('dp', 'seq'))
- reduce_weight_grad: float32 [4096, 1024], P(('dp', 'seq'))
- reduce_bias_grad: float32 [1024], P(('dp', 'seq'))
- third_gain_grad: float32 [1024], P(('dp', 'seq'))
- third_shift_grad: float32 [1024], P(('dp', 'seq'))
Inputs may be any that keep to these rules, and one draw needn't show every extreme that they name: `doc_ids`: along a row the ids never fall; id 1 begins within the first 256 positions and id 2 within the last 256 positions. `block_ids`: along a row the ids never fall and each block holds 1 to 256 tokens.
All inputs are finite; a program needn't handle non-finite values.
Results may differ from a plain program's by a relative error of at most 0.035.
Values may be sent and summed in bfloat16 or wider, within the bound.
A program may use at most 256 MiB of HBM per device.

v0:
```python
import math

import jax
import jax.numpy as jnp
from jax import lax
from jax.sharding import PartitionSpec as P

H = 16
DH = 64


EPS = 1e-05
NEG = -1000000000.0
INV_ROOT_TWO = 0.7071067811865476
DENSITY_CONST = 0.3989422804014327


def matmul(left_arg, right_arg):
    return jnp.dot(left_arg, right_arg, preferred_element_type=jnp.float32)


def left_outer(left_arg, right_arg):
    return lax.dot_general(
        left_arg, right_arg, (((0,), (0,)), ((), ())), preferred_element_type=jnp.float32
    )


def right_trans(left_arg, right_arg):
    return lax.dot_general(
        left_arg, right_arg, (((1,), (1,)), ((), ())), preferred_element_type=jnp.float32
    )


def layer_stats(hidden):
    row_mean = jnp.mean(hidden, axis=-1, keepdims=True)
    centered = hidden - row_mean
    inv_std = lax.rsqrt(jnp.mean(centered * centered, axis=-1, keepdims=True) + EPS)
    return (centered * inv_std, inv_std)


def layer_back(grad_norm, normed, inv_std):
    first_mean = jnp.mean(grad_norm, axis=-1, keepdims=True)
    second_mean = jnp.mean(grad_norm * normed, axis=-1, keepdims=True)
    return inv_std * (grad_norm - first_mean - normed * second_mean)


def head_slice(array, group_index, group_size):
    part = lax.dynamic_slice_in_dim(array, group_index * group_size * DH, group_size * DH, 2)
    return part.reshape(array.shape[0], array.shape[1], group_size, DH)


def regroup(stacked):
    group_count, seq_count, row_count, group_span = stacked.shape
    return jnp.moveaxis(stacked, 0, 2).reshape(seq_count, row_count, group_count * group_span)


def masked_scores(query_part, key_part, allow):
    scores = jnp.einsum("sqhd,skhd->shqk", query_part, key_part, preferred_element_type=jnp.float32)
    if allow is not None:
        scores = jnp.where(allow[:, None], scores, NEG)
    return scores


def attn_forward(queries, keys, values, allow):
    group_size = math.gcd(H, 4)

    def one_group(group_index):
        query_part = head_slice(queries, group_index, group_size)
        key_part = head_slice(keys, group_index, group_size)
        value_part = head_slice(values, group_index, group_size)
        scores = masked_scores(query_part, key_part, allow)
        row_max = jnp.max(scores, axis=-1, keepdims=True)
        expon = jnp.exp(scores - row_max)
        row_total = jnp.sum(expon, axis=-1, keepdims=True)
        probab = (expon / row_total).astype(jnp.bfloat16)
        attended = jnp.einsum(
            "shqk,skhd->sqhd", probab, value_part, preferred_element_type=jnp.float32
        )
        attended = attended.reshape(queries.shape[0], queries.shape[1], group_size * DH)
        return (attended, (row_max + jnp.log(row_total))[..., 0])

    stacked, log_sums = lax.map(one_group, jnp.arange(H // group_size, dtype=jnp.int32))
    return (regroup(stacked), log_sums)


def attn_backward(queries, keys, values, allow, log_sums, grad_attended):
    group_size = math.gcd(H, 4)

    def one_group(items):
        group_index, log_part = items
        query_part = head_slice(queries, group_index, group_size)
        key_part = head_slice(keys, group_index, group_size)
        value_part = head_slice(values, group_index, group_size)
        grad_part = head_slice(grad_attended, group_index, group_size)
        scores = masked_scores(query_part, key_part, allow)
        probab = jnp.exp(scores - log_part[..., None])
        grad_probs = jnp.einsum(
            "sqhd,skhd->shqk", grad_part, value_part, preferred_element_type=jnp.float32
        )
        row_delta = jnp.sum(probab * grad_probs, axis=-1, keepdims=True)
        grad_scores = (probab * (grad_probs - row_delta)).astype(jnp.bfloat16)
        grad_query = jnp.einsum(
            "shqk,skhd->sqhd", grad_scores, key_part, preferred_element_type=jnp.float32
        )
        grad_key = jnp.einsum(
            "shqk,sqhd->skhd", grad_scores, query_part, preferred_element_type=jnp.float32
        )
        grad_value = jnp.einsum(
            "shqk,sqhd->skhd",
            probab.astype(jnp.bfloat16),
            grad_part,
            preferred_element_type=jnp.float32,
        )
        seq_count = queries.shape[0]
        return (
            grad_query.reshape(seq_count, queries.shape[1], group_size * DH),
            grad_key.reshape(seq_count, keys.shape[1], group_size * DH),
            grad_value.reshape(seq_count, keys.shape[1], group_size * DH),
        )

    group_ids = jnp.arange(H // group_size, dtype=jnp.int32)
    grad_queries, grad_keys, grad_values = lax.map(one_group, (group_ids, log_sums))
    return (regroup(grad_queries), regroup(grad_keys), regroup(grad_values))


def local(
    tokens,
    encoded,
    cotangent,
    doc_ids,
    block_ids,
    query_weight,
    key_weight,
    value_weight,
    out_weight,
    query_bias,
    value_bias,
    out_bias,
    first_gain,
    first_shift,
    probe_weight,
    lookup_weight,
    content_weight,
    merge_weight,
    probe_bias,
    content_bias,
    merge_bias,
    second_gain,
    second_shift,
    expand_weight,
    expand_bias,
    reduce_weight,
    reduce_bias,
    third_gain,
    third_shift,
):
    seq_count, local_rows, feat_width = tokens.shape
    enc_local = encoded.shape[1]
    flat_rows = seq_count * local_rows
    scale = DH ** (-0.5)
    (
        query_mat,
        key_mat,
        value_mat,
        out_mat,
        probe_mat,
        lookup_mat,
        content_mat,
        merge_mat,
        expand_mat,
        reduce_mat,
    ) = (
        lax.all_gather(query_weight.astype(jnp.bfloat16), ("dp", "seq"), axis=0, tiled=True),
        lax.all_gather(key_weight.astype(jnp.bfloat16), ("dp", "seq"), axis=0, tiled=True),
        lax.all_gather(value_weight.astype(jnp.bfloat16), ("dp", "seq"), axis=0, tiled=True),
        lax.all_gather(out_weight.astype(jnp.bfloat16), ("dp", "seq"), axis=0, tiled=True),
        lax.all_gather(probe_weight.astype(jnp.bfloat16), ("dp", "seq"), axis=0, tiled=True),
        lax.all_gather(lookup_weight.astype(jnp.bfloat16), ("dp", "seq"), axis=0, tiled=True),
        lax.all_gather(content_weight.astype(jnp.bfloat16), ("dp", "seq"), axis=0, tiled=True),
        lax.all_gather(merge_weight.astype(jnp.bfloat16), ("dp", "seq"), axis=0, tiled=True),
        lax.all_gather(expand_weight.astype(jnp.bfloat16), ("dp", "seq"), axis=0, tiled=True),
        lax.all_gather(reduce_weight.astype(jnp.bfloat16), ("dp", "seq"), axis=0, tiled=True),
    )
    (
        query_vec,
        value_vec,
        out_vec,
        gain_first,
        shift_first,
        probe_vec,
        content_vec,
        merge_vec,
        gain_second,
        shift_second,
        expand_vec,
        reduce_vec,
        gain_third,
        shift_third,
    ) = (
        lax.all_gather(query_bias, ("dp", "seq"), axis=0, tiled=True),
        lax.all_gather(value_bias, ("dp", "seq"), axis=0, tiled=True),
        lax.all_gather(out_bias, ("dp", "seq"), axis=0, tiled=True),
        lax.all_gather(first_gain, ("dp", "seq"), axis=0, tiled=True),
        lax.all_gather(first_shift, ("dp", "seq"), axis=0, tiled=True),
        lax.all_gather(probe_bias, ("dp", "seq"), axis=0, tiled=True),
        lax.all_gather(content_bias, ("dp", "seq"), axis=0, tiled=True),
        lax.all_gather(merge_bias, ("dp", "seq"), axis=0, tiled=True),
        lax.all_gather(second_gain, ("dp", "seq"), axis=0, tiled=True),
        lax.all_gather(second_shift, ("dp", "seq"), axis=0, tiled=True),
        lax.all_gather(expand_bias, ("dp", "seq"), axis=0, tiled=True),
        lax.all_gather(reduce_bias, ("dp", "seq"), axis=0, tiled=True),
        lax.all_gather(third_gain, ("dp", "seq"), axis=0, tiled=True),
        lax.all_gather(third_shift, ("dp", "seq"), axis=0, tiled=True),
    )
    offset = lax.axis_index("seq") * local_rows
    query_doc = lax.dynamic_slice_in_dim(doc_ids, offset, local_rows, 1)
    query_block = lax.dynamic_slice_in_dim(block_ids, offset, local_rows, 1)
    allow = (query_doc[:, :, None] == doc_ids[:, None, :]) & (
        block_ids[:, None, :] <= query_block[:, :, None]
    )
    flat = tokens.reshape(flat_rows, feat_width)
    token_float = flat.astype(jnp.float32)
    queries = ((matmul(flat, query_mat) + query_vec) * scale).astype(jnp.bfloat16)
    keys_local = matmul(flat, key_mat).astype(jnp.bfloat16)
    values_local = (matmul(flat, value_mat) + value_vec).astype(jnp.bfloat16)
    keys_seq = keys_local.reshape(seq_count, local_rows, feat_width)
    values_seq = values_local.reshape(seq_count, local_rows, feat_width)
    all_keys, all_values = (
        lax.all_gather(keys_seq, "seq", axis=1, tiled=True),
        lax.all_gather(values_seq, "seq", axis=1, tiled=True),
    )
    query_seq = queries.reshape(seq_count, local_rows, feat_width)
    self_out, self_logs = attn_forward(query_seq, all_keys, all_values, allow)
    self_outb = self_out.reshape(flat_rows, feat_width).astype(jnp.bfloat16)
    first_sum = token_float + matmul(self_outb, out_mat) + out_vec
    normed_one, inv_one = layer_stats(first_sum)
    stream_one = (normed_one * gain_first + shift_first).astype(jnp.bfloat16)
    probe = ((matmul(stream_one, probe_mat) + probe_vec) * scale).astype(jnp.bfloat16)
    enc_flat = encoded.reshape(seq_count * enc_local, feat_width)
    enc_keys = matmul(enc_flat, lookup_mat).astype(jnp.bfloat16)
    enc_values = (matmul(enc_flat, content_mat) + content_vec).astype(jnp.bfloat16)
    enc_keys_seq = enc_keys.reshape(seq_count, enc_local, feat_width)
    enc_values_seq = enc_values.reshape(seq_count, enc_local, feat_width)
    all_enc_keys, all_enc_values = (
        lax.all_gather(enc_keys_seq, "seq", axis=1, tiled=True),
        lax.all_gather(enc_values_seq, "seq", axis=1, tiled=True),
    )
    probe_seq = probe.reshape(seq_count, local_rows, feat_width)
    cross_out, cross_logs = attn_forward(probe_seq, all_enc_keys, all_enc_values, None)
    cross_outb = cross_out.reshape(flat_rows, feat_width).astype(jnp.bfloat16)
    second_sum = stream_one.astype(jnp.float32) + matmul(cross_outb, merge_mat) + merge_vec
    normed_two, inv_two = layer_stats(second_sum)
    stream_two = (normed_two * gain_second + shift_second).astype(jnp.bfloat16)
    expanded = matmul(stream_two, expand_mat) + expand_vec
    activated = jax.nn.gelu(expanded, approximate=False).astype(jnp.bfloat16)
    third_sum = stream_two.astype(jnp.float32) + matmul(activated, reduce_mat) + reduce_vec
    normed_three, inv_three = layer_stats(third_sum)
    output = (normed_three * gain_third + shift_third).astype(jnp.bfloat16)
    (
        query_mat,
        key_mat,
        value_mat,
        out_mat,
        probe_mat,
        lookup_mat,
        content_mat,
        merge_mat,
        expand_mat,
        reduce_mat,
    ) = (
        lax.all_gather(query_weight.astype(jnp.bfloat16), ("dp", "seq"), axis=0, tiled=True),
        lax.all_gather(key_weight.astype(jnp.bfloat16), ("dp", "seq"), axis=0, tiled=True),
        lax.all_gather(value_weight.astype(jnp.bfloat16), ("dp", "seq"), axis=0, tiled=True),
        lax.all_gather(out_weight.astype(jnp.bfloat16), ("dp", "seq"), axis=0, tiled=True),
        lax.all_gather(probe_weight.astype(jnp.bfloat16), ("dp", "seq"), axis=0, tiled=True),
        lax.all_gather(lookup_weight.astype(jnp.bfloat16), ("dp", "seq"), axis=0, tiled=True),
        lax.all_gather(content_weight.astype(jnp.bfloat16), ("dp", "seq"), axis=0, tiled=True),
        lax.all_gather(merge_weight.astype(jnp.bfloat16), ("dp", "seq"), axis=0, tiled=True),
        lax.all_gather(expand_weight.astype(jnp.bfloat16), ("dp", "seq"), axis=0, tiled=True),
        lax.all_gather(reduce_weight.astype(jnp.bfloat16), ("dp", "seq"), axis=0, tiled=True),
    )
    grad_output = cotangent.reshape(flat_rows, feat_width).astype(jnp.float32)
    g_shift_third = jnp.sum(grad_output, axis=0)
    g_gain_third = jnp.sum(grad_output * normed_three, axis=0)
    grad_three = layer_back(grad_output * gain_third, normed_three, inv_three)
    reduce_rows = grad_three.astype(jnp.bfloat16)
    g_reduce_vec = jnp.sum(grad_three, axis=0)
    g_reduce_mat = left_outer(activated, reduce_rows)
    grad_act = right_trans(reduce_rows, reduce_mat)
    slope = 0.5 * (
        1.0 + jax.scipy.special.erf(expanded * INV_ROOT_TWO)
    ) + expanded * DENSITY_CONST * jnp.exp(-0.5 * expanded * expanded)
    grad_expanded = grad_act * slope
    g_expand_vec = jnp.sum(grad_expanded, axis=0)
    expand_rows = grad_expanded.astype(jnp.bfloat16)
    g_expand_mat = left_outer(stream_two, expand_rows)
    grad_two = grad_three + right_trans(expand_rows, expand_mat)
    g_shift_second = jnp.sum(grad_two, axis=0)
    g_gain_second = jnp.sum(grad_two * normed_two, axis=0)
    grad_second = layer_back(grad_two * gain_second, normed_two, inv_two)
    merge_rows = grad_second.astype(jnp.bfloat16)
    g_merge_vec = jnp.sum(grad_second, axis=0)
    g_merge_mat = left_outer(cross_outb, merge_rows)
    grad_cross = (
        right_trans(merge_rows, merge_mat)
        .astype(jnp.bfloat16)
        .reshape(seq_count, local_rows, feat_width)
    )
    grad_probe, grad_enc_keys, grad_enc_values = attn_backward(
        probe_seq, all_enc_keys, all_enc_values, None, cross_logs, grad_cross
    )
    enc_key_sum, enc_value_sum = (
        lax.psum_scatter(
            grad_enc_keys.astype(jnp.bfloat16), "seq", scatter_dimension=1, tiled=True
        ).astype(jnp.float32),
        lax.psum_scatter(
            grad_enc_values.astype(jnp.bfloat16), "seq", scatter_dimension=1, tiled=True
        ).astype(jnp.float32),
    )
    probe_rows = (
        (grad_probe.astype(jnp.bfloat16).astype(jnp.float32) * scale)
        .astype(jnp.bfloat16)
        .reshape(flat_rows, feat_width)
    )
    g_probe_vec = jnp.sum(probe_rows.astype(jnp.float32), axis=0)
    g_probe_mat = left_outer(stream_one, probe_rows)
    enc_key_rows = enc_key_sum.astype(jnp.bfloat16).reshape(seq_count * enc_local, feat_width)
    enc_value_rows = enc_value_sum.astype(jnp.bfloat16).reshape(seq_count * enc_local, feat_width)
    g_lookup_mat = left_outer(enc_flat, enc_key_rows)
    g_content_mat = left_outer(enc_flat, enc_value_rows)
    g_content_vec = jnp.sum(enc_value_rows.astype(jnp.float32), axis=0)
    encoded_grad = right_trans(enc_key_rows, lookup_mat) + right_trans(enc_value_rows, content_mat)
    grad_one = grad_second + right_trans(probe_rows, probe_mat)
    g_shift_first = jnp.sum(grad_one, axis=0)
    g_gain_first = jnp.sum(grad_one * normed_one, axis=0)
    grad_first = layer_back(grad_one * gain_first, normed_one, inv_one)
    out_rows = grad_first.astype(jnp.bfloat16)
    g_out_vec = jnp.sum(grad_first, axis=0)
    g_out_mat = left_outer(self_outb, out_rows)
    grad_self = (
        right_trans(out_rows, out_mat)
        .astype(jnp.bfloat16)
        .reshape(seq_count, local_rows, feat_width)
    )
    grad_query, grad_keys, grad_values = attn_backward(
        query_seq, all_keys, all_values, allow, self_logs, grad_self
    )
    key_sum, value_sum = (
        lax.psum_scatter(
            grad_keys.astype(jnp.bfloat16), "seq", scatter_dimension=1, tiled=True
        ).astype(jnp.float32),
        lax.psum_scatter(
            grad_values.astype(jnp.bfloat16), "seq", scatter_dimension=1, tiled=True
        ).astype(jnp.float32),
    )
    query_rows = (
        (grad_query.astype(jnp.bfloat16).astype(jnp.float32) * scale)
        .astype(jnp.bfloat16)
        .reshape(flat_rows, feat_width)
    )
    key_rows = key_sum.astype(jnp.bfloat16).reshape(flat_rows, feat_width)
    value_rows = value_sum.astype(jnp.bfloat16).reshape(flat_rows, feat_width)
    g_query_vec = jnp.sum(query_rows.astype(jnp.float32), axis=0)
    g_value_vec = jnp.sum(value_rows.astype(jnp.float32), axis=0)
    g_query_mat = left_outer(flat, query_rows)
    g_key_mat = left_outer(flat, key_rows)
    g_value_mat = left_outer(flat, value_rows)
    tokens_grad = (
        grad_first
        + right_trans(query_rows, query_mat)
        + right_trans(key_rows, key_mat)
        + right_trans(value_rows, value_mat)
    )
    summed = (
        lax.psum_scatter(g_query_mat, ("dp", "seq"), scatter_dimension=0, tiled=True),
        lax.psum_scatter(g_key_mat, ("dp", "seq"), scatter_dimension=0, tiled=True),
        lax.psum_scatter(g_value_mat, ("dp", "seq"), scatter_dimension=0, tiled=True),
        lax.psum_scatter(g_out_mat, ("dp", "seq"), scatter_dimension=0, tiled=True),
        lax.psum_scatter(g_query_vec, ("dp", "seq"), scatter_dimension=0, tiled=True),
        lax.psum_scatter(g_value_vec, ("dp", "seq"), scatter_dimension=0, tiled=True),
        lax.psum_scatter(g_out_vec, ("dp", "seq"), scatter_dimension=0, tiled=True),
        lax.psum_scatter(g_gain_first, ("dp", "seq"), scatter_dimension=0, tiled=True),
        lax.psum_scatter(g_shift_first, ("dp", "seq"), scatter_dimension=0, tiled=True),
        lax.psum_scatter(g_probe_mat, ("dp", "seq"), scatter_dimension=0, tiled=True),
        lax.psum_scatter(g_lookup_mat, ("dp", "seq"), scatter_dimension=0, tiled=True),
        lax.psum_scatter(g_content_mat, ("dp", "seq"), scatter_dimension=0, tiled=True),
        lax.psum_scatter(g_merge_mat, ("dp", "seq"), scatter_dimension=0, tiled=True),
        lax.psum_scatter(g_probe_vec, ("dp", "seq"), scatter_dimension=0, tiled=True),
        lax.psum_scatter(g_content_vec, ("dp", "seq"), scatter_dimension=0, tiled=True),
        lax.psum_scatter(g_merge_vec, ("dp", "seq"), scatter_dimension=0, tiled=True),
        lax.psum_scatter(g_gain_second, ("dp", "seq"), scatter_dimension=0, tiled=True),
        lax.psum_scatter(g_shift_second, ("dp", "seq"), scatter_dimension=0, tiled=True),
        lax.psum_scatter(g_expand_mat, ("dp", "seq"), scatter_dimension=0, tiled=True),
        lax.psum_scatter(g_expand_vec, ("dp", "seq"), scatter_dimension=0, tiled=True),
        lax.psum_scatter(g_reduce_mat, ("dp", "seq"), scatter_dimension=0, tiled=True),
        lax.psum_scatter(g_reduce_vec, ("dp", "seq"), scatter_dimension=0, tiled=True),
        lax.psum_scatter(g_gain_third, ("dp", "seq"), scatter_dimension=0, tiled=True),
        lax.psum_scatter(g_shift_third, ("dp", "seq"), scatter_dimension=0, tiled=True),
    )
    return (
        output.reshape(seq_count, local_rows, feat_width),
        tokens_grad.reshape(seq_count, local_rows, feat_width),
        encoded_grad.reshape(seq_count, enc_local, feat_width),
        summed[0],
        summed[1],
        summed[2],
        summed[3],
        summed[4],
        summed[5],
        summed[6],
        summed[7],
        summed[8],
        summed[9],
        summed[10],
        summed[11],
        summed[12],
        summed[13],
        summed[14],
        summed[15],
        summed[16],
        summed[17],
        summed[18],
        summed[19],
        summed[20],
        summed[21],
        summed[22],
        summed[23],
    )


def solution(mesh):
    return jax.shard_map(
        local,
        mesh=mesh,
        in_specs=(
            P("dp", "seq", None),
            P("dp", "seq", None),
            P("dp", "seq", None),
            P("dp", None),
            P("dp", None),
            P(("dp", "seq"), None),
            P(("dp", "seq"), None),
            P(("dp", "seq"), None),
            P(("dp", "seq"), None),
            P(("dp", "seq")),
            P(("dp", "seq")),
            P(("dp", "seq")),
            P(("dp", "seq")),
            P(("dp", "seq")),
            P(("dp", "seq"), None),
            P(("dp", "seq"), None),
            P(("dp", "seq"), None),
            P(("dp", "seq"), None),
            P(("dp", "seq")),
            P(("dp", "seq")),
            P(("dp", "seq")),
            P(("dp", "seq")),
            P(("dp", "seq")),
            P(("dp", "seq"), None),
            P(("dp", "seq")),
            P(("dp", "seq"), None),
            P(("dp", "seq")),
            P(("dp", "seq")),
            P(("dp", "seq")),
        ),
        out_specs=(
            P("dp", "seq", None),
            P("dp", "seq", None),
            P("dp", "seq", None),
            P(("dp", "seq"), None),
            P(("dp", "seq"), None),
            P(("dp", "seq"), None),
            P(("dp", "seq"), None),
            P(("dp", "seq")),
            P(("dp", "seq")),
            P(("dp", "seq")),
            P(("dp", "seq")),
            P(("dp", "seq")),
            P(("dp", "seq"), None),
            P(("dp", "seq"), None),
            P(("dp", "seq"), None),
            P(("dp", "seq"), None),
            P(("dp", "seq")),
            P(("dp", "seq")),
            P(("dp", "seq")),
            P(("dp", "seq")),
            P(("dp", "seq")),
            P(("dp", "seq"), None),
            P(("dp", "seq")),
            P(("dp", "seq"), None),
            P(("dp", "seq")),
            P(("dp", "seq")),
            P(("dp", "seq")),
        ),
        check_vma=False,
    )
```

profile of v0, /device:TPU:0, one launch (start us, length us, event | category | flops | bytes accessed | tf_op | source)
XLA Modules:
  0.0 3131.8 jit_solution(12351086139852072466)
XLA Ops:
  25.4 43.7 %all-reduce.28 = (f32[1024]{0:T(1024)S(1)}, f32[1024]{0:T(1024)S(1)}, f32[1024]{0:T(1024)S(1)}, f32[1024]{0:T(1024)S(1)}, f32[1024]{0:T(1024)S(1)}, /*index=5*/f...) all-reduce(f32[1024]{0:T(1024)S(1)} %dynamic-update-slice.5, ...), channel_id=1, replica_groups=mesh['dp'=8,'seq'=4] {'dp','seq'}, use_global_device_ids=true, to_apply=%add.5 | all-reduce | flops 12288 | bytes 98304
  73.8 56.1 %all-gather.32.cloned.1.call-done = bf16[1024,1024]{1,0:T(8,128)(2,1)} async-done(((bf16[32,1024]{1,0:T(8,128)(2,1)}), bf16[1024,1024]{1,0:T(8,128)(2,1)}) %all-gather.32.cloned.1.call-update) | async-done | bytes 2097168 | tf_op jit(solution)/shard_map/all_gather | solution.py:178
  132.7 56.0 %all-gather.20.cloned.1.call-done = bf16[1024,1024]{1,0:T(8,128)(2,1)} async-done(((bf16[32,1024]{1,0:T(8,128)(2,1)}), bf16[1024,1024]{1,0:T(8,128)(2,1)}) %all-gather.20.cloned.1.call-update) | async-done | bytes 2097168 | tf_op jit(solution)/shard_map/all_gather | solution.py:175
  192.1 55.4 %all-gather.24.cloned.1.call-done = bf16[1024,1024]{1,0:T(8,128)(2,1)} async-done(((bf16[32,1024]{1,0:T(8,128)(2,1)}), bf16[1024,1024]{1,0:T(8,128)(2,1)}) %all-gather.24.cloned.1.call-update) | async-done | bytes 2097168 | tf_op jit(solution)/shard_map/all_gather | solution.py:174
  254.5 66.3 %all-gather.4 = f32[32,1,128]{2,1,0:T(1,128)S(1)} all-gather(f32[1,1,128]{2,1,0:T(1,128)S(1)} %bitcast.440), channel_id=1, replica_groups=mesh['dp'=8,'seq'=4] {'dp','seq'}, dimensions={0}, use_global_device_ids=true | all-gather | bytes 16896 | tf_op jit(solution)/shard_map/all_gather | solution.py:210
  324.2 10.9 all-gather.44.cloned.1.call-done
  336.5 27.5 all-gather.46.cloned.1.call-done
  366.3 45.3 %all-gather.40.cloned.1.call-done = bf16[1024,1024]{1,0:T(8,128)(2,1)} async-done(((bf16[256,1024]{1,0:T(8,128)(2,1)}), bf16[1024,1024]{1,0:T(8,128)(2,1)}) %all-gather.40.cloned.1.call-update) | async-done | bytes 2097168 | tf_op jit(solution)/shard_map/all_gather | solution.py:230
  414.5 44.0 %all-gather.42.cloned.1.call-done = bf16[1024,1024]{1,0:T(8,128)(2,1)} async-done(((bf16[256,1024]{1,0:T(8,128)(2,1)}), bf16[1024,1024]{1,0:T(8,128)(2,1)}) %all-gather.42.cloned.1.call-update) | async-done | bytes 2097168 | tf_op jit(solution)/shard_map/all_gather | solution.py:229
  458.5 4.0 copy.77
  463.3 30.4 while.64
  493.7 23.4 all-gather.26.cloned.1.call-done
  520.1 55.9 %all-gather.30.cloned.1.call-done = bf16[1024,1024]{1,0:T(8,128)(2,1)} async-done(((bf16[32,1024]{1,0:T(8,128)(2,1)}), bf16[1024,1024]{1,0:T(8,128)(2,1)}) %all-gather.30.cloned.1.call-update) | async-done | bytes 2097168 | tf_op jit(solution)/shard_map/all_gather | solution.py:177
  581.2 19.8 while.62
  601.0 33.7 %all-gather.34.cloned.1.call-done = bf16[1024,1024]{1,0:T(8,128)(2,1)} async-done(((bf16[32,1024]{1,0:T(8,128)(2,1)}), bf16[1024,1024]{1,0:T(8,128)(2,1)}) %all-gather.34.cloned.1.call-update) | async-done | bytes 2097168 | tf_op jit(solution)/shard_map/all_gather | solution.py:180
  637.7 76.8 %all-gather.36.cloned.1.call-done = bf16[1024,4096]{1,0:T(8,128)(2,1)} async-done(((bf16[32,4096]{1,0:T(8,128)(2,1)}), bf16[1024,4096]{1,0:T(8,128)(2,1)}) %all-gather.36.cloned.1.call-update) | async-done | bytes 8388624 | tf_op jit(solution)/shard_map/all_gather | solution.py:181
  714.5 15.5 fusion.20
  730.0 63.3 %all-gather.38.cloned.1.call-done = bf16[4096,1024]{1,0:T(8,128)(2,1)} async-done(((bf16[128,1024]{1,0:T(8,128)(2,1)}), bf16[4096,1024]{1,0:T(8,128)(2,1)}) %all-gather.38.cloned.1.call-update) | async-done | bytes 8388624 | tf_op jit(solution)/shard_map/all_gather | solution.py:182
  793.3 6.5 fusion.94
  802.4 7.6 fusion.95
  817.7 33.2 %while.63 = (s32[]{:T(128)}, bf16[4,1,256,256]{2,3,1,0:T(8,128)(2,1)}, bf16[4,1,512,256]{2,3,1,0:T(8,128)(2,1)}, bf16[4,1,512,256]{2,3,1,0:T(8,128)(2,1)}, s32[4...) while((s32[]{:T(128)}, ...), condition=%wide.region_20.21_spmd, body=%wide.region_18.20_spmd.sunk | while | flops 339213312 | bytes 20862164 | solution.py:122
  852.1 6.1 copy.96
  869.4 71.1 %while.65 = (s32[]{:T(128)}, bf16[4,1,256,256]{2,3,1,0:T(8,128)(2,1)}, bf16[4,1,1024,256]{2,3,1,0:T(8,128)(2,1)}, bf16[4,1,1024,256]{2,3,1,0:T(8,128)(2,1)}, s32...) while((s32[]{:T(128)}, ...), condition=%wide.region_25.26_spmd.clone, body=%wide.region_23.25_spmd.clone.sunk | while | flops 684456960 | bytes 57842960 | solution.py:122
  877.9 4.0 multiply_reduce_fusion.14
  940.5 6.1 copy.94
  956.8 26.3 reduce-scatter.31.cloned.1.call-done
  985.0 4.0 fusion.96
  992.9 5.4 copy.98
  998.4 4.1 fusion.78
  1006.4 5.3 reduce-scatter.43.cloned.1.call-done
  1016.3 5.4 copy.104
  1024.5 5.5 copy.106
  1030.0 26.5 reduce-scatter.29.cloned.1.call-done
  1060.2 5.3 copy.100
  1069.3 5.4 copy.102
  1075.3 9.8 fusion.55
  1087.1 8.1 fusion.84
  1104.2 89.9 %all-reduce.31.cloned.1.call-done = (f32[1024]{0:T(1024)}, f32[1024]{0:T(1024)}, f32[1024]{0:T(1024)}, f32[1024]{0:T(1024)}, f32[1024]{0:T(1024)}, /*index=5*/f3...) async-done(((f32[1024]{0:T(1024)}, f32[1024]{0:T(1024)}, ...) | async-done | bytes 73744
  1213.5 134.1 %reduce-scatter.35.cloned.1.call-done = f32[32,1024]{1,0:T(8,128)} async-done(((f32[1024,1024]{1,0:T(8,128)}), f32[32,1024]{1,0:T(8,128)}) %reduce-scatter.35.cloned.1.call-update) | async-done | bytes 131088 | tf_op jit(solution)/shard_map/reduce_scatter | solution.py:384
  1347.6 149.5 %reduce-scatter.47.cloned.1.call-done = f32[32,1024]{1,0:T(8,128)} async-done(((f32[1024,1024]{1,0:T(8,128)}), f32[32,1024]{1,0:T(8,128)}) %reduce-scatter.47.cloned.1.call-update) | async-done | bytes 131088
  1497.1 149.5 %reduce-scatter.33.cloned.1.call-done = f32[32,1024]{1,0:T(8,128)} async-done(((f32[1024,1024]{1,0:T(8,128)}), f32[32,1024]{1,0:T(8,128)}) %reduce-scatter.33.cloned.1.call-update) | async-done | bytes 131088 | tf_op jit(solution)/shard_map/reduce_scatter | solution.py:378
  1646.6 149.5 %reduce-scatter.37.cloned.1.call-done = f32[32,1024]{1,0:T(8,128)} async-done(((f32[1024,1024]{1,0:T(8,128)}), f32[32,1024]{1,0:T(8,128)}) %reduce-scatter.37.cloned.1.call-update) | async-done | bytes 131088 | tf_op jit(solution)/shard_map/reduce_scatter | solution.py:387
  1796.1 149.1 %reduce-scatter.53.cloned.1.call-done = f32[32,1024]{1,0:T(8,128)} async-done(((f32[1024,1024]{1,0:T(8,128)}), f32[32,1024]{1,0:T(8,128)}) %reduce-scatter.53.cloned.1.call-update) | async-done | bytes 131088
  1945.2 149.5 %reduce-scatter.55.cloned.1.call-done = f32[32,1024]{1,0:T(8,128)} async-done(((f32[1024,1024]{1,0:T(8,128)}), f32[32,1024]{1,0:T(8,128)}) %reduce-scatter.55.cloned.1.call-update) | async-done | bytes 131088
  2094.7 150.5 %reduce-scatter.49.cloned.1.call-done = f32[32,1024]{1,0:T(8,128)} async-done(((f32[1024,1024]{1,0:T(8,128)}), f32[32,1024]{1,0:T(8,128)}) %reduce-scatter.49.cloned.1.call-update) | async-done | bytes 131088
  2245.2 149.6 %reduce-scatter.51.cloned.1.call-done = f32[32,1024]{1,0:T(8,128)} async-done(((f32[1024,1024]{1,0:T(8,128)}), f32[32,1024]{1,0:T(8,128)}) %reduce-scatter.51.cloned.1.call-update) | async-done | bytes 131088
  2394.7 365.2 %reduce-scatter.39.cloned.1.call-done = f32[32,4096]{1,0:T(8,128)} async-done(((f32[1024,4096]{1,0:T(8,128)}), f32[32,4096]{1,0:T(8,128)}) %reduce-scatter.39.cloned.1.call-update) | async-done | bytes 524304 | tf_op jit(solution)/shard_map/reduce_scatter | solution.py:393
  2760.0 365.1 %reduce-scatter.41.cloned.1.call-done = f32[128,1024]{1,0:T(8,128)} async-done(((f32[4096,1024]{1,0:T(8,128)}), f32[128,1024]{1,0:T(8,128)}) %reduce-scatter.41.cloned.1.call-update) | async-done | bytes 524304 | tf_op jit(solution)/shard_map/reduce_scatter | solution.py:395
  (495 shorter events, 284.2 us)
Async XLA Ops:
  7.2 63.8 %copy-start = (bf16[1,128,1024]{2,1,0:T(8,128)(2,1)S(1)}, bf16[1,128,1024]{2,1,0:T(8,128)(2,1)}, u32[]{:S(2)}) copy-start(bf16[1,128,1024]{2,1,0:T(8,128)(2,1)} %param.38) | copy-start | bytes 786436
  7.2 181.6 %copy-start.10 = (bf16[1,256,1024]{2,1,0:T(8,128)(2,1)S(1)}, bf16[1,256,1024]{2,1,0:T(8,128)(2,1)}, u32[]{:S(2)}) copy-start(bf16[1,256,1024]{2,1,0:T(8,128)(2,1)} %param.37) | copy-start | bytes 1572868
  7.2 63.7 %all-gather.28.cloned.1.call-start = ((), (), s32[]{:S(2)}) async-start(), calls=%async_computation.18 | async-start | bytes 2162688 | tf_op jit(solution)/shard_map/all_gather | solution.py:179
  8.9 121.0 %all-gather.32.cloned.1.call-start = ((), (), s32[]{:S(2)}) async-start(), calls=%async_computation.20 | async-start | bytes 2162688 | tf_op jit(solution)/shard_map/all_gather | solution.py:178
  10.5 178.3 %all-gather.20.cloned.1.call-start = ((), (), s32[]{:S(2)}) async-start(), calls=%async_computation.14 | async-start | bytes 2162688 | tf_op jit(solution)/shard_map/all_gather | solution.py:175
  12.1 235.4 %all-gather.24.cloned.1.call-start = ((), (), s32[]{:S(2)}) async-start(), calls=%async_computation.16 | async-start | bytes 2162688 | tf_op jit(solution)/shard_map/all_gather | solution.py:174
  13.8 307.1 %all-gather.22.cloned.1.call-start = ((), (), s32[]{:S(2)}) async-start(), calls=%async_computation.15 | async-start | bytes 2162688 | tf_op jit(solution)/shard_map/all_gather | solution.py:173
  15.4 319.7 %all-gather.44.cloned.1.call-start = ((), (), s32[]{:S(2)}) async-start(), calls=%async_computation.33 | async-start | bytes 1310720 | tf_op jit(solution)/shard_map/all_gather | solution.py:246
  69.2 565.6 %copy-start.43 = (f32[1024]{0:T(1024)}, f32[1024]{0:T(1024)S(1)}, u32[]{:S(2)}) copy-start(f32[1024]{0:T(1024)S(1)} %get-tuple-element.809) | copy-start | bytes 12292
  69.2 724.1 %copy-start.36 = (f32[1024]{0:T(1024)}, f32[1024]{0:T(1024)S(1)}, u32[]{:S(2)}) copy-start(f32[1024]{0:T(1024)S(1)} %get-tuple-element.813) | copy-start | bytes 12292
  69.2 732.0 %copy-start.41 = (f32[1024]{0:T(1024)}, f32[1024]{0:T(1024)S(1)}, u32[]{:S(2)}) copy-start(f32[1024]{0:T(1024)S(1)} %get-tuple-element.816) | copy-start | bytes 12292
  73.7 290.3 %all-gather.46.cloned.1.call-start = ((), (), s32[]{:S(2)}) async-start(), calls=%async_computation.34 | async-start | bytes 1310720 | tf_op jit(solution)/shard_map/all_gather | solution.py:245
  132.7 279.0 %all-gather.40.cloned.1.call-start = ((), (), s32[]{:S(2)}) async-start(), calls=%async_computation.31 | async-start | bytes 2621440 | tf_op jit(solution)/shard_map/all_gather | solution.py:230
  188.8 61.9 %copy-start.38 = (f32[32,1024]{1,0:T(8,128)S(1)}, f32[32,1024]{1,0:T(8,128)}, u32[]{:S(2)}) copy-start(f32[32,1024]{1,0:T(8,128)} %param.45) | copy-start | bytes 393220
  188.8 62.6 %copy-start.39 = (f32[32,1024]{1,0:T(8,128)S(1)}, f32[32,1024]{1,0:T(8,128)}, u32[]{:S(2)}) copy-start(f32[32,1024]{1,0:T(8,128)} %param.51) | copy-start | bytes 393220
  188.8 63.3 %copy-start.40 = (f32[32,1024]{1,0:T(8,128)S(1)}, f32[32,1024]{1,0:T(8,128)}, u32[]{:S(2)}) copy-start(f32[32,1024]{1,0:T(8,128)} %param.54) | copy-start | bytes 393220
  188.8 64.1 %copy-start.32 = (f32[32,4096]{1,0:T(8,128)S(1)}, f32[32,4096]{1,0:T(8,128)}, u32[]{:S(2)}) copy-start(f32[32,4096]{1,0:T(8,128)} %param.60) | copy-start | bytes 1572868
  188.8 64.9 %copy-start.33 = (f32[128,1024]{1,0:T(8,128)S(1)}, f32[128,1024]{1,0:T(8,128)}, u32[]{:S(2)}) copy-start(f32[128,1024]{1,0:T(8,128)} %param.62) | copy-start | bytes 1572868
  192.0 62.5 %copy-start.50 = (f32[128]{0:T(128)S(1)}, f32[128]{0:T(128)}, u32[]{:S(2)}) copy-start(f32[128]{0:T(128)} %param.61) | copy-start | bytes 1540
  192.0 128.8 %copy-start.34 = (s32[1,1024]{1,0:T(1,128)S(1)}, s32[1,1024]{1,0:T(1,128)}, u32[]{:S(2)}) copy-start(s32[1,1024]{1,0:T(1,128)} %param.40) | copy-start | bytes 12292
  192.0 128.8 %copy-start.35 = (s32[1,1024]{1,0:T(1,128)S(1)}, s32[1,1024]{1,0:T(1,128)}, u32[]{:S(2)}) copy-start(s32[1,1024]{1,0:T(1,128)} %param.41) | copy-start | bytes 12292
  192.1 266.5 %all-gather.42.cloned.1.call-start = ((), (), s32[]{:S(2)}) async-start(), calls=%async_computation.32 | async-start | bytes 2621440 | tf_op jit(solution)/shard_map/all_gather | solution.py:229
  250.6 266.5 %all-gather.26.cloned.1.call-start = ((), (), s32[]{:S(2)}) async-start(), calls=%async_computation.17 | async-start | bytes 2162688 | tf_op jit(solution)/shard_map/all_gather | solution.py:176
  251.3 324.7 %all-gather.30.cloned.1.call-start = ((), (), s32[]{:S(2)}) async-start(), calls=%async_computation.19 | async-start | bytes 2162688 | tf_op jit(solution)/shard_map/all_gather | solution.py:177
  252.1 382.6 %all-gather.34.cloned.1.call-start = ((), (), s32[]{:S(2)}) async-start(), calls=%async_computation.21 | async-start | bytes 2162688 | tf_op jit(solution)/shard_map/all_gather | solution.py:180
  252.8 461.7 %all-gather.36.cloned.1.call-start = ((), (), s32[]{:S(2)}) async-start(), calls=%async_computation.22 | async-start | bytes 8650752 | tf_op jit(solution)/shard_map/all_gather | solution.py:181
  253.6 539.7 %all-gather.38.cloned.1.call-start = ((), (), s32[]{:S(2)}) async-start(), calls=%async_computation.23 | async-start | bytes 8650752 | tf_op jit(solution)/shard_map/all_gather | solution.py:182
  254.4 699.9 %reduce-scatter.45.cloned.1.call-start = ((), (), s32[]{:S(2)}) async-start(), calls=%async_computation.36 | async-start | bytes 1310720
  861.2 121.9 %reduce-scatter.31.cloned.1.call-start = ((), (), s32[]{:S(2)}) async-start(), calls=%async_computation.25 | async-start | bytes 2621440 | tf_op jit(solution)/shard_map/reduce_scatter | solution.py:352
  940.5 71.2 %reduce-scatter.43.cloned.1.call-start = ((), (), s32[]{:S(2)}) async-start(), calls=%async_computation.35 | async-start | bytes 1310720
  949.6 35.5 %copy-start.44 = (f32[1024]{0:T(1024)S(1)}, f32[1024]{0:T(1024)}, u32[]{:S(2)}) copy-start(f32[1024]{0:T(1024)} %copy-done.43) | copy-start | bytes 12292
  949.6 106.9 %reduce-scatter.29.cloned.1.call-start = ((), (), s32[]{:S(2)}) async-start(), calls=%async_computation.24 | async-start | bytes 2621440 | tf_op jit(solution)/shard_map/reduce_scatter | solution.py:349
  950.2 243.9 %all-reduce.31.cloned.1.call-start = ((), (), s32[]{:S(2)}) async-start(), calls=%async_computation.42 | async-start | bytes 147456
  956.0 65.8 %copy-start.23 = (bf16[1,128,1024]{1,2,0:T(8,128)(2,1)}, bf16[1,128,1024]{1,2,0:T(8,128)(2,1)S(1)}, u32[]{:S(2)}) copy-start(bf16[1,128,1024]{1,2,0:T(8,128)(2,1)S(1)} %copy.97) | copy-start | bytes 786436
  985.0 362.6 %reduce-scatter.35.cloned.1.call-start = ((), (), s32[]{:S(2)}) async-start(), calls=%async_computation.27 | async-start | bytes 4325376 | tf_op jit(solution)/shard_map/reduce_scatter | solution.py:384
  989.1 508.0 %reduce-scatter.47.cloned.1.call-start = ((), (), s32[]{:S(2)}) async-start(), calls=%async_computation.37 | async-start | bytes 4325376
  998.3 648.3 %reduce-scatter.33.cloned.1.call-start = ((), (), s32[]{:S(2)}) async-start(), calls=%async_computation.26 | async-start | bytes 4325376 | tf_op jit(solution)/shard_map/reduce_scatter | solution.py:378
  1002.5 793.6 %reduce-scatter.37.cloned.1.call-start = ((), (), s32[]{:S(2)}) async-start(), calls=%async_computation.28 | async-start | bytes 4325376 | tf_op jit(solution)/shard_map/reduce_scatter | solution.py:387
  1006.3 938.9 %reduce-scatter.53.cloned.1.call-start = ((), (), s32[]{:S(2)}) async-start(), calls=%async_computation.40 | async-start | bytes 4325376
  1021.8 1072.9 %reduce-scatter.55.cloned.1.call-start = ((), (), s32[]{:S(2)}) async-start(), calls=%async_computation.41 | async-start | bytes 4325376
  1029.9 1215.2 %reduce-scatter.49.cloned.1.call-start = ((), (), s32[]{:S(2)}) async-start(), calls=%async_computation.38 | async-start | bytes 4325376
  1065.6 1329.2 %reduce-scatter.51.cloned.1.call-start = ((), (), s32[]{:S(2)}) async-start(), calls=%async_computation.39 | async-start | bytes 4325376
  1074.7 1685.3 %reduce-scatter.39.cloned.1.call-start = ((), (), s32[]{:S(2)}) async-start(), calls=%async_computation.29 | async-start | bytes 17301504 | tf_op jit(solution)/shard_map/reduce_scatter | solution.py:393
  1085.2 2039.8 %reduce-scatter.41.cloned.1.call-start = ((), (), s32[]{:S(2)}) async-start(), calls=%async_computation.30 | async-start | bytes 17301504 | tf_op jit(solution)/shard_map/reduce_scatter | solution.py:395
  1101.7 110.1 %copy-start.4 = (f32[256,1024]{1,0:T(8,128)S(1)}, f32[256,1024]{1,0:T(8,128)}, u32[]{:S(2)}) copy-start(f32[256,1024]{1,0:T(8,128)} %copy-done.3) | copy-start | bytes 3145732
  1101.7 110.1 %copy-start.42 = (f32[1024]{0:T(1024)S(1)}, f32[1024]{0:T(1024)}, u32[]{:S(2)}) copy-start(f32[1024]{0:T(1024)} %copy-done.41) | copy-start | bytes 12292
  1101.7 110.0 %copy-start.46 = (f32[256]{0:T(256)S(1)}, f32[256]{0:T(256)}, u32[]{:S(2)}) copy-start(f32[256]{0:T(256)} %copy-done.45) | copy-start | bytes 3076
  1101.7 110.0 %copy-start.48 = (f32[256]{0:T(256)S(1)}, f32[256]{0:T(256)}, u32[]{:S(2)}) copy-start(f32[256]{0:T(256)} %copy-done.47) | copy-start | bytes 3076
  (39 other events, 257.8 us)
Sparse Core Ops, SparseCore 0:
  11.6 59.3 all-gather.27
  74.5 55.4 all-gather.31
  133.4 55.3 all-gather.19
  192.1 55.3 all-gather.23
  250.8 55.3 all-gather.21
  308.2 26.7 all-gather.43
  336.6 27.4 all-gather.45
  366.2 45.4 all-gather.39
  413.8 44.6 all-gather.41
  461.9 55.2 all-gather.25
  520.6 55.3 all-gather.29
  579.4 55.3 all-gather.33
  638.2 76.2 all-gather.35
  717.3 75.9 all-gather.37
  861.3 25.7 reduce-scatter.44
  940.6 42.4 reduce-scatter.30
  985.2 26.4 reduce-scatter.42
  1014.0 42.4 reduce-scatter.28
  1062.9 131.0 all-reduce.30
  1196.8 150.7 reduce-scatter.34
  1350.5 146.5 reduce-scatter.46
  1499.9 146.6 reduce-scatter.32
  1649.5 146.5 reduce-scatter.36
  1798.8 146.3 reduce-scatter.52
  1948.1 146.5 reduce-scatter.54
  2097.4 147.7 reduce-scatter.48
  2247.9 146.8 reduce-scatter.50
  2397.6 362.3 reduce-scatter.38
  2762.8 362.1 reduce-scatter.40
where the time goes:
time: 3140 us; the launch traced here: 3130 us
  waiting for transfers between devices  2610 us (83%)
  matrix products  174 us (6%)
  local copies, waits for them, and re-layouts  169 us (5%)
  blocking collectives  110 us (4%)
  other arithmetic  39.4 us (1%)
    unnamed x37, waiting for transfers between devices  844 us
    reduce_scatter x1, waiting for transfers between devices, local(): lax.psum_scatter(g_expand_mat, ('dp', 'seq'), scatter_dimension=0, tiled=...  365 us
    reduce_scatter x1, waiting for transfers between devices, local(): lax.psum_scatter(g_reduce_mat, ('dp', 'seq'), scatter_dimension=0, tiled=...  365 us
    reduce_scatter x1, waiting for transfers between devices, local(): lax.psum_scatter(g_out_mat, ('dp', 'seq'), scatter_dimension=0, tiled=True)  150 us
    reduce_scatter x1, waiting for transfers between devices, local(): lax.psum_scatter(g_merge_mat, ('dp', 'seq'), scatter_dimension=0, tiled=T...  149 us
    reduce_scatter x1, waiting for transfers between devices, local(): lax.psum_scatter(g_probe_mat, ('dp', 'seq'), scatter_dimension=0, tiled=T...  134 us
    unnamed x166, local copies, waits for them, and re-layouts  92.5 us
    all_gather x1, waiting for transfers between devices, local(): lax.all_gather(expand_weight.astype(jnp.bfloat16), ('dp', 'seq'), axis=0,...  76.8 us
  transfers between devices with their start and end apart: 29, of which 27 were waited for; matrix products, arithmetic and copies ran while one was open for 10% of the time, Pallas kernels for 0%

commit v1 on v0

v1 whole, which is shorter than its diff:
```python
import functools
import math

import jax
import jax.numpy as jnp
from jax import lax
from jax.experimental import pallas as pl
from jax.experimental.pallas import tpu as pltpu
from jax.sharding import PartitionSpec as P

H = 16
DH = 64

EPS = 1e-05
NEG = -1000000000.0
INV_ROOT_TWO = 0.7071067811865476
DENSITY_CONST = 0.3989422804014327
MESH = pl.DeviceIdType.MESH
BF = jnp.bfloat16
F32 = jnp.float32


def matmul(left_arg, right_arg):
    return jnp.dot(left_arg, right_arg, preferred_element_type=F32)


def left_outer(left_arg, right_arg):
    return lax.dot_general(
        left_arg, right_arg, (((0,), (0,)), ((), ())), preferred_element_type=F32
    )


def right_trans(left_arg, right_arg):
    return lax.dot_general(
        left_arg, right_arg, (((1,), (1,)), ((), ())), preferred_element_type=F32
    )


def layer_stats(hidden):
    row_mean = jnp.mean(hidden, axis=-1, keepdims=True)
    centered = hidden - row_mean
    inv_std = lax.rsqrt(jnp.mean(centered * centered, axis=-1, keepdims=True) + EPS)
    return (centered * inv_std, inv_std)


def layer_back(grad_norm, normed, inv_std):
    first_mean = jnp.mean(grad_norm, axis=-1, keepdims=True)
    second_mean = jnp.mean(grad_norm * normed, axis=-1, keepdims=True)
    return inv_std * (grad_norm - first_mean - normed * second_mean)


class Cube:
    def __init__(self, mesh):
        self.n_dp = mesh.shape["dp"]
        self.n_seq = mesh.shape["seq"]
        self.dp_bits = self.n_dp.bit_length() - 1
        self.seq_bits = self.n_seq.bit_length() - 1
        assert self.n_dp == 1 << self.dp_bits and self.n_seq == 1 << self.seq_bits
        self.n_dev = self.n_dp * self.n_seq

    def lead(self, full):
        return ((2,) * self.dp_bits if full else ()) + (self.n_seq,)


def bit_of(index, bit):
    return (index // (1 << bit)) % 2


def flipped(index, bit):
    return index + (1 << bit) * (1 - 2 * bit_of(index, bit))


def block_shape(rows, cols):
    if rows % 16 == 0:
        return (rows, cols)
    return (16, rows * cols // 16)


def meet(cube):
    dp, seq = lax.axis_index("dp"), lax.axis_index("seq")
    barrier = pltpu.get_barrier_semaphore()
    for bit in range(cube.dp_bits):
        pl.semaphore_signal(
            barrier, inc=1, device_id=(flipped(dp, bit), seq), device_id_type=MESH
        )
    for bit in range(cube.seq_bits):
        pl.semaphore_signal(
            barrier, inc=1, device_id=(dp, flipped(seq, bit)), device_id_type=MESH
        )
    pl.semaphore_wait(barrier, cube.dp_bits + cube.seq_bits)


def dim_order(cube, variant):
    bits = list(range(1, cube.dp_bits))
    return bits if variant == 0 else bits[::-1]


def gather_kernel(cube, kinds, *refs):
    count = len(kinds)
    ins, outs = refs[:count], refs[count : 2 * count]
    send_sem, recv_sem, local_sem = refs[2 * count :]
    dp, seq = lax.axis_index("dp"), lax.axis_index("seq")
    sends = []

    def region(full, open_bits, fixed, seq_part):
        if not full:
            return (seq_part,)
        places = []
        for bit in reversed(range(cube.dp_bits)):
            if bit in open_bits:
                places.append(slice(None))
            else:
                places.append(fixed.get(bit, bit_of(dp, bit)))
        return tuple(places) + (seq_part,)

    def push(array, slot, place, device):
        copy = pltpu.make_async_remote_copy(
            src_ref=outs[array].at[place],
            dst_ref=outs[array].at[place],
            send_sem=send_sem.at[array, slot],
            recv_sem=recv_sem.at[array, slot],
            device_id=device,
            device_id_type=MESH,
        )
        copy.start()
        sends.append(copy)
        return copy

    own = []
    for array, (full, _) in enumerate(kinds):
        copy = pltpu.make_async_copy(
            ins[array], outs[array].at[region(full, (), {}, seq)], local_sem.at[array]
        )
        copy.start()
        own.append(copy)
    meet(cube)
    latest = own
    for bit in range(cube.seq_bits):
        span = 1 << bit
        started = []
        for array, (full, _) in enumerate(kinds):
            latest[array].wait() if bit == 0 else latest[array].wait_recv()
            place = region(full, (), {}, pl.ds(seq - seq % span, span))
            started.append(push(array, bit, place, (dp, flipped(seq, bit))))
        latest = started
    every = pl.ds(0, cube.n_seq)
    cores = []
    slot = cube.seq_bits
    for stage in range(cube.dp_bits):
        started = []
        for array, (full, variant) in enumerate(kinds):
            if latest[array] is None:
                started.append(None)
                continue
            latest[array].wait_recv()
            if not full:
                started.append(None)
                continue
            order = dim_order(cube, variant)
            if stage < len(order):
                place = region(full, order[:stage], {}, every)
                device = (flipped(dp, order[stage]), seq)
                started.append(push(array, slot + 2 * stage, place, device))
            else:
                started.append(None)
            if stage == 0:
                fresh = region(full, (), {}, every)
            else:
                last = order[stage - 1]
                fresh = region(full, order[: stage - 1], {last: 1 - bit_of(dp, last)}, every)
            cores.append(push(array, slot + 2 * stage + 1, fresh, (flipped(dp, 0), seq)))
        latest = started
    for copy in cores:
        copy.wait_recv()
    for copy in sends:
        copy.wait_send()


def gather_all(cube, arrays, kinds, collective_id):
    outs = [
        jax.ShapeDtypeStruct(cube.lead(full) + array.shape, array.dtype)
        for array, (full, _) in zip(arrays, kinds)
    ]
    slots = cube.seq_bits + 2 * cube.dp_bits
    return pl.pallas_call(
        functools.partial(gather_kernel, cube, kinds),
        out_shape=outs,
        in_specs=[pl.BlockSpec(memory_space=pl.ANY)] * len(arrays),
        out_specs=[pl.BlockSpec(memory_space=pl.ANY)] * len(arrays),
        scratch_shapes=[
            pltpu.SemaphoreType.DMA((len(arrays), slots)),
            pltpu.SemaphoreType.DMA((len(arrays), slots)),
            pltpu.SemaphoreType.DMA((len(arrays),)),
        ],
        compiler_params=pltpu.CompilerParams(
            collective_id=collective_id, has_side_effects=True
        ),
        name="gather_weights",
    )(*arrays)


def add_blocks(total, part, places, rows, cols):
    count, pick = places
    step = rows
    while step * cols > 32768 and step % 32 == 0:
        step //= 2
    chunks = rows // step

    def body(index, carry):
        to, of = pick(index // chunks)
        part_rows = pl.ds(pl.multiple_of((index % chunks) * step, step), step)
        left = total[to + (part_rows,)].astype(F32)
        right = part[of + (part_rows,)].astype(F32)
        total[to + (part_rows,)] = (left + right).astype(total.dtype)
        return carry

    lax.fori_loop(0, count * chunks, body, 0)


def scatter_kernel(cube, kinds, *refs):
    count = len(kinds)
    ins, outs = refs[:count], refs[count : 2 * count]
    refs = refs[2 * count :]
    owns, parts = [], []
    for full, _ in kinds:
        stages = (cube.dp_bits if full else 0) + cube.seq_bits
        owns.append(refs[0])
        parts.append(refs[1 : 1 + stages])
        refs = refs[1 + stages :]
    send_sem, recv_sem, local_sem = refs
    dp, seq = lax.axis_index("dp"), lax.axis_index("seq")
    sends = []

    def push(array, stage, source, device):
        copy = pltpu.make_async_remote_copy(
            src_ref=source,
            dst_ref=parts[array][stage],
            send_sem=send_sem.at[array, stage],
            recv_sem=recv_sem.at[array, stage],
            device_id=device,
            device_id_type=MESH,
        )
        copy.start()
        sends.append(copy)
        return copy

    def dims(fixed, kept):
        return tuple(
            fixed[bit] if bit in fixed else kept for bit in reversed(range(1, cube.dp_bits))
        )

    top = cube.seq_bits - 1
    half = cube.n_seq // 2
    local, latest = [], []
    for array, (full, _) in enumerate(kinds):
        if full:
            lead = (slice(None),) * (cube.dp_bits - 1)
            kept = ins[array].at[lead + (bit_of(dp, 0),)]
        else:
            kept = ins[array].at[pl.ds(half * bit_of(seq, top), half)]
        copy = pltpu.make_async_copy(kept, owns[array], local_sem.at[array])
        copy.start()
        local.append(copy)
    meet(cube)
    for array, (full, _) in enumerate(kinds):
        if full:
            lead = (slice(None),) * (cube.dp_bits - 1)
            source = ins[array].at[lead + (1 - bit_of(dp, 0),)]
            device = (flipped(dp, 0), seq)
        else:
            source = ins[array].at[pl.ds(half * (1 - bit_of(seq, top)), half)]
            device = (dp, flipped(seq, top))
        latest.append(push(array, 0, source, device))

    longest = cube.dp_bits + cube.seq_bits
    for stage in range(longest):
        for array, (full, variant) in enumerate(kinds):
            stages = (cube.dp_bits if full else 0) + cube.seq_bits
            if stage >= stages:
                continue
            rows, cols = outs[array].shape
            order = dim_order(cube, variant) if full else []
            own, part = owns[array], parts[array][stage]
            if stage == 0:
                local[array].wait()
            latest[array].wait_recv()
            after = max(stage - (cube.dp_bits - 1), 0) if full else stage + 1
            closed = order[: min(stage, len(order))]
            fixed = {bit: bit_of(dp, bit) for bit in closed}
            open_bits = [
                bit for bit in reversed(range(1, cube.dp_bits)) if full and bit not in closed
            ]
            span = cube.n_seq >> after
            base = seq - seq % span
            if not full:
                base = base - half * bit_of(seq, top)
            if stage == stages - 1:
                where = (dims(fixed, None) if full else ()) + (base,)
                outs[array][...] = own[where].astype(F32) + part[0].astype(F32)
                continue

            def pick(index, full=full, fixed=fixed, open_bits=open_bits, span=span, base=base):
                place = index % span
                rest = index // span
                values = {}
                for bit in reversed(open_bits):
                    values[bit] = rest % 2
                    rest = rest // 2
                of = tuple(values[bit] for bit in open_bits) + (place,)
                to = (dims({**fixed, **values}, None) if full else ()) + (base + place,)
                return to, of

            amount = span * (1 << len(open_bits))
            add_blocks(own, part, (amount, pick), rows, cols)
            if full and stage < len(order):
                bit = order[stage]
                lead = dims({**fixed, bit: 1 - bit_of(dp, bit)}, slice(None))
                source = own.at[lead + (pl.ds(0, cube.n_seq),)]
                device = (flipped(dp, bit), seq)
            else:
                bit = cube.seq_bits - 1 - after
                other = base + (1 - bit_of(seq, bit)) * (span // 2)
                lead = dims(fixed, None) if full else ()
                source = own.at[lead + (pl.ds(other, span // 2),)]
                device = (dp, flipped(seq, bit))
            latest[array] = push(array, stage + 1, source, device)
    for copy in sends:
        copy.wait_send()


def scatter_all(cube, arrays, kinds, collective_id):
    outs, scratch = [], []
    for array, (full, _) in zip(arrays, kinds):
        block = array.shape[-2:]
        outs.append(jax.ShapeDtypeStruct(block, F32))
        if full:
            shape = (2,) * (cube.dp_bits - 1) + (cube.n_seq,)
            scratch.append(pltpu.VMEM(shape + block, array.dtype))
            for stage in range(cube.dp_bits):
                lead = (2,) * (cube.dp_bits - 1 - stage) + (cube.n_seq,)
                scratch.append(pltpu.VMEM(lead + block, array.dtype))
        else:
            scratch.append(pltpu.VMEM((cube.n_seq // 2,) + block, array.dtype))
        for stage in range(cube.seq_bits):
            scratch.append(pltpu.VMEM((cube.n_seq >> (stage + 1),) + block, array.dtype))
    slots = cube.seq_bits + cube.dp_bits
    scratch += [
        pltpu.SemaphoreType.DMA((len(arrays), slots)),
        pltpu.SemaphoreType.DMA((len(arrays), slots)),
        pltpu.SemaphoreType.DMA((len(arrays),)),
    ]
    return pl.pallas_call(
        functools.partial(scatter_kernel, cube, kinds),
        out_shape=outs,
        in_specs=[pl.BlockSpec(memory_space=pl.ANY)] * len(arrays),
        out_specs=[pl.BlockSpec(memory_space=pltpu.VMEM)] * len(arrays),
        scratch_shapes=scratch,
        compiler_params=pltpu.CompilerParams(
            collective_id=collective_id,
            has_side_effects=True,
            vmem_limit_bytes=56 * 1024 * 1024,
        ),
        name="scatter_grads",
    )(*arrays)


def head_slice(array, group_index, group_size):
    part = lax.dynamic_slice_in_dim(array, group_index * group_size * DH, group_size * DH, 2)
    return part.reshape(array.shape[0], array.shape[1], group_size, DH)


def regroup(stacked):
    group_count, seq_count, row_count, group_span = stacked.shape
    return jnp.moveaxis(stacked, 0, 2).reshape(seq_count, row_count, group_count * group_span)


def masked_scores(query_part, key_part, allow):
    scores = jnp.einsum("sqhd,skhd->shqk", query_part, key_part, preferred_element_type=F32)
    if allow is not None:
        scores = jnp.where(allow[:, None], scores, NEG)
    return scores


def attn_forward(queries, keys, values, allow):
    group_size = math.gcd(H, 4)

    def one_group(group_index):
        query_part = head_slice(queries, group_index, group_size)
        key_part = head_slice(keys, group_index, group_size)
        value_part = head_slice(values, group_index, group_size)
        scores = masked_scores(query_part, key_part, allow)
        row_max = jnp.max(scores, axis=-1, keepdims=True)
        expon = jnp.exp(scores - row_max)
        row_total = jnp.sum(expon, axis=-1, keepdims=True)
        probab = (expon / row_total).astype(BF)
        attended = jnp.einsum("shqk,skhd->sqhd", probab, value_part, preferred_element_type=F32)
        attended = attended.reshape(queries.shape[0], queries.shape[1], group_size * DH)
        return (attended, (row_max + jnp.log(row_total))[..., 0])

    stacked, log_sums = lax.map(one_group, jnp.arange(H // group_size, dtype=jnp.int32))
    return (regroup(stacked), log_sums)


def attn_backward(queries, keys, values, allow, log_sums, grad_attended):
    group_size = math.gcd(H, 4)

    def one_group(items):
        group_index, log_part = items
        query_part = head_slice(queries, group_index, group_size)
        key_part = head_slice(keys, group_index, group_size)
        value_part = head_slice(values, group_index, group_size)
        grad_part = head_slice(grad_attended, group_index, group_size)
        scores = masked_scores(query_part, key_part, allow)
        probab = jnp.exp(scores - log_part[..., None])
        grad_probs = jnp.einsum("sqhd,skhd->shqk", grad_part, value_part, preferred_element_type=F32)
        row_delta = jnp.sum(probab * grad_probs, axis=-1, keepdims=True)
        grad_scores = (probab * (grad_probs - row_delta)).astype(BF)
        grad_query = jnp.einsum("shqk,skhd->sqhd", grad_scores, key_part, preferred_element_type=F32)
        grad_key = jnp.einsum("shqk,sqhd->skhd", grad_scores, query_part, preferred_element_type=F32)
        grad_value = jnp.einsum(
            "shqk,sqhd->skhd", probab.astype(BF), grad_part, preferred_element_type=F32
        )
        seq_count = queries.shape[0]
        return (
            grad_query.reshape(seq_count, queries.shape[1], group_size * DH),
            grad_key.reshape(seq_count, keys.shape[1], group_size * DH),
            grad_value.reshape(seq_count, keys.shape[1], group_size * DH),
        )

    group_ids = jnp.arange(H // group_size, dtype=jnp.int32)
    grad_queries, grad_keys, grad_values = lax.map(one_group, (group_ids, log_sums))
    return (regroup(grad_queries), regroup(grad_keys), regroup(grad_values))


WIDE = 13


def local(
    cube,
    tokens,
    encoded,
    cotangent,
    doc_ids,
    block_ids,
    query_weight,
    key_weight,
    value_weight,
    out_weight,
    query_bias,
    value_bias,
    out_bias,
    first_gain,
    first_shift,
    probe_weight,
    lookup_weight,
    content_weight,
    merge_weight,
    probe_bias,
    content_bias,
    merge_bias,
    second_gain,
    second_shift,
    expand_weight,
    expand_bias,
    reduce_weight,
    reduce_bias,
    third_gain,
    third_shift,
):
    seq_count, local_rows, feat_width = tokens.shape
    assert seq_count == 1
    enc_local = encoded.shape[1]
    scale = DH ** (-0.5)
    flat = tokens.reshape(local_rows, feat_width)
    enc_flat = encoded.reshape(enc_local, feat_width)

    weights = [
        query_weight, key_weight, value_weight, out_weight, probe_weight,
        lookup_weight, content_weight, merge_weight, expand_weight, reduce_weight,
    ]
    vectors = [
        query_bias, value_bias, out_bias, first_gain, first_shift, probe_bias, content_bias,
        merge_bias, second_gain, second_shift, reduce_bias, third_gain, third_shift,
    ]
    part = vectors[0].shape[0]
    long_part = expand_bias.shape[0]
    held = WIDE * part + long_part
    padded = -(-held // 1024) * 1024
    vec_block = (8, padded // 8)
    packed = jnp.concatenate(vectors + [expand_bias, jnp.zeros((padded - held,), F32)])
    blocks = [w.astype(BF).reshape(block_shape(*w.shape)) for w in weights]
    kinds = [(False, 0), (False, 0)] + [(True, i % 2) for i in range(len(blocks))] + [(True, 0)]
    gathered = gather_all(
        cube, [flat, enc_flat] + blocks + [packed.reshape(vec_block)], kinds, 0
    )
    n_dev = cube.n_dev
    tok_all = gathered[0].reshape(cube.n_seq * local_rows, feat_width)
    enc_all = gathered[1].reshape(cube.n_seq * enc_local, feat_width)
    (
        query_mat, key_mat, value_mat, out_mat, probe_mat,
        lookup_mat, content_mat, merge_mat, expand_mat, reduce_mat,
    ) = [
        g.reshape(w.shape[0] * n_dev, w.shape[1]) for g, w in zip(gathered[2:12], weights)
    ]
    vec_all = gathered[12].reshape(n_dev, padded)
    wide_all = (
        vec_all[:, : WIDE * part].reshape(n_dev, WIDE, part).transpose(1, 0, 2).reshape(WIDE, -1)
    )
    (
        query_vec, value_vec, out_vec, gain_first, shift_first, probe_vec, content_vec,
        merge_vec, gain_second, shift_second, reduce_vec, gain_third, shift_third,
    ) = [wide_all[i] for i in range(WIDE)]
    expand_vec = vec_all[:, WIDE * part : held].reshape(-1)

    offset = lax.axis_index("seq") * local_rows
    query_doc = lax.dynamic_slice_in_dim(doc_ids, offset, local_rows, 1)
    query_block = lax.dynamic_slice_in_dim(block_ids, offset, local_rows, 1)
    allow = (query_doc[:, :, None] == doc_ids[:, None, :]) & (
        block_ids[:, None, :] <= query_block[:, :, None]
    )
    token_float = flat.astype(F32)
    queries = ((matmul(flat, query_mat) + query_vec) * scale).astype(BF)
    all_keys = matmul(tok_all, key_mat).astype(BF)
    all_values = (matmul(tok_all, value_mat) + value_vec).astype(BF)
    self_out, self_logs = attn_forward(queries[None], all_keys[None], all_values[None], allow)
    self_outb = self_out[0].astype(BF)
    first_sum = token_float + matmul(self_outb, out_mat) + out_vec
    normed_one, inv_one = layer_stats(first_sum)
    stream_one = (normed_one * gain_first + shift_first).astype(BF)
    probe = ((matmul(stream_one, probe_mat) + probe_vec) * scale).astype(BF)
    enc_keys = matmul(enc_all, lookup_mat).astype(BF)
    enc_values = (matmul(enc_all, content_mat) + content_vec).astype(BF)
    cross_out, cross_logs = attn_forward(probe[None], enc_keys[None], enc_values[None], None)
    cross_outb = cross_out[0].astype(BF)
    second_sum = stream_one.astype(F32) + matmul(cross_outb, merge_mat) + merge_vec
    normed_two, inv_two = layer_stats(second_sum)
    stream_two = (normed_two * gain_second + shift_second).astype(BF)
    expanded = matmul(stream_two, expand_mat) + expand_vec
    activated = jax.nn.gelu(expanded, approximate=False).astype(BF)
    third_sum = stream_two.astype(F32) + matmul(activated, reduce_mat) + reduce_vec
    normed_three, inv_three = layer_stats(third_sum)
    output = (normed_three * gain_third + shift_third).astype(BF)

    grad_output = cotangent.reshape(local_rows, feat_width).astype(F32)
    g_shift_third = jnp.sum(grad_output, axis=0)
    g_gain_third = jnp.sum(grad_output * normed_three, axis=0)
    grad_three = layer_back(grad_output * gain_third, normed_three, inv_three)
    reduce_rows = grad_three.astype(BF)
    g_reduce_vec = jnp.sum(grad_three, axis=0)
    g_reduce_mat = left_outer(activated, reduce_rows)
    grad_act = right_trans(reduce_rows, reduce_mat)
    slope = 0.5 * (
        1.0 + jax.scipy.special.erf(expanded * INV_ROOT_TWO)
    ) + expanded * DENSITY_CONST * jnp.exp(-0.5 * expanded * expanded)
    grad_expanded = grad_act * slope
    g_expand_vec = jnp.sum(grad_expanded, axis=0)
    expand_rows = grad_expanded.astype(BF)
    g_expand_mat = left_outer(stream_two, expand_rows)

    def spread(grad, weight):
        return grad.astype(BF).reshape(cube.lead(True) + block_shape(*weight.shape))

    expand_sum, reduce_sum = scatter_all(
        cube,
        [spread(g_reduce_mat, reduce_weight), spread(g_expand_mat, expand_weight)],
        [(True, 0), (True, 1)],
        1,
    )[::-1]

    grad_two = grad_three + right_trans(expand_rows, expand_mat)
    g_shift_second = jnp.sum(grad_two, axis=0)
    g_gain_second = jnp.sum(grad_two * normed_two, axis=0)
    grad_second = layer_back(grad_two * gain_second, normed_two, inv_two)
    merge_rows = grad_second.astype(BF)
    g_merge_vec = jnp.sum(grad_second, axis=0)
    g_merge_mat = left_outer(cross_outb, merge_rows)
    grad_cross = right_trans(merge_rows, merge_mat).astype(BF)
    grad_probe, grad_enc_keys, grad_enc_values = attn_backward(
        probe[None], enc_keys[None], enc_values[None], None, cross_logs, grad_cross[None]
    )
    probe_rows = (grad_probe[0].astype(BF).astype(F32) * scale).astype(BF)
    g_probe_vec = jnp.sum(probe_rows.astype(F32), axis=0)
    g_probe_mat = left_outer(stream_one, probe_rows)
    enc_key_rows = grad_enc_keys[0].astype(BF)
    enc_value_rows = grad_enc_values[0].astype(BF)
    g_lookup_mat = left_outer(enc_all, enc_key_rows)
    g_content_mat = left_outer(enc_all, enc_value_rows)
    g_content_vec = jnp.sum(grad_enc_values[0], axis=0)
    enc_part = right_trans(enc_key_rows, lookup_mat) + right_trans(enc_value_rows, content_mat)
    grad_one = grad_second + right_trans(probe_rows, probe_mat)
    g_shift_first = jnp.sum(grad_one, axis=0)
    g_gain_first = jnp.sum(grad_one * normed_one, axis=0)
    grad_first = layer_back(grad_one * gain_first, normed_one, inv_one)
    out_rows = grad_first.astype(BF)
    g_out_vec = jnp.sum(grad_first, axis=0)
    g_out_mat = left_outer(self_outb, out_rows)
    grad_self = right_trans(out_rows, out_mat).astype(BF)
    grad_query, grad_keys, grad_values = attn_backward(
        queries[None], all_keys[None], all_values[None], allow, self_logs, grad_self[None]
    )
    query_rows = (grad_query[0].astype(BF).astype(F32) * scale).astype(BF)
    key_rows = grad_keys[0].astype(BF)
    value_rows = grad_values[0].astype(BF)
    g_query_vec = jnp.sum(query_rows.astype(F32), axis=0)
    g_value_vec = jnp.sum(grad_values[0], axis=0)
    g_query_mat = left_outer(flat, query_rows)
    g_key_mat = left_outer(tok_all, key_rows)
    g_value_mat = left_outer(tok_all, value_rows)
    tok_part = right_trans(key_rows, key_mat) + right_trans(value_rows, value_mat)
    tok_own = grad_first + right_trans(query_rows, query_mat)

    wide_grads = jnp.stack(
        [
            g_query_vec, g_value_vec, g_out_vec, g_gain_first, g_shift_first, g_probe_vec, g_content_vec,
            g_merge_vec, g_gain_second, g_shift_second, g_reduce_vec, g_gain_third, g_shift_third,
        ]
    )
    vec_grads = jnp.concatenate(
        [
            wide_grads.reshape(WIDE, n_dev, part).transpose(1, 0, 2).reshape(n_dev, WIDE * part),
            g_expand_vec.reshape(n_dev, long_part),
            jnp.zeros((n_dev, padded - held), F32),
        ],
        axis=1,
    ).reshape(cube.lead(True) + vec_block)
    mats = [
        g_merge_mat, g_probe_mat, g_lookup_mat, g_content_mat, g_out_mat,
        g_query_mat, g_key_mat, g_value_mat,
    ]
    shards = [
        merge_weight, probe_weight, lookup_weight, content_weight, out_weight,
        query_weight, key_weight, value_weight,
    ]
    sums = scatter_all(
        cube,
        [
            enc_part.astype(BF).reshape(cube.n_seq, enc_local, feat_width),
            tok_part.astype(BF).reshape(cube.n_seq, local_rows, feat_width),
        ]
        + [spread(g, w) for g, w in zip(mats, shards)]
        + [vec_grads],
        [(False, 0), (False, 0)] + [(True, i % 2) for i in range(len(mats))] + [(True, 0)],
        2,
    )
    encoded_grad = sums[0]
    tokens_grad = tok_own + sums[1]
    (
        merge_sum, probe_sum, lookup_sum, content_sum, out_sum, query_sum, key_sum, value_sum,
    ) = [s.reshape(w.shape) for s, w in zip(sums[2:10], shards)]
    expand_sum = expand_sum.reshape(expand_weight.shape)
    reduce_sum = reduce_sum.reshape(reduce_weight.shape)
    vec_sum = sums[10].reshape(padded)
    (
        query_vs, value_vs, out_vs, gain1_vs, shift1_vs, probe_vs, content_vs,
        merge_vs, gain2_vs, shift2_vs, reduce_vs, gain3_vs, shift3_vs,
    ) = [vec_sum[i * part : (i + 1) * part] for i in range(WIDE)]
    expand_vs = vec_sum[WIDE * part : held]
    return (
        output[None],
        tokens_grad[None],
        encoded_grad[None],
        query_sum,
        key_sum,
        value_sum,
        out_sum,
        query_vs,
        value_vs,
        out_vs,
        gain1_vs,
        shift1_vs,
        probe_sum,
        lookup_sum,
        content_sum,
        merge_sum,
        probe_vs,
        content_vs,
        merge_vs,
        gain2_vs,
        shift2_vs,
        expand_sum,
        expand_vs,
        reduce_sum,
        reduce_vs,
        gain3_vs,
        shift3_vs,
    )


def solution(mesh):
    rows = P("dp", "seq", None)
    ids = P("dp", None)
    mat = P(("dp", "seq"), None)
    vec = P(("dp", "seq"))
    return jax.shard_map(
        functools.partial(local, Cube(mesh)),
        mesh=mesh,
        in_specs=(
            (rows, rows, rows, ids, ids)
            + (mat, mat, mat, mat, vec, vec, vec, vec, vec)
            + (mat, mat, mat, mat, vec, vec, vec, vec, vec)
            + (mat, vec, mat, vec, vec, vec)
        ),
        out_specs=(
            (rows, rows, rows)
            + (mat, mat, mat, mat, vec, vec, vec, vec, vec)
            + (mat, mat, mat, mat, vec, vec, vec, vec, vec)
            + (mat, vec, mat, vec, vec, vec)
        ),
        check_vma=False,
    )
```

time: 3140 us -> 985 us (0.31)
  waiting for transfers between devices: 2610 us -> 0 us
  Pallas kernels: 0 us -> 646 us
  blocking collectives: 110 us -> 0 us
  local copies, waits for them, and re-layouts: 169 us -> 97.2 us
    reduce_scatter x7 -> x0, waiting for transfers between devices: 1220 us -> none  [the longest x1 365 us: local(): lax.psum_scatter(g_expand_mat, ('dp', 'seq'), scatter_dimension=0, tiled=...]
    unnamed x37 -> x0, waiting for transfers between devices: 844 us -> none
    pallas_call x0 -> x3, Pallas kernels: none -> 646 us  [the longest x1 343 us: gather_all(): pl.pallas_call(functools.partial(gather_kernel, cube, kinds), out_shape=o...]
    all_gather x14 -> x0, waiting for transfers between devices: 550 us -> none  [the longest x1 76.8 us: local(): lax.all_gather(expand_weight.astype(jnp.bfloat16), ('dp', 'seq'), axis=0,...]
    unnamed x166 -> x129, local copies, waits for them, and re-layouts: 92.5 us -> 22.9 us
    all_gather x1 -> x0, blocking collectives: 66.3 us -> none  [local(): lax.all_gather(expand_bias, ('dp', 'seq'), axis=0, tiled=True)]
    unnamed x1 -> x0, blocking collectives: 43.7 us -> none
  transfers between devices with their start and end apart: 29 -> 0, of which waited for: 27 -> 0; matrix products, arithmetic and copies ran while one was open for 10% -> 0% of each run, Pallas kernels for 0% -> 0%
where the time goes in v1:
time: 985 us; the launch traced here: 981 us
  Pallas kernels  646 us (66%)
  matrix products  179 us (18%)
  local copies, waits for them, and re-layouts  97.2 us (10%)
  other arithmetic  44.3 us (4%)
  loops' own time  11.8 us (1%)
    pallas_call x1, Pallas kernels, gather_all(): pl.pallas_call(functools.partial(gather_kernel, cube, kinds), out_shape=o...  343 us
    pallas_call x2, Pallas kernels, scatter_all(): pl.pallas_call(functools.partial(scatter_kernel, cube, kinds), out_shape=...  303 us
    dot_general x10, matrix products, matmul(): return jnp.dot(left_arg, right_arg, preferred_element_type=F32)  49.8 us
    dot_general x10, matrix products, right_trans(): lax.dot_general(left_arg, right_arg, (((1,), (1,)), ((), ())), preferred_...  37.5 us
    dot_general x10, matrix products, left_outer(): lax.dot_general(left_arg, right_arg, (((0,), (0,)), ((), ())), preferred_...  32.7 us
    dynamic_slice x48, local copies, waits for them, and re-layouts, head_slice(): lax.dynamic_slice_in_dim(array, group_index * group_size * DH, group_size...  30.3 us
    unnamed x129, local copies, waits for them, and re-layouts  22.9 us

profile of v1, /device:TPU:0, one launch (start us, length us, event | category | flops | bytes accessed | tf_op | source)
XLA Modules:
  0.0 980.6 jit_solution(1429860804796528361)
XLA Ops:
  18.0 343.2 %gather_weights.1 = (bf16[4,256,1024]{2,1,0:T(8,128)(2,1)}, bf16[4,128,1024]{2,1,0:T(8,128)(2,1)}, bf16[2,2,2,4,32,1024]{5,4,3,2,1,0:T(8,128)(2,1)}, bf16[2,2,2,...) custom-call(bf16[256,1024]{1,0:T(8,128)(2,1)} %bitcast.421, ...), custom_call_target="tpu_custom_call" | custom-call | tf_op jit(solution)/shard_map/gather_weights/pallas_call | solution.py:185
  363.2 3.2 fusion.33
  368.1 5.9 fusion.31
  374.0 2.9 copy.68
  377.0 3.3 fusion.51
  380.3 3.7 convert_bitcast_fusion
  384.0 4.0 copy.69
  388.8 30.4 %while.64 = (s32[]{:T(128)}, bf16[4,1,256,256]{2,3,1,0:T(8,128)(2,1)}, f32[4,1,4,256]{3,2,1,0:T(4,128)S(1)}, s32[4]{0:T(128)S(1)}, bf16[1,1024,1024]{1,2,0:T(8,1...) while((s32[]{:T(128)}, ...), condition=%wide.region_3.4_spmd.clone, body=%wide.region_0.3_spmd.clone.sunk | while | flops 278658048 | bytes 17606880 | solution.py:400
  420.5 2.6 fusion.73
  423.9 2.4 fusion.50
  426.6 4.2 fusion.32
  430.8 2.3 copy.72
  433.1 17.8 %while.62 = (s32[]{:T(128)}, bf16[4,1,256,256]{2,3,1,0:T(8,128)(2,1)S(1)}, f32[4,1,4,256]{3,2,1,0:T(4,128)S(1)}, s32[4]{0:T(128)S(1)}, bf16[1,512,1024]{1,2,0:T(...) while((s32[]{:T(128)}, ...), condition=%wide.region_9.10_spmd, body=%wide.region_6.9_spmd.sunk | while | flops 137362432 | bytes 8683711 | solution.py:400
  450.9 2.9 fusion.74
  454.2 15.0 %fusion.20 = (bf16[256,4096]{1,0:T(8,128)(2,1)S(1)}, f32[256,4096]{1,0:T(8,128)}) fusion(f32[4096]{0:T(1024)S(1)} %slice_bitcast_fusion, bf16[1024,4096]{1,0:T(8,128)(2,1)} %bitcast.458, f32[256,1024]{1,0:T(8,128)S(1)} %get-tuple-element.844, f32[1024]{0:T(1024)S(1)} %add.292, f32[1024]{0:T(1024)S(1)} %mul.304, f32[256]{0:T(256)S(1)} %add_rsqrt_fusion.1, ...), kind=kOutput, calls=%fused_computation.62 | convolution fusion | flops 2218000384 | bytes 15755264 | tf_op jit(solution)/shard_map/dot_general | solution.py:24
  469.3 6.6 fusion.75
  476.2 2.1 fusion.55
  478.5 2.7 fusion.67
  481.1 8.9 fusion.76
  490.0 6.9 multiply_reduce_fusion.2
  499.9 32.7 %while.63 = (s32[]{:T(128)}, bf16[4,1,256,256]{2,3,1,0:T(8,128)(2,1)}, bf16[4,1,512,256]{2,3,1,0:T(8,128)(2,1)}, f32[4,1,512,256]{2,3,1,0:T(8,128)}, s32[4]{0:T(...) while((s32[]{:T(128)}, ...), condition=%wide.region_20.21_spmd, body=%wide.region_18.20_spmd.sunk | while | flops 339213312 | bytes 21647588 | solution.py:431
  532.7 3.4 fusion.83
  537.2 2.3 add_convert_fusion.2
  540.7 3.0 multiply_reduce_fusion.3
  546.7 67.2 %while.65 = (s32[]{:T(128)}, bf16[4,1,256,256]{2,3,1,0:T(8,128)(2,1)}, bf16[4,1,1024,256]{2,3,1,0:T(8,128)(2,1)}, f32[4,1,1024,256]{2,3,1,0:T(8,128)}, s32[4]{0:...) while((s32[]{:T(128)}, ...), condition=%wide.region_25.26_spmd.clone, body=%wide.region_23.25_spmd.clone.sunk | while | flops 684456960 | bytes 59414812 | solution.py:431
  550.1 2.7 fusion.233
  553.3 3.9 multiply_reduce_fusion.14
  566.8 2.7 fusion.233
  570.0 3.9 multiply_reduce_fusion.14
  583.6 2.7 fusion.233
  586.8 3.9 multiply_reduce_fusion.14
  600.3 2.7 fusion.233
  603.5 3.9 multiply_reduce_fusion.14
  613.8 4.8 fusion.84
  620.2 3.7 add_convert_fusion
  624.0 2.1 convolution_convert_fusion.9
  626.0 2.1 convolution_convert_fusion.8
  628.1 2.7 convolution_convert_fusion.7
  630.8 2.6 convolution_convert_fusion.6
  633.4 2.1 convolution_convert_fusion.5
  637.8 4.1 convolution_convert_fusion.3
  641.9 3.7 convolution_convert_fusion.2
  645.7 2.5 bitcast_reduce_fusion
  652.5 161.9 %scatter_grads.2 = (f32[128,1024]{1,0:T(8,128)}, f32[256,1024]{1,0:T(8,128)}, f32[32,1024]{1,0:T(8,128)}, f32[32,1024]{1,0:T(8,128)}, f32[32,1024]{1,0:T(8,128)}...) custom-call(bf16[4,128,1024]{2,1,0:T(8,128)(2,1)} %bitcast.439, ...), custom_call_target="tpu_custom_call" | custom-call | tf_op jit(solution)/shard_map/scatter_grads/pallas_call | solution.py:352
  814.5 3.1 fusion.35
  818.3 5.6 convolution_convert_fusion.1
  823.9 5.7 convolution_convert_fusion
  829.7 141.1 %scatter_grads.3 = (f32[128,1024]{1,0:T(8,128)}, f32[32,4096]{1,0:T(8,128)}) custom-call(bf16[2,2,2,4,128,1024]{5,4,3,2,1,0:T(8,128)(2,1)} %bitcast.390, bf16[2,2,2,4,32,4096]{5,4,3,2,1,0:T(8,128)(2,1)} %bitcast.391), custom_call_target="tpu_custom_call" | custom-call | tf_op jit(solution)/shard_map/scatter_grads/pallas_call | solution.py:352
  (411 shorter events, 161.2 us)
Async XLA Ops:
  16.5 345.6 %copy-start.46 = (f32[480]{0:T(512)}, f32[480]{0:T(512)S(1)}, u32[]{:S(2)}) copy-start(f32[480]{0:T(512)S(1)} %broadcast_in_dim.149) | copy-start | bytes 5764
  384.0 4.0 copy-start.34
  384.0 4.0 copy-start.35
  423.8 6.9 copy-start.18
  450.9 18.3 %copy-start.11 = (bf16[1,256,1024]{1,2,0:T(8,128)(2,1)}, bf16[1,256,1024]{1,2,0:T(8,128)(2,1)S(1)}, u32[]{:S(2)}) copy-start(bf16[1,256,1024]{1,2,0:T(8,128)(2,1)S(1)} %get-tuple-element.1374) | copy-start | bytes 1572868
  450.9 18.3 %copy-start.13 = (bf16[4,1,256,256]{2,3,1,0:T(8,128)(2,1)}, bf16[4,1,256,256]{2,3,1,0:T(8,128)(2,1)S(1)}, u32[]{:S(2)}) copy-start(bf16[4,1,256,256]{2,3,1,0:T(8,128)(2,1)S(1)} %get-tuple-element.522) | copy-start | bytes 1572868
  453.9 15.4 %copy-start.44 = (f32[1024]{0:T(1024)}, f32[1024]{0:T(1024)S(1)}, u32[]{:S(2)}) copy-start(f32[1024]{0:T(1024)S(1)} %add.292) | copy-start | bytes 12292
  469.3 6.6 copy-start.24
  481.1 8.9 copy-start.22
  490.0 6.9 copy-start.26
  490.0 8.3 copy-start.9
  532.6 3.4 copy-start.10
  532.6 4.5 copy-start.54
  537.2 3.6 copy-start.4
  540.7 3.4 copy-start.20
  540.7 4.3 copy-start.8
  553.2 4.0 copy-start
  570.0 4.0 copy-start
  586.8 4.0 copy-start
  603.5 3.9 copy-start
  613.8 4.8 copy-start.2
  620.2 3.8 copy-start.5
  620.2 3.8 copy-start.14
  620.2 5.8 copy-start.19
  620.2 5.8 copy-start.21
  623.9 4.1 copy-start.56
  623.9 4.1 copy-start.57
  630.8 4.7 copy-start.28
  633.4 4.4 copy-start.51
  633.4 4.4 copy-start.55
  645.6 5.4 copy-start.48
  645.6 5.5 copy-start.17
  645.6 6.1 copy-start.47
  652.5 162.0 %copy-start.29 = (bf16[2,2,2,4,32,1024]{5,4,3,2,1,0:T(8,128)(2,1)S(1)}, bf16[2,2,2,4,32,1024]{5,4,3,2,1,0:T(8,128)(2,1)}, u32[]{:S(2)}) copy-start(bf16[2,2,2,4,32,1024]{5,4,3,2,1,0:T(8,128)(2,1)} %get-tuple-element.514) | copy-start | bytes 6291460
  814.5 3.8 copy-start.23
  814.5 3.8 copy-start.25
  818.3 5.6 copy-start.27
  818.3 5.6 copy-start.45
  829.6 141.7 %copy-start.32 = (f32[128,1024]{1,0:T(8,128)S(1)}, f32[128,1024]{1,0:T(8,128)}, u32[]{:S(2)}) copy-start(f32[128,1024]{1,0:T(8,128)} %get-tuple-element.535) | copy-start | bytes 1572868
  829.6 142.5 %copy-start.43 = (f32[32,1024]{1,0:T(8,128)S(1)}, f32[32,1024]{1,0:T(8,128)}, u32[]{:S(2)}) copy-start(f32[32,1024]{1,0:T(8,128)} %get-tuple-element.1349) | copy-start | bytes 393220
  829.6 143.2 %copy-start.42 = (f32[32,1024]{1,0:T(8,128)S(1)}, f32[32,1024]{1,0:T(8,128)}, u32[]{:S(2)}) copy-start(f32[32,1024]{1,0:T(8,128)} %get-tuple-element.1350) | copy-start | bytes 393220
  829.6 143.8 %copy-start.41 = (f32[32,1024]{1,0:T(8,128)S(1)}, f32[32,1024]{1,0:T(8,128)}, u32[]{:S(2)}) copy-start(f32[32,1024]{1,0:T(8,128)} %get-tuple-element.1351) | copy-start | bytes 393220
  829.6 144.5 %copy-start.40 = (f32[32,1024]{1,0:T(8,128)S(1)}, f32[32,1024]{1,0:T(8,128)}, u32[]{:S(2)}) copy-start(f32[32,1024]{1,0:T(8,128)} %get-tuple-element.1352) | copy-start | bytes 393220
  829.7 145.1 %copy-start.39 = (f32[32,1024]{1,0:T(8,128)S(1)}, f32[32,1024]{1,0:T(8,128)}, u32[]{:S(2)}) copy-start(f32[32,1024]{1,0:T(8,128)} %get-tuple-element.1358) | copy-start | bytes 393220
  829.7 145.8 %copy-start.38 = (f32[32,1024]{1,0:T(8,128)S(1)}, f32[32,1024]{1,0:T(8,128)}, u32[]{:S(2)}) copy-start(f32[32,1024]{1,0:T(8,128)} %get-tuple-element.1359) | copy-start | bytes 393220
  829.7 146.4 %copy-start.37 = (f32[32,1024]{1,0:T(8,128)S(1)}, f32[32,1024]{1,0:T(8,128)}, u32[]{:S(2)}) copy-start(f32[32,1024]{1,0:T(8,128)} %get-tuple-element.1360) | copy-start | bytes 393220
  829.7 147.1 %copy-start.36 = (f32[32,1024]{1,0:T(8,128)S(1)}, f32[32,1024]{1,0:T(8,128)}, u32[]{:S(2)}) copy-start(f32[32,1024]{1,0:T(8,128)} %get-tuple-element.1361) | copy-start | bytes 393220
  970.8 8.5 copy-start.33
  (13 other events, 29.0 us)

commit v2 on v1

--- a/solution.py
+++ b/solution.py
@@ -1,4 +1,5 @@
 import functools
+import itertools
 import math
 
 import jax
@@ -16,6 +17,7 @@
 INV_ROOT_TWO = 0.7071067811865476
 DENSITY_CONST = 0.3989422804014327
 MESH = pl.DeviceIdType.MESH
+PIECE = 16384
 BF = jnp.bfloat16
 F32 = jnp.float32
 
@@ -54,20 +56,23 @@
         self.n_dp = mesh.shape["dp"]
         self.n_seq = mesh.shape["seq"]
         self.dp_bits = self.n_dp.bit_length() - 1
-        self.seq_bits = self.n_seq.bit_length() - 1
-        assert self.n_dp == 1 << self.dp_bits and self.n_seq == 1 << self.seq_bits
+        assert self.n_dp == 1 << self.dp_bits
         self.n_dev = self.n_dp * self.n_seq
 
     def lead(self, full):
         return ((2,) * self.dp_bits if full else ()) + (self.n_seq,)
 
 
-def bit_of(index, bit):
-    return (index // (1 << bit)) % 2
-
-
-def flipped(index, bit):
-    return index + (1 << bit) * (1 - 2 * bit_of(index, bit))
+class Place:
+    def __init__(self, cube):
+        self.dp, self.seq = lax.axis_index("dp"), lax.axis_index("seq")
+        self.bits, self.flips = [], []
+        rest = self.dp
+        for bit in range(cube.dp_bits):
+            half = rest // 2
+            self.bits.append(rest - 2 * half)
+            self.flips.append(self.dp + (1 << bit) * (1 - 2 * self.bits[-1]))
+            rest = half
 
 
 def block_shape(rows, cols):
@@ -76,33 +81,53 @@
     return (16, rows * cols // 16)
 
 
-def meet(cube):
-    dp, seq = lax.axis_index("dp"), lax.axis_index("seq")
-    barrier = pltpu.get_barrier_semaphore()
-    for bit in range(cube.dp_bits):
-        pl.semaphore_signal(
-            barrier, inc=1, device_id=(flipped(dp, bit), seq), device_id_type=MESH
-        )
-    for bit in range(cube.seq_bits):
-        pl.semaphore_signal(
-            barrier, inc=1, device_id=(dp, flipped(seq, bit)), device_id_type=MESH
-        )
-    pl.semaphore_wait(barrier, cube.dp_bits + cube.seq_bits)
-
-
 def dim_order(cube, variant):
     bits = list(range(1, cube.dp_bits))
     return bits if variant == 0 else bits[::-1]
 
 
-def gather_kernel(cube, kinds, *refs):
-    count = len(kinds)
-    ins, outs = refs[:count], refs[count : 2 * count]
-    send_sem, recv_sem, local_sem = refs[2 * count :]
-    dp, seq = lax.axis_index("dp"), lax.axis_index("seq")
-    sends = []
-
-    def region(full, open_bits, fixed, seq_part):
+def meet(cube, here):
+    dp, seq = here.dp, here.seq
+    barrier = pltpu.get_barrier_semaphore()
+
+    def greet(device):
+        pl.semaphore_signal(barrier, inc=1, device_id=device, device_id_type=MESH)
+
+    for bit in range(cube.dp_bits):
+        greet((here.flips[bit], seq))
+    greet((dp, lax.rem(seq + 1, cube.n_seq)))
+    greet((dp, lax.rem(seq + cube.n_seq - 1, cube.n_seq)))
+    pl.semaphore_wait(barrier, cube.dp_bits + 2)
+
+
+def in_slots(pieces, lag):
+    depth = max(len(stages) for stages in pieces)
+    for slot in range(len(pieces) + lag * (depth - 1)):
+        for k in reversed(range(depth)):
+            p = slot - lag * k
+            if 0 <= p < len(pieces) and k < len(pieces[p]):
+                pieces[p][k]()
+
+
+def remote(source, target, send_sem, recv_sem, device):
+    return pltpu.make_async_remote_copy(
+        src_ref=source,
+        dst_ref=target,
+        send_sem=send_sem,
+        recv_sem=recv_sem,
+        device_id=device,
+        device_id_type=MESH,
+    )
+
+
+def gather_stages(cube, here, full, variant, source, target, send_sem, recv_sem, local_sem):
+    dp, seq = here.dp, here.seq
+    n = cube.n_seq
+    order = dim_order(cube, variant)
+    every = pl.ds(0, n)
+    waits = []
+
+    def region(open_bits, fixed, seq_part):
         if not full:
             return (seq_part,)
         places = []
@@ -110,87 +135,166 @@
             if bit in open_bits:
                 places.append(slice(None))
             else:
-                places.append(fixed.get(bit, bit_of(dp, bit)))
+                places.append(fixed.get(bit, here.bits[bit]))
         return tuple(places) + (seq_part,)
 
-    def push(array, slot, place, device):
-        copy = pltpu.make_async_remote_copy(
-            src_ref=outs[array].at[place],
-            dst_ref=outs[array].at[place],
-            send_sem=send_sem.at[array, slot],
-            recv_sem=recv_sem.at[array, slot],
-            device_id=device,
-            device_id_type=MESH,
+    def move(place, slot, device):
+        at = target.at[place]
+        return remote(at, at, send_sem.at[slot], recv_sem.at[slot], device)
+
+    own = pltpu.make_async_copy(source, target.at[region((), {}, seq)], local_sem)
+
+    def line(step, way):
+        slot = 2 * step + (1 if way > 0 else 0)
+        block = seq - way * step
+        inside = (seq + way >= 0) & (seq + way < n)
+        sends = inside & (block >= 0) & (block < n)
+        copy = lambda: move(region((), {}, block), slot, (dp, seq + way))
+        came = seq - way * (step + 1)
+        gets = (came >= 0) & (came < n)
+        arrival = lambda: move(region((), {}, came), slot, (dp, seq - way))
+        return sends, copy, gets, arrival
+
+    def line_start(step):
+        for way in (1, -1):
+            sends, copy, _, _ = line(step, way)
+            pl.when(sends)(lambda: copy().start())
+            waits.append((sends, copy))
+
+    def line_wait(step):
+        for way in (1, -1):
+            _, _, gets, arrival = line(step, way)
+            pl.when(gets)(lambda: arrival().wait_recv())
+
+    base = 2 * (n - 1)
+    cores, arrivals = [], []
+
+    def dims_start(stage):
+        if stage < len(order):
+            copy = move(
+                region(order[:stage], {}, every), base + 2 * stage, (here.flips[order[stage]], seq)
+            )
+            copy.start()
+            waits.append((None, copy))
+            arrivals.append(copy)
+        if stage == 0:
+            fresh = region((), {}, every)
+        else:
+            last = order[stage - 1]
+            fresh = region(order[: stage - 1], {last: 1 - here.bits[last]}, every)
+        copy = move(fresh, base + 2 * stage + 1, (here.flips[0], seq))
+        copy.start()
+        waits.append((None, copy))
+        cores.append(copy)
+
+    def first():
+        own.wait()
+        line_start(0)
+
+    stages = [first]
+    for step in range(n - 1):
+
+        def after_line(step=step):
+            line_wait(step)
+            if step < n - 2:
+                line_start(step + 1)
+            elif full:
+                dims_start(0)
+
+        stages.append(after_line)
+    if full:
+        for stage in range(len(order)):
+
+            def after_dims(stage=stage):
+                arrivals[stage].wait_recv()
+                dims_start(stage + 1)
+
+            stages.append(after_dims)
+
+        def last():
+            for copy in cores:
+                copy.wait_recv()
+
+        stages.append(last)
+
+    def finish():
+        for sends, copy in waits:
+            if sends is None:
+                copy.wait_send()
+            else:
+                pl.when(sends)(lambda: copy().wait_send())
+
+    return own, stages, finish
+
+
+def gather_slots(cube):
+    return 2 * (cube.n_seq - 1) + 2 * cube.dp_bits
+
+
+def gather_kernel(cube, pieces, *refs):
+    count = 1 + max(piece[0] for piece in pieces)
+    ins, outs = refs[:count], refs[count : 2 * count]
+    send_sem, recv_sem, local_sem = refs[2 * count :]
+    here = Place(cube)
+    plans = []
+    for index, (array, full, variant, col, cols) in enumerate(pieces):
+        lead = cube.dp_bits * full + 1
+        cut = (slice(None), pl.ds(col, cols))
+        plans.append(
+            gather_stages(
+                cube,
+                here,
+                full,
+                variant,
+                ins[array].at[cut],
+                outs[array].at[(slice(None),) * lead + cut],
+                send_sem.at[index],
+                recv_sem.at[index],
+                local_sem.at[index],
+            )
         )
-        copy.start()
-        sends.append(copy)
-        return copy
-
-    own = []
-    for array, (full, _) in enumerate(kinds):
-        copy = pltpu.make_async_copy(
-            ins[array], outs[array].at[region(full, (), {}, seq)], local_sem.at[array]
-        )
-        copy.start()
-        own.append(copy)
-    meet(cube)
-    latest = own
-    for bit in range(cube.seq_bits):
-        span = 1 << bit
-        started = []
-        for array, (full, _) in enumerate(kinds):
-            latest[array].wait() if bit == 0 else latest[array].wait_recv()
-            place = region(full, (), {}, pl.ds(seq - seq % span, span))
-            started.append(push(array, bit, place, (dp, flipped(seq, bit))))
-        latest = started
-    every = pl.ds(0, cube.n_seq)
-    cores = []
-    slot = cube.seq_bits
-    for stage in range(cube.dp_bits):
-        started = []
-        for array, (full, variant) in enumerate(kinds):
-            if latest[array] is None:
-                started.append(None)
-                continue
-            latest[array].wait_recv()
-            if not full:
-                started.append(None)
-                continue
-            order = dim_order(cube, variant)
-            if stage < len(order):
-                place = region(full, order[:stage], {}, every)
-                device = (flipped(dp, order[stage]), seq)
-                started.append(push(array, slot + 2 * stage, place, device))
+    for own, _, _ in plans:
+        own.start()
+    meet(cube, here)
+    in_slots([stages for _, stages, _ in plans], 3)
+    for _, _, finish in plans:
+        finish()
+
+
+def cut_columns(kinds, arrays):
+    whole, along = [], []
+    for index, (full, array) in enumerate(zip(kinds, arrays)):
+        cols = array.shape[-1]
+        count = max(1, math.prod(array.shape[-2:]) // (PIECE if full else PIECE))
+        while cols % (128 * count):
+            count //= 2
+        width = cols // count
+        for i in range(count):
+            if full:
+                whole.append((index, True, len(whole) % 2, width * i, width))
             else:
-                started.append(None)
-            if stage == 0:
-                fresh = region(full, (), {}, every)
-            else:
-                last = order[stage - 1]
-                fresh = region(full, order[: stage - 1], {last: 1 - bit_of(dp, last)}, every)
-            cores.append(push(array, slot + 2 * stage + 1, fresh, (flipped(dp, 0), seq)))
-        latest = started
-    for copy in cores:
-        copy.wait_recv()
-    for copy in sends:
-        copy.wait_send()
+                along.append((index, False, 0, width * i, width))
+    placed = [((i + 0.5) / len(whole), 0, piece) for i, piece in enumerate(whole)]
+    placed += [((i + 0.5) / len(along), 1, piece) for i, piece in enumerate(along)]
+    return tuple(piece for _, _, piece in sorted(placed, key=lambda item: item[:2]))
 
 
 def gather_all(cube, arrays, kinds, collective_id):
+    pieces = cut_columns(kinds, arrays)
     outs = [
         jax.ShapeDtypeStruct(cube.lead(full) + array.shape, array.dtype)
-        for array, (full, _) in zip(arrays, kinds)
+        for array, full in zip(arrays, kinds)
     ]
-    slots = cube.seq_bits + 2 * cube.dp_bits
+    slots = gather_slots(cube)
     return pl.pallas_call(
-        functools.partial(gather_kernel, cube, kinds),
+        functools.partial(gather_kernel, cube, pieces),
         out_shape=outs,
         in_specs=[pl.BlockSpec(memory_space=pl.ANY)] * len(arrays),
         out_specs=[pl.BlockSpec(memory_space=pl.ANY)] * len(arrays),
         scratch_shapes=[
-            pltpu.SemaphoreType.DMA((len(arrays), slots)),
-            pltpu.SemaphoreType.DMA((len(arrays), slots)),
-            pltpu.SemaphoreType.DMA((len(arrays),)),
+            pltpu.SemaphoreType.DMA((len(pieces), slots)),
+            pltpu.SemaphoreType.DMA((len(pieces), slots)),
+            pltpu.SemaphoreType.DMA((len(pieces),)),
         ],
         compiler_params=pltpu.CompilerParams(
             collective_id=collective_id, has_side_effects=True
@@ -199,158 +303,219 @@
     )(*arrays)
 
 
-def add_blocks(total, part, places, rows, cols):
-    count, pick = places
+def add_block(total, part):
+    total[...] = (total[...].astype(F32) + part[...].astype(F32)).astype(total.dtype)
+
+
+def add_rows(pairs, count, rows, cols):
     step = rows
     while step * cols > 32768 and step % 32 == 0:
         step //= 2
-    chunks = rows // step
 
     def body(index, carry):
-        to, of = pick(index // chunks)
-        part_rows = pl.ds(pl.multiple_of((index % chunks) * step, step), step)
-        left = total[to + (part_rows,)].astype(F32)
-        right = part[of + (part_rows,)].astype(F32)
-        total[to + (part_rows,)] = (left + right).astype(total.dtype)
+        for total, part in pairs:
+            for row in range(0, rows, step):
+                at = (index, pl.ds(row, step))
+                add_block(total.at[at], part.at[at])
         return carry
 
-    lax.fori_loop(0, count * chunks, body, 0)
-
-
-def scatter_kernel(cube, kinds, *refs):
-    count = len(kinds)
-    ins, outs = refs[:count], refs[count : 2 * count]
-    refs = refs[2 * count :]
-    owns, parts = [], []
-    for full, _ in kinds:
-        stages = (cube.dp_bits if full else 0) + cube.seq_bits
-        owns.append(refs[0])
-        parts.append(refs[1 : 1 + stages])
-        refs = refs[1 + stages :]
-    send_sem, recv_sem, local_sem = refs
-    dp, seq = lax.axis_index("dp"), lax.axis_index("seq")
-    sends = []
-
-    def push(array, stage, source, device):
-        copy = pltpu.make_async_remote_copy(
-            src_ref=source,
-            dst_ref=parts[array][stage],
-            send_sem=send_sem.at[array, stage],
-            recv_sem=recv_sem.at[array, stage],
-            device_id=device,
-            device_id_type=MESH,
-        )
-        copy.start()
-        sends.append(copy)
-        return copy
+    lax.fori_loop(0, count, body, 0)
+
+
+def scatter_stages(
+    cube, here, full, variant, source, out, own, parts, send_sem, recv_sem, local_sem
+):
+    dp, seq = here.dp, here.seq
+    n = cube.n_seq
+    order = dim_order(cube, variant) if full else []
+    rows, cols = out.shape
+    line_part = parts[-1]
+    waits = []
+    arrivals = []
 
     def dims(fixed, kept):
         return tuple(
             fixed[bit] if bit in fixed else kept for bit in reversed(range(1, cube.dp_bits))
         )
 
-    top = cube.seq_bits - 1
-    half = cube.n_seq // 2
-    local, latest = [], []
-    for array, (full, _) in enumerate(kinds):
+    mine = {bit: here.bits[bit] for bit in range(1, cube.dp_bits)}
+    settled = dims(mine, None) if full else ()
+    lead = (slice(None),) * (cube.dp_bits - 1)
+    kept = source.at[lead + (here.bits[0],)] if full else source
+    local = pltpu.make_async_copy(kept, own, local_sem)
+
+    def push(stage, what, device):
+        copy = remote(what, parts[stage], send_sem.at[stage], recv_sem.at[stage], device)
+        copy.start()
+        waits.append((None, copy))
+        arrivals.append(copy)
+
+    base = cube.dp_bits if full else 0
+
+    def line(step, way):
+        target = seq + way * (n - 1 - step)
+        passes = (target >= 0) & (target < n)
+        further = passes & ((seq > 0) if way > 0 else (seq < n - 1))
+        slot = n if way < 0 and step == n - 2 else target
+        block = own.at[settled + (target,)]
+        index = base + 2 * step + (1 if way > 0 else 0)
+
+        def copy():
+            return remote(
+                block, line_part.at[slot], send_sem.at[index], recv_sem.at[index], (dp, seq + way)
+            )
+
+        def arrival():
+            at = line_part.at[target]
+            return remote(at, at, send_sem.at[index - 2], recv_sem.at[index - 2], (dp, seq - way))
+
+        return target, passes, further, copy, arrival
+
+    def line_step(step):
+        for way in (1, -1):
+            target, passes, further, copy, arrival = line(step, way)
+            if step > 0:
+
+                @pl.when(further)
+                def _():
+                    arrival().wait_recv()
+                    to, of = own.at[settled + (pl.ds(target, 1),)], line_part.at[pl.ds(target, 1)]
+                    add_rows([(to, of)], 1, rows, cols)
+
+            pl.when(passes)(lambda: copy().start())
+            waits.append((passes, copy))
+
+    def start():
+        local.start()
         if full:
-            lead = (slice(None),) * (cube.dp_bits - 1)
-            kept = ins[array].at[lead + (bit_of(dp, 0),)]
+            push(0, source.at[lead + (1 - here.bits[0],)], (here.flips[0], seq))
+
+    def after_dims(stage):
+        if stage == 0:
+            local.wait()
+        arrivals[stage].wait_recv()
+        closed = order[:stage]
+        fixed = {bit: mine[bit] for bit in closed}
+        open_bits = [bit for bit in reversed(range(1, cube.dp_bits)) if bit not in closed]
+
+        pairs = []
+        for values in itertools.product((0, 1), repeat=len(open_bits)):
+            to = dims({**fixed, **dict(zip(open_bits, values))}, None)
+            pairs.append((own.at[to], parts[stage].at[values]))
+        add_rows(pairs, n, rows, cols)
+        if stage < len(order):
+            bit = order[stage]
+            at = dims({**fixed, bit: 1 - mine[bit]}, slice(None)) + (pl.ds(0, n),)
+            push(stage + 1, own.at[at], (here.flips[bit], seq))
         else:
-            kept = ins[array].at[pl.ds(half * bit_of(seq, top), half)]
-        copy = pltpu.make_async_copy(kept, owns[array], local_sem.at[array])
-        copy.start()
-        local.append(copy)
-    meet(cube)
-    for array, (full, _) in enumerate(kinds):
+            line_step(0)
+
+    def last():
+        where = settled + (seq,)
+
+        def sem(way):
+            return recv_sem.at[base + 2 * (n - 2) + (1 if way > 0 else 0)]
+
+        @pl.when(seq > 0)
+        def _():
+            at = line_part.at[seq]
+            remote(at, at, send_sem.at[base], sem(1), (dp, seq - 1)).wait_recv()
+
+        @pl.when(seq < n - 1)
+        def _():
+            at = line_part.at[n]
+            remote(at, at, send_sem.at[base], sem(-1), (dp, seq + 1)).wait_recv()
+
+        @pl.when(seq == 0)
+        def _():
+            out[...] = own[where].astype(F32) + line_part[n].astype(F32)
+
+        @pl.when(seq == n - 1)
+        def _():
+            out[...] = own[where].astype(F32) + line_part[n - 1].astype(F32)
+
+        @pl.when((seq > 0) & (seq < n - 1))
+        def _():
+            both = line_part[seq].astype(F32) + line_part[n].astype(F32)
+            out[...] = own[where].astype(F32) + both
+
+    stages = [start]
+    if full:
+        stages += [functools.partial(after_dims, stage) for stage in range(cube.dp_bits)]
+    else:
+
+        def begin():
+            local.wait()
+            line_step(0)
+
+        stages.append(begin)
+    stages += [functools.partial(line_step, step) for step in range(1, n - 1)]
+    stages.append(last)
+
+    def finish():
+        for passes, copy in waits:
+            if passes is None:
+                copy.wait_send()
+            else:
+                pl.when(passes)(lambda: copy().wait_send())
+
+    return stages, finish
+
+
+def scatter_kernel(cube, pieces, *refs):
+    count = 1 + max(piece[0] for piece in pieces)
+    ins, outs = refs[:count], refs[count : 2 * count]
+    refs = refs[2 * count :]
+    send_sem, recv_sem, local_sem = refs[-3:]
+    here = Place(cube)
+    plans = []
+    for index, (array, full, variant, col, cols) in enumerate(pieces):
+        held = 2 + (cube.dp_bits if full else 0)
+        cut = (slice(None), pl.ds(col, cols))
+        plans.append(
+            scatter_stages(
+                cube,
+                here,
+                full,
+                variant,
+                ins[array].at[(slice(None),) * (cube.dp_bits * full + 1) + cut],
+                outs[array].at[cut],
+                refs[0],
+                refs[1:held],
+                send_sem.at[index],
+                recv_sem.at[index],
+                local_sem.at[index],
+            )
+        )
+        refs = refs[held:]
+    meet(cube, here)
+    in_slots([stages for stages, _ in plans], 2)
+    for _, finish in plans:
+        finish()
+
+
+def scatter_all(cube, arrays, kinds, collective_id):
+    pieces = cut_columns(kinds, arrays)
+    outs = [jax.ShapeDtypeStruct(array.shape[-2:], F32) for array in arrays]
+    scratch = []
+    for array, full, _, _, cols in pieces:
+        block = (arrays[array].shape[-2], cols)
+        dtype = arrays[array].dtype
         if full:
-            lead = (slice(None),) * (cube.dp_bits - 1)
-            source = ins[array].at[lead + (1 - bit_of(dp, 0),)]
-            device = (flipped(dp, 0), seq)
+            for stage in range(-1, cube.dp_bits):
+                lead = (2,) * (cube.dp_bits - 1 - max(stage, 0)) + (cube.n_seq,)
+                scratch.append(pltpu.VMEM(lead + block, dtype))
         else:
-            source = ins[array].at[pl.ds(half * (1 - bit_of(seq, top)), half)]
-            device = (dp, flipped(seq, top))
-        latest.append(push(array, 0, source, device))
-
-    longest = cube.dp_bits + cube.seq_bits
-    for stage in range(longest):
-        for array, (full, variant) in enumerate(kinds):
-            stages = (cube.dp_bits if full else 0) + cube.seq_bits
-            if stage >= stages:
-                continue
-            rows, cols = outs[array].shape
-            order = dim_order(cube, variant) if full else []
-            own, part = owns[array], parts[array][stage]
-            if stage == 0:
-                local[array].wait()
-            latest[array].wait_recv()
-            after = max(stage - (cube.dp_bits - 1), 0) if full else stage + 1
-            closed = order[: min(stage, len(order))]
-            fixed = {bit: bit_of(dp, bit) for bit in closed}
-            open_bits = [
-                bit for bit in reversed(range(1, cube.dp_bits)) if full and bit not in closed
-            ]
-            span = cube.n_seq >> after
-            base = seq - seq % span
-            if not full:
-                base = base - half * bit_of(seq, top)
-            if stage == stages - 1:
-                where = (dims(fixed, None) if full else ()) + (base,)
-                outs[array][...] = own[where].astype(F32) + part[0].astype(F32)
-                continue
-
-            def pick(index, full=full, fixed=fixed, open_bits=open_bits, span=span, base=base):
-                place = index % span
-                rest = index // span
-                values = {}
-                for bit in reversed(open_bits):
-                    values[bit] = rest % 2
-                    rest = rest // 2
-                of = tuple(values[bit] for bit in open_bits) + (place,)
-                to = (dims({**fixed, **values}, None) if full else ()) + (base + place,)
-                return to, of
-
-            amount = span * (1 << len(open_bits))
-            add_blocks(own, part, (amount, pick), rows, cols)
-            if full and stage < len(order):
-                bit = order[stage]
-                lead = dims({**fixed, bit: 1 - bit_of(dp, bit)}, slice(None))
-                source = own.at[lead + (pl.ds(0, cube.n_seq),)]
-                device = (flipped(dp, bit), seq)
-            else:
-                bit = cube.seq_bits - 1 - after
-                other = base + (1 - bit_of(seq, bit)) * (span // 2)
-                lead = dims(fixed, None) if full else ()
-                source = own.at[lead + (pl.ds(other, span // 2),)]
-                device = (dp, flipped(seq, bit))
-            latest[array] = push(array, stage + 1, source, device)
-    for copy in sends:
-        copy.wait_send()
-
-
-def scatter_all(cube, arrays, kinds, collective_id):
-    outs, scratch = [], []
-    for array, (full, _) in zip(arrays, kinds):
-        block = array.shape[-2:]
-        outs.append(jax.ShapeDtypeStruct(block, F32))
-        if full:
-            shape = (2,) * (cube.dp_bits - 1) + (cube.n_seq,)
-            scratch.append(pltpu.VMEM(shape + block, array.dtype))
-            for stage in range(cube.dp_bits):
-                lead = (2,) * (cube.dp_bits - 1 - stage) + (cube.n_seq,)
-                scratch.append(pltpu.VMEM(lead + block, array.dtype))
-        else:
-            scratch.append(pltpu.VMEM((cube.n_seq // 2,) + block, array.dtype))
-        for stage in range(cube.seq_bits):
-            scratch.append(pltpu.VMEM((cube.n_seq >> (stage + 1),) + block, array.dtype))
-    slots = cube.seq_bits + cube.dp_bits
+            scratch.append(pltpu.VMEM((cube.n_seq,) + block, dtype))
+        scratch.append(pltpu.VMEM((cube.n_seq + 1,) + block, dtype))
+    slots = 2 * cube.n_seq + cube.dp_bits
     scratch += [
-        pltpu.SemaphoreType.DMA((len(arrays), slots)),
-        pltpu.SemaphoreType.DMA((len(arrays), slots)),
-        pltpu.SemaphoreType.DMA((len(arrays),)),
+        pltpu.SemaphoreType.DMA((len(pieces), slots)),
+        pltpu.SemaphoreType.DMA((len(pieces), slots)),
+        pltpu.SemaphoreType.DMA((len(pieces),)),
     ]
     return pl.pallas_call(
-        functools.partial(scatter_kernel, cube, kinds),
+        functools.partial(scatter_kernel, cube, pieces),
         out_shape=outs,
         in_specs=[pl.BlockSpec(memory_space=pl.ANY)] * len(arrays),
         out_specs=[pl.BlockSpec(memory_space=pltpu.VMEM)] * len(arrays),
@@ -358,7 +523,7 @@
         compiler_params=pltpu.CompilerParams(
             collective_id=collective_id,
             has_side_effects=True,
-            vmem_limit_bytes=56 * 1024 * 1024,
+            vmem_limit_bytes=60 * 1024 * 1024,
         ),
         name="scatter_grads",
     )(*arrays)
@@ -489,7 +654,7 @@
     vec_block = (8, padded // 8)
     packed = jnp.concatenate(vectors + [expand_bias, jnp.zeros((padded - held,), F32)])
     blocks = [w.astype(BF).reshape(block_shape(*w.shape)) for w in weights]
-    kinds = [(False, 0), (False, 0)] + [(True, i % 2) for i in range(len(blocks))] + [(True, 0)]
+    kinds = [False, False] + [True] * (len(blocks) + 1)
     gathered = gather_all(
         cube, [flat, enc_flat] + blocks + [packed.reshape(vec_block)], kinds, 0
     )
@@ -563,7 +728,7 @@
     expand_sum, reduce_sum = scatter_all(
         cube,
         [spread(g_reduce_mat, reduce_weight), spread(g_expand_mat, expand_weight)],
-        [(True, 0), (True, 1)],
+        [True, True],
         1,
     )[::-1]
 
@@ -639,7 +804,7 @@
         ]
         + [spread(g, w) for g, w in zip(mats, shards)]
         + [vec_grads],
-        [(False, 0), (False, 0)] + [(True, i % 2) for i in range(len(mats))] + [(True, 0)],
+        [False, False] + [True] * (len(mats) + 1),
         2,
     )
     encoded_grad = sums[0]

time: 985 us -> 758 us (0.77)
  Pallas kernels: 646 us -> 413 us
    pallas_call x3, Pallas kernels: 646 us -> 413 us  [the longest x2 239 us: scatter_all(): pl.pallas_call(functools.partial(scatter_kernel, cube, pieces), out_shape...]
    unnamed x129 -> x127, local copies, waits for them, and re-layouts: 22.9 us -> 22.9 us
where the time goes in v2:
time: 758 us; the launch traced here: 748 us
  Pallas kernels  413 us (54%)
  matrix products  180 us (24%)
  local copies, waits for them, and re-layouts  97.4 us (13%)
  other arithmetic  44.3 us (6%)
  loops' own time  12 us (2%)
    pallas_call x2, Pallas kernels, scatter_all(): pl.pallas_call(functools.partial(scatter_kernel, cube, pieces), out_shape...  239 us
    pallas_call x1, Pallas kernels, gather_all(): pl.pallas_call(functools.partial(gather_kernel, cube, pieces), out_shape=...  175 us
    dot_general x10, matrix products, matmul(): return jnp.dot(left_arg, right_arg, preferred_element_type=F32)  49.9 us
    dot_general x10, matrix products, right_trans(): lax.dot_general(left_arg, right_arg, (((1,), (1,)), ((), ())), preferred_...  37.9 us
    dot_general x10, matrix products, left_outer(): lax.dot_general(left_arg, right_arg, (((0,), (0,)), ((), ())), preferred_...  32.6 us
    dynamic_slice x48, local copies, waits for them, and re-layouts, head_slice(): lax.dynamic_slice_in_dim(array, group_index * group_size * DH, group_size...  30.3 us
    unnamed x127, local copies, waits for them, and re-layouts  22.9 us
    dot_general x16, matrix products, masked_scores(): jnp.einsum('sqhd,skhd->shqk', query_part, key_part, preferred_element_typ...  19.7 us

profile of v2, /device:TPU:0, one launch (start us, length us, event | category | flops | bytes accessed | tf_op | source)
XLA Modules:
  0.0 748.3 jit_solution(2686897302801960107)
XLA Ops:
  18.0 174.6 %gather_weights.1 = (bf16[4,256,1024]{2,1,0:T(8,128)(2,1)}, bf16[4,128,1024]{2,1,0:T(8,128)(2,1)}, bf16[2,2,2,4,32,1024]{5,4,3,2,1,0:T(8,128)(2,1)}, bf16[2,2,2,...) custom-call(bf16[256,1024]{1,0:T(8,128)(2,1)} %bitcast.421, ...), custom_call_target="tpu_custom_call" | custom-call | tf_op jit(solution)/shard_map/gather_weights/pallas_call | solution.py:289
  194.7 3.2 fusion.33
  199.8 5.9 fusion.31
  205.7 2.9 copy.68
  208.7 3.3 fusion.51
  212.0 3.7 convert_bitcast_fusion
  215.7 4.0 copy.69
  220.5 30.4 %while.64 = (s32[]{:T(128)}, bf16[4,1,256,256]{2,3,1,0:T(8,128)(2,1)}, f32[4,1,4,256]{3,2,1,0:T(4,128)S(1)}, s32[4]{0:T(128)S(1)}, bf16[1,1024,1024]{1,2,0:T(8,1...) while((s32[]{:T(128)}, ...), condition=%wide.region_3.4_spmd.clone, body=%wide.region_0.3_spmd.clone.sunk | while | flops 278658048 | bytes 17606880 | solution.py:565
  252.2 2.7 fusion.73
  255.7 2.4 fusion.50
  258.3 4.2 fusion.32
  262.5 2.3 copy.72
  264.8 17.7 %while.62 = (s32[]{:T(128)}, bf16[4,1,256,256]{2,3,1,0:T(8,128)(2,1)S(1)}, f32[4,1,4,256]{3,2,1,0:T(4,128)S(1)}, s32[4]{0:T(128)S(1)}, bf16[1,512,1024]{1,2,0:T(...) while((s32[]{:T(128)}, ...), condition=%wide.region_9.10_spmd, body=%wide.region_6.9_spmd.sunk | while | flops 137362432 | bytes 8683711 | solution.py:565
  282.6 2.9 fusion.74
  285.9 15.0 %fusion.20 = (bf16[256,4096]{1,0:T(8,128)(2,1)S(1)}, f32[256,4096]{1,0:T(8,128)}) fusion(f32[4096]{0:T(1024)S(1)} %slice_bitcast_fusion, bf16[1024,4096]{1,0:T(8,128)(2,1)} %bitcast.458, f32[256,1024]{1,0:T(8,128)S(1)} %get-tuple-element.844, f32[1024]{0:T(1024)S(1)} %add.292, f32[1024]{0:T(1024)S(1)} %mul.304, f32[256]{0:T(256)S(1)} %add_rsqrt_fusion.1, ...), kind=kOutput, calls=%fused_computation.62 | convolution fusion | flops 2218000384 | bytes 15755264 | tf_op jit(solution)/shard_map/dot_general | solution.py:26
  300.9 6.6 fusion.75
  307.9 2.1 fusion.55
  310.1 2.7 fusion.67
  312.8 8.6 %fusion.76 = (f32[4096]{0:T(1024)S(1)}, bf16[256,4096]{1,0:T(8,128)(2,1)S(1)}) fusion(f32[256,4096]{1,0:T(8,128)} %get-tuple-element.846, bf16[4096,1024]{1,0:T(8,128)(2,1)} %bitcast.461, f32[256,1024]{1,0:T(8,128)} %get-tuple-element.802), kind=kOutput, calls=%fused_computation.206 | convolution fusion | flops 2159276032 | bytes 15745024 | tf_op jit(solution)/shard_map/dot_general | solution.py:36
  321.4 6.9 multiply_reduce_fusion.2
  331.3 32.9 %while.63 = (s32[]{:T(128)}, bf16[4,1,256,256]{2,3,1,0:T(8,128)(2,1)}, bf16[4,1,512,256]{2,3,1,0:T(8,128)(2,1)}, f32[4,1,512,256]{2,3,1,0:T(8,128)}, s32[4]{0:T(...) while((s32[]{:T(128)}, ...), condition=%wide.region_20.21_spmd, body=%wide.region_18.20_spmd.sunk | while | flops 339213312 | bytes 21647588 | solution.py:596
  364.3 3.4 fusion.83
  368.8 2.3 add_convert_fusion.2
  372.3 3.0 multiply_reduce_fusion.3
  378.3 67.1 %while.65 = (s32[]{:T(128)}, bf16[4,1,256,256]{2,3,1,0:T(8,128)(2,1)}, bf16[4,1,1024,256]{2,3,1,0:T(8,128)(2,1)}, f32[4,1,1024,256]{2,3,1,0:T(8,128)}, s32[4]{0:...) while((s32[]{:T(128)}, ...), condition=%wide.region_25.26_spmd.clone, body=%wide.region_23.25_spmd.clone.sunk | while | flops 684456960 | bytes 59414812 | solution.py:596
  381.7 2.7 fusion.233
  384.9 3.9 multiply_reduce_fusion.14
  398.5 2.7 fusion.233
  401.6 3.9 multiply_reduce_fusion.14
  415.3 2.7 fusion.233
  418.4 3.9 multiply_reduce_fusion.14
  432.0 2.7 fusion.233
  435.1 3.9 multiply_reduce_fusion.14
  445.4 4.8 fusion.84
  451.8 3.7 add_convert_fusion
  455.5 2.1 convolution_convert_fusion.9
  457.6 2.1 convolution_convert_fusion.8
  459.7 2.7 convolution_convert_fusion.7
  462.4 2.6 convolution_convert_fusion.6
  465.0 2.1 convolution_convert_fusion.5
  469.4 4.0 convolution_convert_fusion.3
  473.4 3.7 convolution_convert_fusion.2
  477.2 2.5 bitcast_reduce_fusion
  484.1 147.7 %scatter_grads.2 = (f32[128,1024]{1,0:T(8,128)}, f32[256,1024]{1,0:T(8,128)}, f32[32,1024]{1,0:T(8,128)}, f32[32,1024]{1,0:T(8,128)}, f32[32,1024]{1,0:T(8,128)}...) custom-call(bf16[4,128,1024]{2,1,0:T(8,128)(2,1)} %bitcast.439, ...), custom_call_target="tpu_custom_call" | custom-call | tf_op jit(solution)/shard_map/scatter_grads/pallas_call | solution.py:517
  631.8 3.7 fusion.35
  636.2 5.6 convolution_convert_fusion.1
  641.8 5.7 convolution_convert_fusion
  647.6 90.9 %scatter_grads.3 = (f32[128,1024]{1,0:T(8,128)}, f32[32,4096]{1,0:T(8,128)}) custom-call(bf16[2,2,2,4,128,1024]{5,4,3,2,1,0:T(8,128)(2,1)} %bitcast.390, bf16[2,2,2,4,32,4096]{5,4,3,2,1,0:T(8,128)(2,1)} %bitcast.391), custom_call_target="tpu_custom_call" | custom-call | tf_op jit(solution)/shard_map/scatter_grads/pallas_call | solution.py:517
  (409 shorter events, 161.4 us)
Async XLA Ops:
  16.5 177.1 %copy-start.45 = (f32[480]{0:T(512)}, f32[480]{0:T(512)S(1)}, u32[]{:S(2)}) copy-start(f32[480]{0:T(512)S(1)} %broadcast_in_dim.149) | copy-start | bytes 5764
  215.7 4.0 copy-start.33
  215.7 4.0 copy-start.34
  255.6 6.9 copy-start.18
  282.6 18.4 %copy-start.11 = (bf16[1,256,1024]{1,2,0:T(8,128)(2,1)}, bf16[1,256,1024]{1,2,0:T(8,128)(2,1)S(1)}, u32[]{:S(2)}) copy-start(bf16[1,256,1024]{1,2,0:T(8,128)(2,1)S(1)} %get-tuple-element.1374) | copy-start | bytes 1572868
  282.6 18.3 %copy-start.13 = (bf16[4,1,256,256]{2,3,1,0:T(8,128)(2,1)}, bf16[4,1,256,256]{2,3,1,0:T(8,128)(2,1)S(1)}, u32[]{:S(2)}) copy-start(bf16[4,1,256,256]{2,3,1,0:T(8,128)(2,1)S(1)} %get-tuple-element.522) | copy-start | bytes 1572868
  285.5 15.4 %copy-start.43 = (f32[1024]{0:T(1024)}, f32[1024]{0:T(1024)S(1)}, u32[]{:S(2)}) copy-start(f32[1024]{0:T(1024)S(1)} %add.292) | copy-start | bytes 12292
  300.9 6.6 copy-start.24
  312.8 8.6 %copy-start.22 = (f32[256,1024]{1,0:T(8,128)S(1)}, f32[256,1024]{1,0:T(8,128)}, u32[]{:S(2)}) copy-start(f32[256,1024]{1,0:T(8,128)} %get-tuple-element.802) | copy-start | bytes 3145732
  321.4 6.9 copy-start.26
  321.4 8.3 %copy-start.9 = (bf16[2,2,2,4,32,1024]{5,4,3,2,1,0:T(8,128)(2,1)S(1)}, bf16[2,2,2,4,32,1024]{5,4,3,2,1,0:T(8,128)(2,1)}, u32[]{:S(2)}) copy-start(bf16[2,2,2,4,32,1024]{5,4,3,2,1,0:T(8,128)(2,1)} %get-tuple-element.523) | copy-start | bytes 6291460
  364.3 3.4 copy-start.10
  364.3 4.5 copy-start.53
  368.8 3.5 copy-start.4
  372.3 3.4 copy-start.20
  372.3 4.3 copy-start.8
  384.9 4.0 copy-start
  401.6 4.0 copy-start
  418.4 4.0 copy-start
  435.1 3.9 copy-start
  445.4 4.8 copy-start.2
  451.8 3.8 copy-start.5
  451.8 3.8 copy-start.14
  451.8 5.8 copy-start.19
  451.8 5.8 copy-start.21
  455.5 4.1 copy-start.55
  455.5 4.1 copy-start.56
  462.4 4.7 copy-start.28
  465.0 4.4 copy-start.50
  465.0 4.4 copy-start.54
  477.1 5.4 copy-start.47
  477.1 5.5 copy-start.17
  477.1 6.1 copy-start.46
  631.8 3.8 copy-start.48
  631.8 4.4 copy-start.23
  631.8 4.4 copy-start.25
  636.2 5.6 copy-start.27
  636.2 5.6 copy-start.44
  647.6 91.6 %copy-start.31 = (f32[128,1024]{1,0:T(8,128)S(1)}, f32[128,1024]{1,0:T(8,128)}, u32[]{:S(2)}) copy-start(f32[128,1024]{1,0:T(8,128)} %get-tuple-element.535) | copy-start | bytes 1572868
  647.6 92.4 %copy-start.42 = (f32[32,1024]{1,0:T(8,128)S(1)}, f32[32,1024]{1,0:T(8,128)}, u32[]{:S(2)}) copy-start(f32[32,1024]{1,0:T(8,128)} %get-tuple-element.1349) | copy-start | bytes 393220
  647.6 93.1 %copy-start.41 = (f32[32,1024]{1,0:T(8,128)S(1)}, f32[32,1024]{1,0:T(8,128)}, u32[]{:S(2)}) copy-start(f32[32,1024]{1,0:T(8,128)} %get-tuple-element.1350) | copy-start | bytes 393220
  647.6 93.7 %copy-start.40 = (f32[32,1024]{1,0:T(8,128)S(1)}, f32[32,1024]{1,0:T(8,128)}, u32[]{:S(2)}) copy-start(f32[32,1024]{1,0:T(8,128)} %get-tuple-element.1351) | copy-start | bytes 393220
  647.6 94.4 %copy-start.39 = (f32[32,1024]{1,0:T(8,128)S(1)}, f32[32,1024]{1,0:T(8,128)}, u32[]{:S(2)}) copy-start(f32[32,1024]{1,0:T(8,128)} %get-tuple-element.1352) | copy-start | bytes 393220
  647.6 95.0 %copy-start.38 = (f32[32,1024]{1,0:T(8,128)S(1)}, f32[32,1024]{1,0:T(8,128)}, u32[]{:S(2)}) copy-start(f32[32,1024]{1,0:T(8,128)} %get-tuple-element.1358) | copy-start | bytes 393220
  647.6 95.7 %copy-start.37 = (f32[32,1024]{1,0:T(8,128)S(1)}, f32[32,1024]{1,0:T(8,128)}, u32[]{:S(2)}) copy-start(f32[32,1024]{1,0:T(8,128)} %get-tuple-element.1359) | copy-start | bytes 393220
  647.6 96.3 %copy-start.36 = (f32[32,1024]{1,0:T(8,128)S(1)}, f32[32,1024]{1,0:T(8,128)}, u32[]{:S(2)}) copy-start(f32[32,1024]{1,0:T(8,128)} %get-tuple-element.1360) | copy-start | bytes 393220
  647.6 97.0 %copy-start.35 = (f32[32,1024]{1,0:T(8,128)S(1)}, f32[32,1024]{1,0:T(8,128)}, u32[]{:S(2)}) copy-start(f32[32,1024]{1,0:T(8,128)} %get-tuple-element.1361) | copy-start | bytes 393220
  738.6 8.5 %copy-start.32 = (f32[128,1024]{1,0:T(8,128)S(1)}, f32[128,1024]{1,0:T(8,128)}, u32[]{:S(2)}) copy-start(f32[128,1024]{1,0:T(8,128)} %get-tuple-element.1369) | copy-start | bytes 1572868
  (12 other events, 25.8 us)

commit v3 on v2

--- a/solution.py
+++ b/solution.py
@@ -489,7 +489,7 @@
         )
         refs = refs[held:]
     meet(cube, here)
-    in_slots([stages for stages, _ in plans], 2)
+    in_slots([stages for stages, _ in plans], 4)
     for _, finish in plans:
         finish()
 
@@ -529,72 +529,111 @@
     )(*arrays)
 
 
-def head_slice(array, group_index, group_size):
-    part = lax.dynamic_slice_in_dim(array, group_index * group_size * DH, group_size * DH, 2)
-    return part.reshape(array.shape[0], array.shape[1], group_size, DH)
-
-
-def regroup(stacked):
-    group_count, seq_count, row_count, group_span = stacked.shape
-    return jnp.moveaxis(stacked, 0, 2).reshape(seq_count, row_count, group_count * group_span)
-
-
-def masked_scores(query_part, key_part, allow):
-    scores = jnp.einsum("sqhd,skhd->shqk", query_part, key_part, preferred_element_type=F32)
-    if allow is not None:
-        scores = jnp.where(allow[:, None], scores, NEG)
-    return scores
-
-
-def attn_forward(queries, keys, values, allow):
-    group_size = math.gcd(H, 4)
-
-    def one_group(group_index):
-        query_part = head_slice(queries, group_index, group_size)
-        key_part = head_slice(keys, group_index, group_size)
-        value_part = head_slice(values, group_index, group_size)
-        scores = masked_scores(query_part, key_part, allow)
-        row_max = jnp.max(scores, axis=-1, keepdims=True)
-        expon = jnp.exp(scores - row_max)
-        row_total = jnp.sum(expon, axis=-1, keepdims=True)
-        probab = (expon / row_total).astype(BF)
-        attended = jnp.einsum("shqk,skhd->sqhd", probab, value_part, preferred_element_type=F32)
-        attended = attended.reshape(queries.shape[0], queries.shape[1], group_size * DH)
-        return (attended, (row_max + jnp.log(row_total))[..., 0])
-
-    stacked, log_sums = lax.map(one_group, jnp.arange(H // group_size, dtype=jnp.int32))
-    return (regroup(stacked), log_sums)
-
-
-def attn_backward(queries, keys, values, allow, log_sums, grad_attended):
-    group_size = math.gcd(H, 4)
-
-    def one_group(items):
-        group_index, log_part = items
-        query_part = head_slice(queries, group_index, group_size)
-        key_part = head_slice(keys, group_index, group_size)
-        value_part = head_slice(values, group_index, group_size)
-        grad_part = head_slice(grad_attended, group_index, group_size)
-        scores = masked_scores(query_part, key_part, allow)
-        probab = jnp.exp(scores - log_part[..., None])
-        grad_probs = jnp.einsum("sqhd,skhd->shqk", grad_part, value_part, preferred_element_type=F32)
-        row_delta = jnp.sum(probab * grad_probs, axis=-1, keepdims=True)
-        grad_scores = (probab * (grad_probs - row_delta)).astype(BF)
-        grad_query = jnp.einsum("shqk,skhd->sqhd", grad_scores, key_part, preferred_element_type=F32)
-        grad_key = jnp.einsum("shqk,sqhd->skhd", grad_scores, query_part, preferred_element_type=F32)
-        grad_value = jnp.einsum(
-            "shqk,sqhd->skhd", probab.astype(BF), grad_part, preferred_element_type=F32
-        )
-        seq_count = queries.shape[0]
-        return (
-            grad_query.reshape(seq_count, queries.shape[1], group_size * DH),
-            grad_key.reshape(seq_count, keys.shape[1], group_size * DH),
-            grad_value.reshape(seq_count, keys.shape[1], group_size * DH),
-        )
-
-    group_ids = jnp.arange(H // group_size, dtype=jnp.int32)
-    grad_queries, grad_keys, grad_values = lax.map(one_group, (group_ids, log_sums))
-    return (regroup(grad_queries), regroup(grad_keys), regroup(grad_values))
+def write_bias(bias, key_ids, query_ids):
+    same = key_ids[:, 0:1] == query_ids[0:1, :]
+    early = key_ids[:, 1:2] <= query_ids[1:2, :]
+    bias[...] = jnp.where(same & early, 0.0, NEG)
+
+
+def one_head(array, head):
+    lane = lax.broadcasted_iota(jnp.int32, array.shape, 1)
+    keep = (lane < DH) if head == 0 else (lane >= DH)
+    return jnp.where(keep, array, jnp.zeros_like(array))
+
+
+def attend_kernel(masked, *refs):
+    if masked:
+        key_ids, query_ids, query_ref, key_ref, value_ref, out_ref, log_ref, bias = refs
+        pl.when(pl.program_id(0) == 0)(lambda: write_bias(bias, key_ids[...], query_ids[...]))
+    else:
+        query_ref, key_ref, value_ref, out_ref, log_ref = refs
+    query, key = query_ref[...], key_ref[...]
+    value_t = value_ref[...].T
+    outs, logs = [], []
+    for head in range(2):
+        scores = right_trans(key, one_head(query, head))
+        if masked:
+            scores = scores + bias[...]
+        top = jnp.max(scores, axis=0, keepdims=True)
+        expon = jnp.exp(scores - top)
+        total = jnp.sum(expon, axis=0, keepdims=True)
+        got = matmul(value_t[head * DH : (head + 1) * DH], expon.astype(BF))
+        outs.append(got * (1.0 / total))
+        logs.append(top + jnp.log(total))
+    out_ref[...] = jnp.concatenate(outs, axis=0).T.astype(BF)
+    log_ref[0] = jnp.concatenate(logs, axis=0)
+
+
+def attend_back_kernel(masked, *refs):
+    if masked:
+        key_ids, query_ids, query_ref, key_ref, value_ref, grad_ref, log_ref = refs[:7]
+        dq_ref, dk_ref, dv_ref, bias = refs[7:]
+        pl.when(pl.program_id(0) == 0)(lambda: write_bias(bias, key_ids[...], query_ids[...]))
+    else:
+        query_ref, key_ref, value_ref, grad_ref, log_ref, dq_ref, dk_ref, dv_ref = refs
+    query, key, value, grad = query_ref[...], key_ref[...], value_ref[...], grad_ref[...]
+    key_t = key.T
+    dq, dk, dv = [], None, None
+    for head in range(2):
+        query_head, grad_head = one_head(query, head), one_head(grad, head)
+        scores = right_trans(key, query_head)
+        if masked:
+            scores = scores + bias[...]
+        probs = jnp.exp(scores - log_ref[0, head : head + 1, :])
+        grad_probs = right_trans(value, grad_head)
+        delta = jnp.sum(probs * grad_probs, axis=0, keepdims=True)
+        grad_scores = (probs * (grad_probs - delta)).astype(BF)
+        dq.append(matmul(key_t[head * DH : (head + 1) * DH], grad_scores))
+        dk_head = matmul(grad_scores, query_head)
+        dv_head = matmul(probs.astype(BF), grad_head)
+        dk = dk_head if dk is None else dk + dk_head
+        dv = dv_head if dv is None else dv + dv_head
+    scale = DH ** (-0.5)
+    dq_ref[...] = (jnp.concatenate(dq, axis=0).T.astype(BF).astype(F32) * scale).astype(BF)
+    dk_ref[...] = dk.astype(BF)
+    dv_ref[...] = dv.astype(BF)
+
+
+def attend_call(back, ids, arrays):
+    rows, width = arrays[0].shape
+    keys = arrays[1].shape[0]
+    pair = 2 * DH
+    steps = width // pair
+    masked = ids is not None
+    by_query = pl.BlockSpec((rows, pair), lambda i: (0, i))
+    by_key = pl.BlockSpec((keys, pair), lambda i: (0, i))
+    logs = pl.BlockSpec((1, 2, rows), lambda i: (i, 0, 0))
+    in_specs = [by_query, by_key, by_key]
+    if masked:
+        in_specs = [
+            pl.BlockSpec((keys, 2), lambda i: (0, 0)),
+            pl.BlockSpec((2, rows), lambda i: (0, 0)),
+        ] + in_specs
+        arrays = list(ids) + list(arrays)
+    log_shape = jax.ShapeDtypeStruct((steps, 2, rows), F32)
+    query_shape = jax.ShapeDtypeStruct((rows, width), BF)
+    key_shape = jax.ShapeDtypeStruct((keys, width), BF)
+    if back:
+        in_specs += [by_query, logs]
+        out_specs, out_shape = [by_query, by_key, by_key], [query_shape, key_shape, key_shape]
+    else:
+        out_specs, out_shape = [by_query, logs], [query_shape, log_shape]
+    products = 7 if back else 2
+    return pl.pallas_call(
+        functools.partial(attend_back_kernel if back else attend_kernel, masked),
+        grid=(steps,),
+        in_specs=in_specs,
+        out_specs=out_specs,
+        out_shape=out_shape,
+        scratch_shapes=[pltpu.VMEM((keys, rows), F32)] if masked else [],
+        cost_estimate=pl.CostEstimate(
+            flops=2 * products * rows * keys * width,
+            bytes_accessed=2 * width * (rows + keys) * products,
+            transcendentals=rows * keys * width // DH,
+        ),
+        compiler_params=pltpu.CompilerParams(vmem_limit_bytes=48 * 1024 * 1024),
+        name="attend_back" if back else "attend",
+    )(*arrays)
 
 
 WIDE = 13
@@ -680,23 +719,22 @@
     offset = lax.axis_index("seq") * local_rows
     query_doc = lax.dynamic_slice_in_dim(doc_ids, offset, local_rows, 1)
     query_block = lax.dynamic_slice_in_dim(block_ids, offset, local_rows, 1)
-    allow = (query_doc[:, :, None] == doc_ids[:, None, :]) & (
-        block_ids[:, None, :] <= query_block[:, :, None]
+    ids = (
+        jnp.concatenate([doc_ids, block_ids], axis=0).T,
+        jnp.concatenate([query_doc, query_block], axis=0),
     )
     token_float = flat.astype(F32)
     queries = ((matmul(flat, query_mat) + query_vec) * scale).astype(BF)
     all_keys = matmul(tok_all, key_mat).astype(BF)
     all_values = (matmul(tok_all, value_mat) + value_vec).astype(BF)
-    self_out, self_logs = attn_forward(queries[None], all_keys[None], all_values[None], allow)
-    self_outb = self_out[0].astype(BF)
+    self_outb, self_logs = attend_call(False, ids, [queries, all_keys, all_values])
     first_sum = token_float + matmul(self_outb, out_mat) + out_vec
     normed_one, inv_one = layer_stats(first_sum)
     stream_one = (normed_one * gain_first + shift_first).astype(BF)
     probe = ((matmul(stream_one, probe_mat) + probe_vec) * scale).astype(BF)
     enc_keys = matmul(enc_all, lookup_mat).astype(BF)
     enc_values = (matmul(enc_all, content_mat) + content_vec).astype(BF)
-    cross_out, cross_logs = attn_forward(probe[None], enc_keys[None], enc_values[None], None)
-    cross_outb = cross_out[0].astype(BF)
+    cross_outb, cross_logs = attend_call(False, None, [probe, enc_keys, enc_values])
     second_sum = stream_one.astype(F32) + matmul(cross_outb, merge_mat) + merge_vec
     normed_two, inv_two = layer_stats(second_sum)
     stream_two = (normed_two * gain_second + shift_second).astype(BF)
@@ -740,17 +778,14 @@
     g_merge_vec = jnp.sum(grad_second, axis=0)
     g_merge_mat = left_outer(cross_outb, merge_rows)
     grad_cross = right_trans(merge_rows, merge_mat).astype(BF)
-    grad_probe, grad_enc_keys, grad_enc_values = attn_backward(
-        probe[None], enc_keys[None], enc_values[None], None, cross_logs, grad_cross[None]
-    )
-    probe_rows = (grad_probe[0].astype(BF).astype(F32) * scale).astype(BF)
+    probe_rows, enc_key_rows, enc_value_rows = attend_call(
+        True, None, [probe, enc_keys, enc_values, grad_cross, cross_logs]
+    )
     g_probe_vec = jnp.sum(probe_rows.astype(F32), axis=0)
     g_probe_mat = left_outer(stream_one, probe_rows)
-    enc_key_rows = grad_enc_keys[0].astype(BF)
-    enc_value_rows = grad_enc_values[0].astype(BF)
     g_lookup_mat = left_outer(enc_all, enc_key_rows)
     g_content_mat = left_outer(enc_all, enc_value_rows)
-    g_content_vec = jnp.sum(grad_enc_values[0], axis=0)
+    g_content_vec = jnp.sum(enc_value_rows.astype(F32), axis=0)
     enc_part = right_trans(enc_key_rows, lookup_mat) + right_trans(enc_value_rows, content_mat)
     grad_one = grad_second + right_trans(probe_rows, probe_mat)
     g_shift_first = jnp.sum(grad_one, axis=0)
@@ -760,14 +795,11 @@
     g_out_vec = jnp.sum(grad_first, axis=0)
     g_out_mat = left_outer(self_outb, out_rows)
     grad_self = right_trans(out_rows, out_mat).astype(BF)
-    grad_query, grad_keys, grad_values = attn_backward(
-        queries[None], all_keys[None], all_values[None], allow, self_logs, grad_self[None]
-    )
-    query_rows = (grad_query[0].astype(BF).astype(F32) * scale).astype(BF)
-    key_rows = grad_keys[0].astype(BF)
-    value_rows = grad_values[0].astype(BF)
+    query_rows, key_rows, value_rows = attend_call(
+        True, ids, [queries, all_keys, all_values, grad_self, self_logs]
+    )
     g_query_vec = jnp.sum(query_rows.astype(F32), axis=0)
-    g_value_vec = jnp.sum(grad_values[0], axis=0)
+    g_value_vec = jnp.sum(value_rows.astype(F32), axis=0)
     g_query_mat = left_outer(flat, query_rows)
     g_key_mat = left_outer(tok_all, key_rows)
     g_value_mat = left_outer(tok_all, value_rows)

time: 758 us -> 597 us (0.79)
  local copies, waits for them, and re-layouts: 97.4 us -> 18.8 us
  matrix products: 180 us -> 105 us
  Pallas kernels: 413 us -> 436 us
  other arithmetic: 44.3 us -> 24.6 us
  loops' own time: 12 us -> 0 us
    dot_general x56 -> x0, matrix products: 59.2 us -> none  [the longest x16 19.7 us: masked_scores(): jnp.einsum('sqhd,skhd->shqk', query_part, key_part, preferred_element_typ...]
    pallas_call x0 -> x4, Pallas kernels: none -> 55.2 us  [attend_call(): pl.pallas_call(functools.partial(attend_back_kernel if back else attend_k...]
    dynamic_slice x64 -> x0, local copies, waits for them, and re-layouts: 39.6 us -> none  [the longest x48 30.3 us: head_slice(): lax.dynamic_slice_in_dim(array, group_index * group_size * DH, group_size...]
    pallas_call x2, Pallas kernels: 239 us -> 207 us  [scatter_all(): pl.pallas_call(functools.partial(scatter_kernel, cube, pieces), out_shape...]
    dynamic_update_slice x32 -> x0, local copies, waits for them, and re-layouts: 22 us -> none  [the longest x16 13.9 us: attn_backward(): lax.map(one_group, (group_ids, log_sums))]
    another operation x4 -> x0, loops' own time: 12 us -> none  [the longest x2 6.27 us: attn_backward(): lax.map(one_group, (group_ids, log_sums))]
    dot_general x10, matrix products: 37.9 us -> 26.2 us  [right_trans(): lax.dot_general(left_arg, right_arg, (((1,), (1,)), ((), ())), preferred_...]
    unnamed x127 -> x125, local copies, waits for them, and re-layouts: 22.9 us -> 12.5 us
where the time goes in v3:
time: 597 us; the launch traced here: 587 us
  Pallas kernels  436 us (73%)
  matrix products  105 us (18%)
  other arithmetic  24.6 us (4%)
  local copies, waits for them, and re-layouts  18.8 us (3%)
    pallas_call x2, Pallas kernels, scatter_all(): pl.pallas_call(functools.partial(scatter_kernel, cube, pieces), out_shape...  207 us
    pallas_call x1, Pallas kernels, gather_all(): pl.pallas_call(functools.partial(gather_kernel, cube, pieces), out_shape=...  175 us
    pallas_call x4, Pallas kernels, attend_call(): pl.pallas_call(functools.partial(attend_back_kernel if back else attend_k...  55.2 us
    dot_general x10, matrix products, matmul(): return jnp.dot(left_arg, right_arg, preferred_element_type=F32)  45.9 us
    dot_general x10, matrix products, left_outer(): lax.dot_general(left_arg, right_arg, (((0,), (0,)), ((), ())), preferred_...  32.6 us
    dot_general x10, matrix products, right_trans(): lax.dot_general(left_arg, right_arg, (((1,), (1,)), ((), ())), preferred_...  26.2 us
    convert_element_type x10, other arithmetic, local(): blocks = [w.astype(BF).reshape(block_shape(*w.shape)) for w in weights]  15.9 us
    unnamed x125, local copies, waits for them, and re-layouts  12.5 us

profile of v3, /device:TPU:0, one launch (start us, length us, event | category | flops | bytes accessed | tf_op | source)
XLA Modules:
  0.0 586.7 jit_solution(2974041641188814550)
XLA Ops:
  0.7 1.6 convert_element_type.147.refs_2_
  2.3 1.5 convert_element_type.148.refs_3_
  3.8 1.5 convert_element_type.149.refs_4_
  5.4 1.5 convert_element_type.150.refs_5_
  6.9 1.5 convert_element_type.151.refs_6_
  8.5 1.5 convert_element_type.152.refs_7_
  10.0 1.5 convert_element_type.153.refs_8_
  11.5 1.5 convert_element_type.154.refs_9_
  13.1 1.8 convert_element_type.155.refs_10_
  14.9 1.8 convert_element_type.156.refs_11_
  16.6 1.5 concatenate.15
  18.1 174.6 %gather_weights.1 = (bf16[4,256,1024]{2,1,0:T(8,128)(2,1)}, bf16[4,128,1024]{2,1,0:T(8,128)(2,1)}, bf16[2,2,2,4,32,1024]{5,4,3,2,1,0:T(8,128)(2,1)}, bf16[2,2,2,...) custom-call(bf16[256,1024]{1,0:T(8,128)(2,1)} %bitcast.145, ...), custom_call_target="tpu_custom_call" | custom-call | tf_op jit(solution)/shard_map/gather_weights/pallas_call | solution.py:289
  195.1 2.4 fusion.27.refs_2_
  197.5 6.1 %convolution_convert_fusion.10.refs_3_ = bf16[1024,1024]{1,0:T(8,128)(2,1)} fusion(bf16[1024,1024]{1,0:T(8,128)(2,1)} %bitcast.169, bf16[1024,1024]{1,0:T(8,128)(2,1)} %bitcast.175), kind=kOutput, calls=%fused_computation.41 | convolution fusion | flops 2148532224 | bytes 6291456 | tf_op jit(solution)/shard_map/dot_general | solution.py:26
  203.7 4.9 add_convert_fusion.1.refs_4_
  208.6 14.3 %attend.2 = (bf16[256,1024]{1,0:T(8,128)(2,1)S(1)}, f32[8,2,256]{2,1,0:T(2,128)S(1)}) custom-call(s32[1024,2]{1,0:T(8,128)S(1)} %bitcast.128, s32[2,256]{1,0:T(2,128)S(1)} %pad_add_fusion.1.refs_1_, bf16[256,1024]{1,0:T(8,128)(2,1)S(1)} %fusion.27.refs_2_, bf16[1024,1024]{1,0:T(8,128)(2,1)S(1)} %copy-done.8, bf16[1024,1024]{1,0:T(8,128)(2,1)S(1)} %add_convert_fusion.1.refs_4_), custom_call_target="tpu_custom_call" | custom-call | flops 1073741824 | bytes 5242880 | tf_op jit(solution)/shard_map/attend/pallas_call | solution.py:622
  224.8 2.3 fusion.25.refs_0_
  227.1 3.2 convolution_convert_fusion.11.refs_1_
  230.4 3.5 add_convert_fusion.3.refs_2_
  233.9 9.3 %attend.3 = (bf16[256,1024]{1,0:T(8,128)(2,1)S(1)}, f32[8,2,256]{2,1,0:T(2,128)S(1)}) custom-call(bf16[256,1024]{1,0:T(8,128)(2,1)S(1)} %fusion.25.refs_0_, bf16[512,1024]{1,0:T(8,128)(2,1)S(1)} %convolution_convert_fusion.11.refs_1_, bf16[512,1024]{1,0:T(8,128)(2,1)S(1)} %add_convert_fusion.3.refs_2_), custom_call_target="tpu_custom_call" | custom-call | flops 536870912 | bytes 3145728 | tf_op jit(solution)/shard_map/attend/pallas_call | solution.py:622
  244.5 15.3 %fusion.2 = (bf16[256,4096]{1,0:T(8,128)(2,1)S(1)}, f32[256,4096]{1,0:T(8,128)}) fusion(f32[4096]{0:T(1024)S(1)} %slice_bitcast_fusion, bf16[1024,4096]{1,0:T(8,128)(2,1)} %bitcast.163, f32[256,1024]{1,0:T(8,128)S(1)} %get-tuple-element.146, f32[1024]{0:T(1024)S(1)} %add.198, f32[1024]{0:T(1024)S(1)} %mul.199, f32[256]{0:T(256)S(1)} %add_rsqrt_fusion.1, ...), kind=kOutput, calls=%fused_computation.8 | convolution fusion | flops 2218000384 | bytes 15755264 | tf_op jit(solution)/shard_map/dot_general | solution.py:26
  259.8 6.7 %fusion.50 = (f32[256]{0:T(256)S(1)}, f32[256,1024]{1,0:T(8,128)S(1)}) fusion(f32[1024]{0:T(1024)S(1)} %add.205, bf16[256,4096]{1,0:T(8,128)(2,1)S(1)} %get-tuple-element.147, bf16[4096,1024]{1,0:T(8,128)(2,1)} %bitcast.167, f32[1024]{0:T(1024)S(1)} %add.198, f32[1024]{0:T(1024)S(1)} %mul.199, f32[256]{0:T(256)S(1)} %add_rsqrt_fusion.1, ...), kind=kOutput, calls=%fused_computation.142 | convolution fusion | flops 2149842688 | bytes 12598272 | tf_op jit(solution)/shard_map/dot_general | solution.py:26
  267.7 1.7 fusion.31
  269.6 2.6 fusion.43
  272.2 7.4 %fusion.51 = (f32[4096]{0:T(1024)S(1)}, bf16[256,4096]{1,0:T(8,128)(2,1)S(1)}) fusion(f32[256,4096]{1,0:T(8,128)} %get-tuple-element.148, bf16[4096,1024]{1,0:T(8,128)(2,1)} %bitcast.168, f32[256,1024]{1,0:T(8,128)S(1)} %get-tuple-element.124), kind=kOutput, calls=%fused_computation.143 | convolution fusion | flops 2159276032 | bytes 15745024 | tf_op jit(solution)/shard_map/dot_general | solution.py:36
  279.7 2.7 multiply_reduce_fusion
  284.0 11.8 %attend_back.2 = (bf16[256,1024]{1,0:T(8,128)(2,1)S(1)}, bf16[512,1024]{1,0:T(8,128)(2,1)S(1)}, bf16[512,1024]{1,0:T(8,128)(2,1)S(1)}) custom-call(bf16[256,1024]{1,0:T(8,128)(2,1)S(1)} %fusion.25.refs_0_, bf16[512,1024]{1,0:T(8,128)(2,1)S(1)} %copy-done.5, bf16[512,1024]{1,0:T(8,128)(2,1)S(1)} %copy-done.7, ...), custom_call_target="tpu_custom_call" | custom-call | flops 1879048192 | bytes 11010048 | tf_op jit(solution)/shard_map/attend_back/pallas_call | solution.py:622
  295.8 1.3 fusion.52
  297.4 2.3 add_convert_fusion.2
  299.6 1.1 multiply_reduce_fusion.1
  302.1 19.9 %attend_back.3 = (bf16[256,1024]{1,0:T(8,128)(2,1)S(1)}, bf16[1024,1024]{1,0:T(8,128)(2,1)S(1)}, bf16[1024,1024]{1,0:T(8,128)(2,1)}) custom-call(s32[1024,2]{1,0:T(8,128)S(1)} %bitcast.129, s32[2,256]{1,0:T(2,128)S(1)} %pad_add_fusion.1.refs_1_, bf16[256,1024]{1,0:T(8,128)(2,1)S(1)} %copy-done.3, bf16[1024,1024]{1,0:T(8,128)(2,1)} %convolution_convert_fusion.10.refs_3_, ...), custom_call_target="tpu_custom_call" | custom-call | flops 3758096384 | bytes 18350080 | tf_op jit(solution)/shard_map/attend_back/pallas_call | solution.py:622
  322.0 2.4 fusion.53
  324.4 3.8 add_convert_fusion
  328.2 2.1 convolution_convert_fusion.9
  330.2 2.1 convolution_convert_fusion.8
  332.3 2.6 convolution_convert_fusion.7
  335.0 2.6 convolution_convert_fusion.6
  337.6 2.1 convolution_convert_fusion.5
  339.7 2.1 convolution_convert_fusion.4
  341.8 3.7 convolution_convert_fusion.3
  345.5 3.9 convolution_convert_fusion.2
  349.6 2.0 convert_reduce_fusion
  354.4 115.8 %scatter_grads.2 = (f32[128,1024]{1,0:T(8,128)}, f32[256,1024]{1,0:T(8,128)}, f32[32,1024]{1,0:T(8,128)}, f32[32,1024]{1,0:T(8,128)}, f32[32,1024]{1,0:T(8,128)}...) custom-call(bf16[4,128,1024]{2,1,0:T(8,128)(2,1)} %bitcast.150, ...), custom_call_target="tpu_custom_call" | custom-call | tf_op jit(solution)/shard_map/scatter_grads/pallas_call | solution.py:517
  470.2 3.8 fusion.15
  474.7 5.6 convolution_convert_fusion.1
  480.3 5.7 convolution_convert_fusion
  486.1 90.8 %scatter_grads.3 = (f32[128,1024]{1,0:T(8,128)}, f32[32,4096]{1,0:T(8,128)}) custom-call(bf16[2,2,2,4,128,1024]{5,4,3,2,1,0:T(8,128)(2,1)} %bitcast.130, bf16[2,2,2,4,32,4096]{5,4,3,2,1,0:T(8,128)(2,1)} %bitcast.131), custom_call_target="tpu_custom_call" | custom-call | tf_op jit(solution)/shard_map/scatter_grads/pallas_call | solution.py:517
  583.6 1.9 copy.89
  (192 shorter events, 21.0 us)
Async XLA Ops:
  0.7 194.4 %copy-start.30 = (bf16[1,256,1024]{2,1,0:T(8,128)(2,1)S(1)}, bf16[1,256,1024]{2,1,0:T(8,128)(2,1)}, u32[]{:S(2)}) copy-start(bf16[1,256,1024]{2,1,0:T(8,128)(2,1)} %param.29) | copy-start | bytes 1572868
  0.7 194.0 %copy-start.46 = (s32[1,1024]{1,0:T(1,128)S(1)}, s32[1,1024]{1,0:T(1,128)}, u32[]{:S(2)}) copy-start(s32[1,1024]{1,0:T(1,128)} %param.33) | copy-start | bytes 12292
  0.7 194.0 %copy-start.47 = (s32[1,1024]{1,0:T(1,128)S(1)}, s32[1,1024]{1,0:T(1,128)}, u32[]{:S(2)}) copy-start(s32[1,1024]{1,0:T(1,128)} %param.32) | copy-start | bytes 12292
  195.0 13.6 %copy-start = (s32[2,1024]{0,1:T(8,128)}, s32[2,1024]{0,1:T(8,128)S(1)}, u32[]{:S(2)}) copy-start(s32[2,1024]{0,1:T(8,128)S(1)} %copy.62) | copy-start | bytes 24580
  197.5 11.1 %copy-start.2 = (bf16[256,1024]{1,0:T(8,128)(2,1)}, bf16[256,1024]{1,0:T(8,128)(2,1)S(1)}, u32[]{:S(2)}) copy-start(bf16[256,1024]{1,0:T(8,128)(2,1)S(1)} %fusion.27.refs_2_) | copy-start | bytes 1572868
  203.7 4.9 copy-start.8
  208.6 15.2 %copy-start.9 = (bf16[1024,1024]{1,0:T(8,128)(2,1)}, bf16[1024,1024]{1,0:T(8,128)(2,1)S(1)}, u32[]{:S(2)}) copy-start(bf16[1024,1024]{1,0:T(8,128)(2,1)S(1)} %add_convert_fusion.1.refs_4_) | copy-start | bytes 6291460
  208.6 14.3 %copy-start.25 = (bf16[2,2,2,4,32,1024]{5,4,3,2,1,0:T(8,128)(2,1)S(1)}, bf16[2,2,2,4,32,1024]{5,4,3,2,1,0:T(8,128)(2,1)}, u32[]{:S(2)}) copy-start(bf16[2,2,2,4,32,1024]{5,4,3,2,1,0:T(8,128)(2,1)} %get-tuple-element.69) | copy-start | bytes 6291460
  224.5 18.8 %copy-start.32 = (bf16[256,1024]{1,0:T(8,128)(2,1)}, bf16[256,1024]{1,0:T(8,128)(2,1)S(1)}, u32[]{:S(2)}) copy-start(bf16[256,1024]{1,0:T(8,128)(2,1)S(1)} %add_convert_fusion.6) | copy-start | bytes 1572868
  230.3 12.9 %copy-start.4 = (bf16[512,1024]{1,0:T(8,128)(2,1)}, bf16[512,1024]{1,0:T(8,128)(2,1)S(1)}, u32[]{:S(2)}) copy-start(bf16[512,1024]{1,0:T(8,128)(2,1)S(1)} %convolution_convert_fusion.11.refs_1_) | copy-start | bytes 3145732
  230.4 12.8 %copy-start.27 = (bf16[2,2,2,4,32,1024]{5,4,3,2,1,0:T(8,128)(2,1)S(1)}, bf16[2,2,2,4,32,1024]{5,4,3,2,1,0:T(8,128)(2,1)}, u32[]{:S(2)}) copy-start(bf16[2,2,2,4,32,1024]{5,4,3,2,1,0:T(8,128)(2,1)} %get-tuple-element.75) | copy-start | bytes 6291460
  233.9 10.1 %copy-start.6 = (bf16[512,1024]{1,0:T(8,128)(2,1)}, bf16[512,1024]{1,0:T(8,128)(2,1)S(1)}, u32[]{:S(2)}) copy-start(bf16[512,1024]{1,0:T(8,128)(2,1)S(1)} %add_convert_fusion.3.refs_2_) | copy-start | bytes 3145732
  244.1 38.4 %copy-start.14 = (f32[256,1024]{1,0:T(8,128)}, f32[256,1024]{1,0:T(8,128)S(1)}, u32[]{:S(2)}) copy-start(f32[256,1024]{1,0:T(8,128)S(1)} %get-tuple-element.146) | copy-start | bytes 3145732
  259.8 6.7 %copy-start.21 = (bf16[256,4096]{1,0:T(8,128)(2,1)}, bf16[256,4096]{1,0:T(8,128)(2,1)S(1)}, u32[]{:S(2)}) copy-start(bf16[256,4096]{1,0:T(8,128)(2,1)S(1)} %get-tuple-element.147) | copy-start | bytes 6291460
  259.8 8.0 %copy-start.17 = (bf16[1,256,1024]{2,1,0:T(8,128)(2,1)S(1)}, bf16[1,256,1024]{2,1,0:T(8,128)(2,1)}, u32[]{:S(2)}) copy-start(bf16[1,256,1024]{2,1,0:T(8,128)(2,1)} %param.31) | copy-start | bytes 1572868
  269.6 10.1 %slice-start = ((s8[8388608]{0:T(1024)(128)(4,1)}), s8[4194304]{0:T(1024)(128)(4,1)S(1)}, s32[]{:S(2)}) async-start(s8[8388608]{0:T(1024)(128)(4,1)} %bitcast.164), calls=%async_computation | async-start | bytes 8388608
  272.2 7.5 %copy-start.19 = (f32[256,1024]{1,0:T(8,128)}, f32[256,1024]{1,0:T(8,128)S(1)}, u32[]{:S(2)}) copy-start(f32[256,1024]{1,0:T(8,128)S(1)} %get-tuple-element.124) | copy-start | bytes 3145732
  272.2 7.5 %slice-start.1 = ((s8[8388608]{0:T(1024)(128)(4,1)}), s8[4194304]{0:T(1024)(128)(4,1)S(1)}, s32[]{:S(2)}) async-start(s8[8388608]{0:T(1024)(128)(4,1)} %bitcast.164), calls=%async_computation.1 | async-start | bytes 8388608
  279.6 2.8 copy-start.23
  279.7 3.2 copy-start.28
  283.6 12.1 %copy-start.52 = (bf16[2,2,2,4,32,1024]{5,4,3,2,1,0:T(8,128)(2,1)S(1)}, bf16[2,2,2,4,32,1024]{5,4,3,2,1,0:T(8,128)(2,1)}, u32[]{:S(2)}) copy-start(bf16[2,2,2,4,32,1024]{5,4,3,2,1,0:T(8,128)(2,1)} %get-tuple-element.72) | copy-start | bytes 6291460
  297.1 2.6 copy-start.13
  297.1 2.6 copy-start.34
  301.2 36.4 %copy-start.10 = (f32[256,1024]{1,0:T(8,128)}, f32[256,1024]{1,0:T(8,128)S(1)}, u32[]{:S(2)}) copy-start(f32[256,1024]{1,0:T(8,128)S(1)} %get-tuple-element.128) | copy-start | bytes 3145732
  302.1 19.9 %copy-start.50 = (bf16[2,2,2,4,32,1024]{5,4,3,2,1,0:T(8,128)(2,1)S(1)}, bf16[2,2,2,4,32,1024]{5,4,3,2,1,0:T(8,128)(2,1)}, u32[]{:S(2)}) copy-start(bf16[2,2,2,4,32,1024]{5,4,3,2,1,0:T(8,128)(2,1)} %get-tuple-element.66) | copy-start | bytes 6291460
  322.0 2.4 copy-start.29
  322.0 2.4 copy-start.49
  324.4 5.8 copy-start.33
  328.2 4.1 copy-start.53
  335.0 4.7 copy-start.31
  337.6 4.2 copy-start.48
  349.4 3.4 copy-start.18
  354.4 115.9 %copy-start.11 = (f32[256,1024]{1,0:T(8,128)S(1)}, f32[256,1024]{1,0:T(8,128)}, u32[]{:S(2)}) copy-start(f32[256,1024]{1,0:T(8,128)} %copy-done.10) | copy-start | bytes 3145732
  470.2 3.8 copy-start.45
  470.2 4.4 copy-start.20
  470.2 4.4 copy-start.22
  474.7 5.6 copy-start.15
  474.7 5.6 copy-start.24
  486.0 91.5 %copy-start.35 = (f32[128,1024]{1,0:T(8,128)S(1)}, f32[128,1024]{1,0:T(8,128)}, u32[]{:S(2)}) copy-start(f32[128,1024]{1,0:T(8,128)} %get-tuple-element.87) | copy-start | bytes 1572868
  486.0 92.3 %copy-start.44 = (f32[32,1024]{1,0:T(8,128)S(1)}, f32[32,1024]{1,0:T(8,128)}, u32[]{:S(2)}) copy-start(f32[32,1024]{1,0:T(8,128)} %get-tuple-element.189) | copy-start | bytes 393220
  486.0 92.9 %copy-start.43 = (f32[32,1024]{1,0:T(8,128)S(1)}, f32[32,1024]{1,0:T(8,128)}, u32[]{:S(2)}) copy-start(f32[32,1024]{1,0:T(8,128)} %get-tuple-element.190) | copy-start | bytes 393220
  486.0 93.6 %copy-start.42 = (f32[32,1024]{1,0:T(8,128)S(1)}, f32[32,1024]{1,0:T(8,128)}, u32[]{:S(2)}) copy-start(f32[32,1024]{1,0:T(8,128)} %get-tuple-element.191) | copy-start | bytes 393220
  486.0 94.2 %copy-start.41 = (f32[32,1024]{1,0:T(8,128)S(1)}, f32[32,1024]{1,0:T(8,128)}, u32[]{:S(2)}) copy-start(f32[32,1024]{1,0:T(8,128)} %get-tuple-element.192) | copy-start | bytes 393220
  486.0 94.9 %copy-start.40 = (f32[32,1024]{1,0:T(8,128)S(1)}, f32[32,1024]{1,0:T(8,128)}, u32[]{:S(2)}) copy-start(f32[32,1024]{1,0:T(8,128)} %get-tuple-element.198) | copy-start | bytes 393220
  486.1 95.5 %copy-start.39 = (f32[32,1024]{1,0:T(8,128)S(1)}, f32[32,1024]{1,0:T(8,128)}, u32[]{:S(2)}) copy-start(f32[32,1024]{1,0:T(8,128)} %get-tuple-element.199) | copy-start | bytes 393220
  486.1 96.2 %copy-start.38 = (f32[32,1024]{1,0:T(8,128)S(1)}, f32[32,1024]{1,0:T(8,128)}, u32[]{:S(2)}) copy-start(f32[32,1024]{1,0:T(8,128)} %get-tuple-element.200) | copy-start | bytes 393220
  486.1 96.8 %copy-start.37 = (f32[32,1024]{1,0:T(8,128)S(1)}, f32[32,1024]{1,0:T(8,128)}, u32[]{:S(2)}) copy-start(f32[32,1024]{1,0:T(8,128)} %get-tuple-element.201) | copy-start | bytes 393220
  576.9 8.5 %copy-start.36 = (f32[128,1024]{1,0:T(8,128)S(1)}, f32[128,1024]{1,0:T(8,128)}, u32[]{:S(2)}) copy-start(f32[128,1024]{1,0:T(8,128)} %get-tuple-element.209) | copy-start | bytes 1572868
  (8 other events, 10.4 us)

commit v4 on v3

--- a/solution.py
+++ b/solution.py
@@ -231,11 +231,22 @@
     return 2 * (cube.n_seq - 1) + 2 * cube.dp_bits
 
 
-def gather_kernel(cube, pieces, *refs):
+def gather_kernel(cube, pieces, casts, *refs):
     count = 1 + max(piece[0] for piece in pieces)
-    ins, outs = refs[:count], refs[count : 2 * count]
-    send_sem, recv_sem, local_sem = refs[2 * count :]
+    ins, outs = list(refs[:count]), refs[count : 2 * count]
+    wide, stage = refs[2 * count : -4][: len(casts)], refs[2 * count : -4][len(casts) :]
+    send_sem, recv_sem, local_sem, cast_sem = refs[-4:]
     here = Place(cube)
+    loads = [
+        pltpu.make_async_copy(ins[array], held, cast_sem.at[turn])
+        for turn, (array, held) in enumerate(zip(casts, wide))
+    ]
+    for copy in loads:
+        copy.start()
+    for array, copy, held, narrow in zip(casts, loads, wide, stage):
+        copy.wait()
+        narrow[...] = held[...].astype(BF)
+        ins[array] = narrow
     plans = []
     for index, (array, full, variant, col, cols) in enumerate(pieces):
         lead = cube.dp_bits * full + 1
@@ -279,25 +290,33 @@
     return tuple(piece for _, _, piece in sorted(placed, key=lambda item: item[:2]))
 
 
-def gather_all(cube, arrays, kinds, collective_id):
+def gather_all(cube, arrays, kinds, casts, collective_id):
     pieces = cut_columns(kinds, arrays)
     outs = [
-        jax.ShapeDtypeStruct(cube.lead(full) + array.shape, array.dtype)
-        for array, full in zip(arrays, kinds)
+        jax.ShapeDtypeStruct(
+            cube.lead(full) + array.shape, BF if index in casts else array.dtype
+        )
+        for index, (array, full) in enumerate(zip(arrays, kinds))
     ]
     slots = gather_slots(cube)
+    anywhere = pl.BlockSpec(memory_space=pl.ANY)
     return pl.pallas_call(
-        functools.partial(gather_kernel, cube, pieces),
+        functools.partial(gather_kernel, cube, pieces, casts),
         out_shape=outs,
-        in_specs=[pl.BlockSpec(memory_space=pl.ANY)] * len(arrays),
-        out_specs=[pl.BlockSpec(memory_space=pl.ANY)] * len(arrays),
-        scratch_shapes=[
+        in_specs=[anywhere] * len(arrays),
+        out_specs=[anywhere] * len(arrays),
+        scratch_shapes=[pltpu.VMEM(arrays[index].shape, F32) for index in casts]
+        + [pltpu.VMEM(arrays[index].shape, BF) for index in casts]
+        + [
             pltpu.SemaphoreType.DMA((len(pieces), slots)),
             pltpu.SemaphoreType.DMA((len(pieces), slots)),
             pltpu.SemaphoreType.DMA((len(pieces),)),
+            pltpu.SemaphoreType.DMA((len(casts),)),
         ],
         compiler_params=pltpu.CompilerParams(
-            collective_id=collective_id, has_side_effects=True
+            collective_id=collective_id,
+            has_side_effects=True,
+            vmem_limit_bytes=60 * 1024 * 1024,
         ),
         name="gather_weights",
     )(*arrays)
@@ -494,20 +513,26 @@
         finish()
 
 
-def scatter_all(cube, arrays, kinds, collective_id):
+def scatter_shapes(cube, array, full, cols):
+    block = (array.shape[-2], cols)
+    shapes = []
+    if full:
+        for stage in range(-1, cube.dp_bits):
+            lead = (2,) * (cube.dp_bits - 1 - max(stage, 0)) + (cube.n_seq,)
+            shapes.append(lead + block)
+    else:
+        shapes.append((cube.n_seq,) + block)
+    shapes.append((cube.n_seq + 1,) + block)
+    return shapes
+
+
+def scatter_group(cube, arrays, kinds, collective_id):
     pieces = cut_columns(kinds, arrays)
     outs = [jax.ShapeDtypeStruct(array.shape[-2:], F32) for array in arrays]
     scratch = []
     for array, full, _, _, cols in pieces:
-        block = (arrays[array].shape[-2], cols)
-        dtype = arrays[array].dtype
-        if full:
-            for stage in range(-1, cube.dp_bits):
-                lead = (2,) * (cube.dp_bits - 1 - max(stage, 0)) + (cube.n_seq,)
-                scratch.append(pltpu.VMEM(lead + block, dtype))
-        else:
-            scratch.append(pltpu.VMEM((cube.n_seq,) + block, dtype))
-        scratch.append(pltpu.VMEM((cube.n_seq + 1,) + block, dtype))
+        for shape in scatter_shapes(cube, arrays[array], full, cols):
+            scratch.append(pltpu.VMEM(shape, arrays[array].dtype))
     slots = 2 * cube.n_seq + cube.dp_bits
     scratch += [
         pltpu.SemaphoreType.DMA((len(pieces), slots)),
@@ -527,6 +552,68 @@
         ),
         name="scatter_grads",
     )(*arrays)
+
+
+def scatter_all(cube, arrays, kinds, collective_id):
+    groups, room = [[]], 0
+    for index, (array, full) in enumerate(zip(arrays, kinds)):
+        shapes = scatter_shapes(cube, array, full, array.shape[-1])
+        need = sum(math.prod(shape) for shape in shapes) * array.dtype.itemsize
+        need += 4 * math.prod(array.shape[-2:])
+        if groups[-1] and room + need > 54 * 1024 * 1024:
+            groups.append([])
+            room = 0
+        groups[-1].append(index)
+        room += need
+    sums = []
+    for turn, group in enumerate(groups):
+        sums += scatter_group(
+            cube, [arrays[i] for i in group], [kinds[i] for i in group], collective_id + turn
+        )
+    return sums
+
+
+def hand_out_kernel(count, parts, *refs):
+    sums, vec, part_sum, part_own = refs[:count], refs[count], refs[count + 1], refs[count + 2]
+    refs = refs[count + 3 :]
+    outs, vec_outs, part_out = refs[:count], refs[count : count + len(parts)], refs[count + len(parts)]
+    held, sem = refs[-1 - count : -1], refs[-1]
+    ins = [
+        pltpu.make_async_copy(one, mid, sem.at[0, turn])
+        for turn, (one, mid) in enumerate(zip(sums, held))
+    ]
+    copies = [
+        pltpu.make_async_copy(mid, out, sem.at[1, turn])
+        for turn, (mid, out) in enumerate(zip(held, outs))
+    ]
+    for copy in ins:
+        copy.start()
+    for row, (size, out) in enumerate(zip(parts, vec_outs)):
+        out[...] = vec[row, 0:size]
+    part_out[...] = part_own[...] + part_sum[...]
+    for before, copy in zip(ins, copies):
+        before.wait()
+        copy.start()
+    for copy in copies:
+        copy.wait()
+
+
+def hand_out(sums, vec, parts, part_sum, part_own):
+    anywhere = pl.BlockSpec(memory_space=pl.ANY)
+    inside = pl.BlockSpec(memory_space=pltpu.VMEM)
+    count = len(sums)
+    return pl.pallas_call(
+        functools.partial(hand_out_kernel, count, parts),
+        out_shape=[jax.ShapeDtypeStruct(one.shape, F32) for one in sums]
+        + [jax.ShapeDtypeStruct((size,), F32) for size in parts]
+        + [jax.ShapeDtypeStruct(part_sum.shape, F32)],
+        in_specs=[anywhere] * count + [inside] * 3,
+        out_specs=[anywhere] * count + [inside] * (len(parts) + 1),
+        scratch_shapes=[pltpu.VMEM(one.shape, F32) for one in sums]
+        + [pltpu.SemaphoreType.DMA((2, count))],
+        compiler_params=pltpu.CompilerParams(vmem_limit_bytes=60 * 1024 * 1024),
+        name="hand_out",
+    )(*sums, vec, part_sum, part_own)
 
 
 def write_bias(bias, key_ids, query_ids):
@@ -692,21 +779,27 @@
     padded = -(-held // 1024) * 1024
     vec_block = (8, padded // 8)
     packed = jnp.concatenate(vectors + [expand_bias, jnp.zeros((padded - held,), F32)])
-    blocks = [w.astype(BF).reshape(block_shape(*w.shape)) for w in weights]
+    blocks = [w.reshape(block_shape(*w.shape)) for w in weights[:9]]
     kinds = [False, False] + [True] * (len(blocks) + 1)
     gathered = gather_all(
-        cube, [flat, enc_flat] + blocks + [packed.reshape(vec_block)], kinds, 0
-    )
+        cube,
+        [flat, enc_flat] + blocks + [packed.reshape(vec_block)],
+        kinds,
+        tuple(range(2, 2 + len(blocks))),
+        0,
+    )
+    late, vec_all = lax.optimization_barrier((reduce_weight.astype(BF), gathered[11]))
+    reduce_mat = lax.all_gather(late, ("dp", "seq"), axis=0, tiled=True)
     n_dev = cube.n_dev
     tok_all = gathered[0].reshape(cube.n_seq * local_rows, feat_width)
     enc_all = gathered[1].reshape(cube.n_seq * enc_local, feat_width)
     (
         query_mat, key_mat, value_mat, out_mat, probe_mat,
-        lookup_mat, content_mat, merge_mat, expand_mat, reduce_mat,
+        lookup_mat, content_mat, merge_mat, expand_mat,
     ) = [
-        g.reshape(w.shape[0] * n_dev, w.shape[1]) for g, w in zip(gathered[2:12], weights)
+        g.reshape(w.shape[0] * n_dev, w.shape[1]) for g, w in zip(gathered[2:11], weights)
     ]
-    vec_all = gathered[12].reshape(n_dev, padded)
+    vec_all = vec_all.reshape(n_dev, padded)
     wide_all = (
         vec_all[:, : WIDE * part].reshape(n_dev, WIDE, part).transpose(1, 0, 2).reshape(WIDE, -1)
     )
@@ -750,7 +843,11 @@
     grad_three = layer_back(grad_output * gain_third, normed_three, inv_three)
     reduce_rows = grad_three.astype(BF)
     g_reduce_vec = jnp.sum(grad_three, axis=0)
-    g_reduce_mat = left_outer(activated, reduce_rows)
+    g_reduce_mat = left_outer(activated, reduce_rows).astype(BF)
+    reduce_part = g_reduce_mat.reshape((cube.n_dp, cube.n_seq) + reduce_weight.shape)
+    reduce_part = lax.psum_scatter(reduce_part, "dp", scatter_dimension=0, tiled=True)
+    reduce_part = lax.psum_scatter(reduce_part, "seq", scatter_dimension=1, tiled=True)
+    reduce_sum = reduce_part.astype(F32)
     grad_act = right_trans(reduce_rows, reduce_mat)
     slope = 0.5 * (
         1.0 + jax.scipy.special.erf(expanded * INV_ROOT_TWO)
@@ -762,13 +859,6 @@
 
     def spread(grad, weight):
         return grad.astype(BF).reshape(cube.lead(True) + block_shape(*weight.shape))
-
-    expand_sum, reduce_sum = scatter_all(
-        cube,
-        [spread(g_reduce_mat, reduce_weight), spread(g_expand_mat, expand_weight)],
-        [True, True],
-        1,
-    )[::-1]
 
     grad_two = grad_three + right_trans(expand_rows, expand_mat)
     g_shift_second = jnp.sum(grad_two, axis=0)
@@ -812,20 +902,19 @@
             g_merge_vec, g_gain_second, g_shift_second, g_reduce_vec, g_gain_third, g_shift_third,
         ]
     )
-    vec_grads = jnp.concatenate(
-        [
-            wide_grads.reshape(WIDE, n_dev, part).transpose(1, 0, 2).reshape(n_dev, WIDE * part),
-            g_expand_vec.reshape(n_dev, long_part),
-            jnp.zeros((n_dev, padded - held), F32),
-        ],
-        axis=1,
-    ).reshape(cube.lead(True) + vec_block)
+    lanes = 128
+    vec_grads = jnp.pad(
+        wide_grads.reshape(WIDE, n_dev, part).transpose(1, 0, 2), ((0, 0), (0, 0), (0, lanes - part))
+    )
+    long_row = jnp.pad(g_expand_vec.reshape(n_dev, 1, long_part), ((0, 0), (0, 0), (0, lanes - long_part)))
+    vec_grads = jnp.concatenate([vec_grads, long_row, jnp.zeros((n_dev, 2, lanes), F32)], axis=1)
+    vec_grads = vec_grads.reshape(cube.lead(True) + (WIDE + 3, lanes))
     mats = [
-        g_merge_mat, g_probe_mat, g_lookup_mat, g_content_mat, g_out_mat,
+        g_expand_mat, g_merge_mat, g_probe_mat, g_lookup_mat, g_content_mat, g_out_mat,
         g_query_mat, g_key_mat, g_value_mat,
     ]
     shards = [
-        merge_weight, probe_weight, lookup_weight, content_weight, out_weight,
+        expand_weight, merge_weight, probe_weight, lookup_weight, content_weight, out_weight,
         query_weight, key_weight, value_weight,
     ]
     sums = scatter_all(
@@ -837,21 +926,21 @@
         + [spread(g, w) for g, w in zip(mats, shards)]
         + [vec_grads],
         [False, False] + [True] * (len(mats) + 1),
-        2,
-    )
-    encoded_grad = sums[0]
-    tokens_grad = tok_own + sums[1]
+        1,
+    )
+    done = hand_out(
+        [sums[0]] + list(sums[2:11]), sums[11], (part,) * WIDE + (long_part,), sums[1], tok_own
+    )
+    encoded_grad = done[0]
     (
-        merge_sum, probe_sum, lookup_sum, content_sum, out_sum, query_sum, key_sum, value_sum,
-    ) = [s.reshape(w.shape) for s, w in zip(sums[2:10], shards)]
-    expand_sum = expand_sum.reshape(expand_weight.shape)
+        expand_sum, merge_sum, probe_sum, lookup_sum, content_sum, out_sum, query_sum, key_sum, value_sum,
+    ) = [one.reshape(w.shape) for one, w in zip(done[1:10], shards)]
     reduce_sum = reduce_sum.reshape(reduce_weight.shape)
-    vec_sum = sums[10].reshape(padded)
     (
         query_vs, value_vs, out_vs, gain1_vs, shift1_vs, probe_vs, content_vs,
-        merge_vs, gain2_vs, shift2_vs, reduce_vs, gain3_vs, shift3_vs,
-    ) = [vec_sum[i * part : (i + 1) * part] for i in range(WIDE)]
-    expand_vs = vec_sum[WIDE * part : held]
+        merge_vs, gain2_vs, shift2_vs, reduce_vs, gain3_vs, shift3_vs, expand_vs,
+    ) = done[10:24]
+    tokens_grad = done[24]
     return (
         output[None],
         tokens_grad[None],

time: 597 us -> 520 us (0.87)
  Pallas kernels: 436 us -> 351 us
  matrix products: 105 us -> 119 us
  other arithmetic: 24.6 us -> 11 us
  between operations: 1.99 us -> 14.9 us
  local copies, waits for them, and re-layouts: 18.8 us -> 12.8 us
    pallas_call x3, Pallas kernels: 381 us -> 296 us  [the longest x1 146 us: gather_all(): pl.pallas_call(functools.partial(gather_kernel, cube, pieces, casts), out...]
    convert_element_type x10 -> x1, other arithmetic: 15.9 us -> 1.83 us  [local(): reduce_weight.astype(BF)]
    dot_general x10, matrix products: 26.2 us -> 35.8 us  [right_trans(): lax.dot_general(left_arg, right_arg, (((1,), (1,)), ((), ())), preferred_...]
    unnamed x125 -> x111, local copies, waits for them, and re-layouts: 12.5 us -> 5.46 us
  transfers between devices with their start and end apart: 0 -> 3, of which waited for: 0 -> 1; matrix products, arithmetic and copies ran while one was open for 0% -> 23% of each run, Pallas kernels for 0% -> 40%
where the time goes in v4:
time: 520 us; the launch traced here: 514 us
  Pallas kernels  351 us (68%)
  matrix products  119 us (23%)
  between operations  14.9 us (3%)
  local copies, waits for them, and re-layouts  12.8 us (2%)
  other arithmetic  11 us (2%)
    pallas_call x1, Pallas kernels, gather_all(): pl.pallas_call(functools.partial(gather_kernel, cube, pieces, casts), out...  146 us
    pallas_call x1, Pallas kernels, scatter_group(): pl.pallas_call(functools.partial(scatter_kernel, cube, pieces), out_shape...  144 us
    pallas_call x4, Pallas kernels, attend_call(): pl.pallas_call(functools.partial(attend_back_kernel if back else attend_k...  55.7 us
    dot_general x10, matrix products, matmul(): return jnp.dot(left_arg, right_arg, preferred_element_type=F32)  48.4 us
    dot_general x10, matrix products, right_trans(): lax.dot_general(left_arg, right_arg, (((1,), (1,)), ((), ())), preferred_...  35.8 us
    dot_general x10, matrix products, left_outer(): lax.dot_general(left_arg, right_arg, (((0,), (0,)), ((), ())), preferred_...  34.8 us
  transfers between devices with their start and end apart: 3, of which 1 were waited for; matrix products, arithmetic and copies ran while one was open for 23% of the time, Pallas kernels for 40%

profile of v4, /device:TPU:0, one launch (start us, length us, event | category | flops | bytes accessed | tf_op | source)
XLA Modules:
  0.0 514.4 jit_solution(6641153465428532022)
XLA Ops:
  7.3 1.8 convert_element_type.123
  9.1 1.5 concatenate.20
  10.6 146.2 %gather_weights.1 = (bf16[4,256,1024]{2,1,0:T(8,128)(2,1)}, bf16[4,128,1024]{2,1,0:T(8,128)(2,1)}, bf16[2,2,2,4,32,1024]{5,4,3,2,1,0:T(8,128)(2,1)}, bf16[2,2,2,...) custom-call(bf16[256,1024]{1,0:T(8,128)(2,1)} %bitcast.146, ...), custom_call_target="tpu_custom_call" | custom-call | tf_op jit(solution)/shard_map/gather_weights/pallas_call | solution.py:303
  157.1 0.9 copy.67
  160.0 2.3 fusion.25.refs_2_
  162.3 4.9 convolution_convert_fusion.10.refs_3_
  167.3 2.3 add_convert_fusion.1.refs_4_
  169.7 14.6 %attend.2 = (bf16[256,1024]{1,0:T(8,128)(2,1)S(1)}, f32[8,2,256]{2,1,0:T(2,128)S(1)}) custom-call(s32[1024,2]{1,0:T(8,128)S(1)} %bitcast.125, s32[2,256]{1,0:T(2,128)S(1)} %pad_add_fusion.1.refs_1_, bf16[256,1024]{1,0:T(8,128)(2,1)S(1)} %fusion.25.refs_2_, bf16[1024,1024]{1,0:T(8,128)(2,1)S(1)} %convolution_convert_fusion.10.refs_3_, ...), custom_call_target="tpu_custom_call" | custom-call | flops 1073741824 | bytes 5242880 | tf_op jit(solution)/shard_map/attend/pallas_call | solution.py:709
  184.3 0.8 fusion.45
  186.6 0.9 copy-done.49
  187.7 1.2 convolution_convert_fusion.11.refs_1_
  189.1 1.3 add_convert_fusion.3.refs_2_
  190.3 9.3 %attend.3 = (bf16[256,1024]{1,0:T(8,128)(2,1)S(1)}, f32[8,2,256]{2,1,0:T(2,128)S(1)}) custom-call(bf16[256,1024]{1,0:T(8,128)(2,1)S(1)} %fusion.23.refs_0_, bf16[512,1024]{1,0:T(8,128)(2,1)S(1)} %convolution_convert_fusion.11.refs_1_, bf16[512,1024]{1,0:T(8,128)(2,1)S(1)} %add_convert_fusion.3.refs_2_), custom_call_target="tpu_custom_call" | custom-call | flops 536870912 | bytes 3145728 | tf_op jit(solution)/shard_map/attend/pallas_call | solution.py:709
  199.6 0.8 fusion.46
  201.4 27.2 %fusion.2 = (bf16[256,4096]{1,0:T(8,128)(2,1)}, f32[256,4096]{1,0:T(8,128)}) fusion(f32[4096]{0:T(1024)S(1)} %slice_bitcast_fusion, bf16[1024,4096]{1,0:T(8,128)(2,1)S(1)} %bitcast.160, f32[256,1024]{1,0:T(8,128)S(1)} %get-tuple-element.183, f32[1024]{0:T(1024)S(1)} %add.201, f32[1024]{0:T(1024)S(1)} %mul.199, f32[256]{0:T(256)S(1)} %add_rsqrt_fusion.1, ...), kind=kOutput, calls=%fused_computation.8 | convolution fusion | flops 2218000384 | bytes 15755264 | tf_op jit(solution)/shard_map/dot_general | solution.py:26
  228.7 4.9 all-gather.2.cloned.1.call-done
  233.5 6.7 %fusion.47 = (f32[256]{0:T(256)S(1)}, f32[256,1024]{1,0:T(8,128)S(1)}) fusion(f32[1024]{0:T(1024)S(1)} %add.208, bf16[256,4096]{1,0:T(8,128)(2,1)} %get-tuple-element.184, bf16[4096,1024]{1,0:T(8,128)(2,1)} %all-gather.2.cloned.1.call-done, f32[1024]{0:T(1024)S(1)} %add.201, f32[1024]{0:T(1024)S(1)} %mul.199, f32[256]{0:T(256)S(1)} %add_rsqrt_fusion.1, ...), kind=kOutput, calls=%fused_computation.140 | convolution fusion | flops 2149842688 | bytes 12598272 | tf_op jit(solution)/shard_map/dot_general | solution.py:26
  241.1 1.3 fusion.41
  242.4 5.6 %convolution_convert_fusion = bf16[4096,1024]{1,0:T(8,128)(2,1)} fusion(bf16[256,4096]{1,0:T(8,128)(2,1)S(1)} %copy-done.28, f32[256,1024]{1,0:T(8,128)S(1)} %get-tuple-element.174), kind=kOutput, calls=%fused_computation | convolution fusion | flops 2151940096 | bytes 11534336 | tf_op jit(solution)/shard_map/dot_general | solution.py:30
  248.3 7.7 %fusion.48 = (f32[4096]{0:T(1024)S(1)}, bf16[256,4096]{1,0:T(8,128)(2,1)S(1)}) fusion(f32[256,4096]{1,0:T(8,128)} %get-tuple-element.185, bf16[4096,1024]{1,0:T(8,128)(2,1)} %all-gather.2.cloned.1.call-done, f32[256,1024]{1,0:T(8,128)} %copy-done.26), kind=kOutput, calls=%fused_computation.141 | convolution fusion | flops 2159276032 | bytes 15745024 | tf_op jit(solution)/shard_map/dot_general | solution.py:36
  256.1 8.4 %multiply_reduce_fusion = (f32[1024]{0:T(1024)S(1)}, f32[256]{0:T(256)S(1)}, f32[256]{0:T(256)S(1)}, f32[1024]{0:T(1024)S(1)}, f32[256,1024]{1,0:T(8,128)S(1)}) fusion(f32[256,1024]{1,0:T(8,128)S(1)} %copy-done.23, f32[256]{0:T(256)S(1)} %add_rsqrt_fusion.1, f32[256]{0:T(256)S(1)} %broadcast_multiply_fusion.7, f32[1024]{0:T(1024)S(1)} %mul.199, ...), kind=kOutput, calls=%fused_computation.72 | convolution fusion | flops 2150102528 | bytes 13647872 | tf_op jit(solution)/shard_map/dot_general | solution.py:36
  264.9 0.7 convolution_convert_fusion.13.refs_3_
  266.4 11.8 %attend_back.2 = (bf16[256,1024]{1,0:T(8,128)(2,1)S(1)}, bf16[512,1024]{1,0:T(8,128)(2,1)S(1)}, bf16[512,1024]{1,0:T(8,128)(2,1)S(1)}) custom-call(bf16[256,1024]{1,0:T(8,128)(2,1)S(1)} %fusion.23.refs_0_, bf16[512,1024]{1,0:T(8,128)(2,1)S(1)} %copy-done.5, bf16[512,1024]{1,0:T(8,128)(2,1)S(1)} %copy-done.7, ...), custom_call_target="tpu_custom_call" | custom-call | flops 1879048192 | bytes 11010048 | tf_op jit(solution)/shard_map/attend_back/pallas_call | solution.py:709
  278.2 1.1 multiply_reduce_fusion.1
  280.2 0.7 convolution_convert_fusion.12.refs_5_
  281.0 20.1 %attend_back.3 = (bf16[256,1024]{1,0:T(8,128)(2,1)S(1)}, bf16[1024,1024]{1,0:T(8,128)(2,1)S(1)}, bf16[1024,1024]{1,0:T(8,128)(2,1)}) custom-call(s32[1024,2]{1,0:T(8,128)S(1)} %bitcast.126, s32[2,256]{1,0:T(2,128)S(1)} %pad_add_fusion.1.refs_1_, bf16[256,1024]{1,0:T(8,128)(2,1)S(1)} %copy-done.3, bf16[1024,1024]{1,0:T(8,128)(2,1)} %copy-done.8, ...), custom_call_target="tpu_custom_call" | custom-call | flops 3758096384 | bytes 18350080 | tf_op jit(solution)/shard_map/attend_back/pallas_call | solution.py:709
  301.1 1.3 copy-done.12
  302.5 2.6 convert_reduce_fusion
  306.4 1.6 stack.55
  308.0 1.1 pad.4
  309.0 3.2 convolution_convert_fusion.8
  312.2 3.2 convolution_convert_fusion.4
  315.5 2.1 convolution_convert_fusion.5
  317.5 2.1 convolution_convert_fusion.9
  319.6 2.7 convolution_convert_fusion.6
  322.3 2.6 convolution_convert_fusion.7
  324.9 2.6 fusion.49
  327.6 5.7 %convolution_convert_fusion.1 = bf16[1024,4096]{1,0:T(8,128)(2,1)} fusion(bf16[256,4096]{1,0:T(8,128)(2,1)S(1)} %copy-done.30, f32[256,1024]{1,0:T(8,128)S(1)} %copy-done.24, f32[1024]{0:T(1024)S(1)} %add.201, f32[1024]{0:T(1024)S(1)} %mul.199, f32[256]{0:T(256)S(1)} %add_rsqrt_fusion.1, f32[256]{0:T(256)S(1)} %broadcast_multiply_fusion.7), kind=kOutput, calls=%fused_computation.1 | convolution fusion | flops 2152988672 | bytes 11544576 | tf_op jit(solution)/shard_map/dot_general | solution.py:30
  333.3 3.9 convolution_convert_fusion.2
  337.2 3.7 convolution_convert_fusion.3
  340.9 0.8 maximum_maximum_fusion.refs_11_
  341.7 5.0 add_convert_fusion.2
  346.8 2.4 fusion.50
  349.2 3.7 add_convert_fusion
  352.9 144.4 %scatter_grads.1 = (f32[128,1024]{1,0:T(8,128)}, f32[256,1024]{1,0:T(8,128)}, f32[32,4096]{1,0:T(8,128)}, f32[32,1024]{1,0:T(8,128)}, f32[32,1024]{1,0:T(8,128)}...) custom-call(bf16[4,128,1024]{2,1,0:T(8,128)(2,1)} %bitcast.147, ...), custom_call_target="tpu_custom_call" | custom-call | tf_op jit(solution)/shard_map/scatter_grads/pallas_call | solution.py:542
  497.3 3.4 convolution_add_fusion.2.refs_12_
  500.7 5.1 hand_out.1
  505.8 1.8 bitcast_convert_fusion
  (178 shorter events, 9.5 us)
Async XLA Ops:
  7.2 152.7 %copy-start.40 = (bf16[1,256,1024]{2,1,0:T(8,128)(2,1)S(1)}, bf16[1,256,1024]{2,1,0:T(8,128)(2,1)}, u32[]{:S(2)}) copy-start(bf16[1,256,1024]{2,1,0:T(8,128)(2,1)} %param.29) | copy-start | bytes 1572868
  7.2 151.7 %copy-start.42 = (s32[1,1024]{1,0:T(1,128)S(1)}, s32[1,1024]{1,0:T(1,128)}, u32[]{:S(2)}) copy-start(s32[1,1024]{1,0:T(1,128)} %param.32) | copy-start | bytes 12292
  7.2 151.6 %copy-start.41 = (s32[1,1024]{1,0:T(1,128)S(1)}, s32[1,1024]{1,0:T(1,128)}, u32[]{:S(2)}) copy-start(s32[1,1024]{1,0:T(1,128)} %param.33) | copy-start | bytes 12292
  7.2 226.3 %all-gather.2.cloned.1.call-start = ((), (), s32[]{:S(2)}) async-start(), calls=%async_computation.2 | async-start | bytes 8650752 | tf_op jit(solution)/shard_map/all_gather | solution.py:792
  156.8 184.1 %reduce-scatter.3.cloned.1.call-start = ((), (), s32[]{:S(2)}) async-start(), calls=%async_computation.3 | async-start | bytes 9437184 | tf_op jit(solution)/shard_map/reduce_scatter | solution.py:848
  159.1 10.5 %copy-start = (s32[2,1024]{0,1:T(8,128)}, s32[2,1024]{0,1:T(8,128)S(1)}, u32[]{:S(2)}) copy-start(s32[2,1024]{0,1:T(8,128)S(1)} %copy.62) | copy-start | bytes 24580
  162.3 7.4 %copy-start.2 = (bf16[256,1024]{1,0:T(8,128)(2,1)}, bf16[256,1024]{1,0:T(8,128)(2,1)S(1)}, u32[]{:S(2)}) copy-start(bf16[256,1024]{1,0:T(8,128)(2,1)S(1)} %fusion.25.refs_2_) | copy-start | bytes 1572868
  162.3 5.0 copy-start.43
  162.3 5.0 copy-start.47
  167.3 2.4 copy-start.8
  169.6 15.5 %copy-start.9 = (bf16[1024,1024]{1,0:T(8,128)(2,1)}, bf16[1024,1024]{1,0:T(8,128)(2,1)S(1)}, u32[]{:S(2)}) copy-start(bf16[1024,1024]{1,0:T(8,128)(2,1)S(1)} %add_convert_fusion.1.refs_4_) | copy-start | bytes 6291460
  169.6 14.7 %copy-start.31 = (bf16[2,2,2,4,32,1024]{5,4,3,2,1,0:T(8,128)(2,1)S(1)}, bf16[2,2,2,4,32,1024]{5,4,3,2,1,0:T(8,128)(2,1)}, u32[]{:S(2)}) copy-start(bf16[2,2,2,4,32,1024]{5,4,3,2,1,0:T(8,128)(2,1)} %get-tuple-element.95) | copy-start | bytes 6291460
  185.1 3.9 copy-start.20
  185.2 2.3 copy-start.49
  185.2 2.6 copy-start.51
  185.7 13.9 %copy-start.37 = (bf16[256,1024]{1,0:T(8,128)(2,1)}, bf16[256,1024]{1,0:T(8,128)(2,1)S(1)}, u32[]{:S(2)}) copy-start(bf16[256,1024]{1,0:T(8,128)(2,1)S(1)} %add_convert_fusion.6) | copy-start | bytes 1572868
  186.6 2.4 copy-start.46
  189.0 10.6 %copy-start.4 = (bf16[512,1024]{1,0:T(8,128)(2,1)}, bf16[512,1024]{1,0:T(8,128)(2,1)S(1)}, u32[]{:S(2)}) copy-start(bf16[512,1024]{1,0:T(8,128)(2,1)S(1)} %convolution_convert_fusion.11.refs_1_) | copy-start | bytes 3145732
  189.0 10.6 %copy-start.33 = (bf16[2,2,2,4,32,1024]{5,4,3,2,1,0:T(8,128)(2,1)S(1)}, bf16[2,2,2,4,32,1024]{5,4,3,2,1,0:T(8,128)(2,1)}, u32[]{:S(2)}) copy-start(bf16[2,2,2,4,32,1024]{5,4,3,2,1,0:T(8,128)(2,1)} %get-tuple-element.101) | copy-start | bytes 6291460
  189.0 12.4 %slice-start = ((s8[8388608]{0:T(1024)(128)(4,1)}), s8[4194304]{0:T(1024)(128)(4,1)S(1)}, s32[]{:S(2)}) async-start(s8[8388608]{0:T(1024)(128)(4,1)} %bitcast.158), calls=%async_computation.5 | async-start | bytes 8388608
  190.3 10.1 %copy-start.6 = (bf16[512,1024]{1,0:T(8,128)(2,1)}, bf16[512,1024]{1,0:T(8,128)(2,1)S(1)}, u32[]{:S(2)}) copy-start(bf16[512,1024]{1,0:T(8,128)(2,1)S(1)} %add_convert_fusion.3.refs_2_) | copy-start | bytes 3145732
  190.3 11.1 %slice-start.1 = ((s8[8388608]{0:T(1024)(128)(4,1)}), s8[4194304]{0:T(1024)(128)(4,1)S(1)}, s32[]{:S(2)}) async-start(s8[8388608]{0:T(1024)(128)(4,1)} %bitcast.158), calls=%async_computation.6 | async-start | bytes 8388608
  233.5 7.0 %copy-start.25 = (bf16[1,256,1024]{2,1,0:T(8,128)(2,1)S(1)}, bf16[1,256,1024]{2,1,0:T(8,128)(2,1)}, u32[]{:S(2)}) copy-start(bf16[1,256,1024]{2,1,0:T(8,128)(2,1)} %param.31) | copy-start | bytes 1572868
  240.3 2.1 copy-start.28
  242.4 5.6 %copy-start.26 = (f32[256,1024]{1,0:T(8,128)}, f32[256,1024]{1,0:T(8,128)S(1)}, u32[]{:S(2)}) copy-start(f32[256,1024]{1,0:T(8,128)S(1)} %get-tuple-element.174) | copy-start | bytes 3145732
  248.0 257.8 %reduce-scatter.5.cloned.1.call-start = ((), (), s32[]{:S(2)}) async-start(), calls=%async_computation.4 | async-start | bytes 1310720 | tf_op jit(solution)/shard_map/reduce_scatter | solution.py:849
  248.3 7.7 %copy-start.23 = (f32[256,1024]{1,0:T(8,128)S(1)}, f32[256,1024]{1,0:T(8,128)}, u32[]{:S(2)}) copy-start(f32[256,1024]{1,0:T(8,128)} %copy-done.22) | copy-start | bytes 3145732
  248.3 7.7 %copy-start.27 = (f32[256,1024]{1,0:T(8,128)S(1)}, f32[256,1024]{1,0:T(8,128)}, u32[]{:S(2)}) copy-start(f32[256,1024]{1,0:T(8,128)} %copy-done.26) | copy-start | bytes 3145732
  256.0 8.4 %copy-start.29 = (bf16[256,4096]{1,0:T(8,128)(2,1)}, bf16[256,4096]{1,0:T(8,128)(2,1)S(1)}, u32[]{:S(2)}) copy-start(bf16[256,4096]{1,0:T(8,128)(2,1)S(1)} %get-tuple-element.191) | copy-start | bytes 6291460
  256.1 8.8 %copy-start.34 = (bf16[2,2,2,4,32,1024]{5,4,3,2,1,0:T(8,128)(2,1)S(1)}, bf16[2,2,2,4,32,1024]{5,4,3,2,1,0:T(8,128)(2,1)}, u32[]{:S(2)}) copy-start(bf16[2,2,2,4,32,1024]{5,4,3,2,1,0:T(8,128)(2,1)} %get-tuple-element.101) | copy-start | bytes 6291460
  264.9 13.3 %copy-start.18 = (f32[256,1024]{1,0:T(8,128)}, f32[256,1024]{1,0:T(8,128)S(1)}, u32[]{:S(2)}) copy-start(f32[256,1024]{1,0:T(8,128)S(1)} %get-tuple-element.176) | copy-start | bytes 3145732
  265.7 12.5 %copy-start.21 = (f32[256,1024]{1,0:T(8,128)S(1)}, f32[256,1024]{1,0:T(8,128)}, u32[]{:S(2)}) copy-start(f32[256,1024]{1,0:T(8,128)} %copy-done.20) | copy-start | bytes 3145732
  265.7 12.5 %copy-start.39 = (bf16[2,2,2,4,32,1024]{5,4,3,2,1,0:T(8,128)(2,1)S(1)}, bf16[2,2,2,4,32,1024]{5,4,3,2,1,0:T(8,128)(2,1)}, u32[]{:S(2)}) copy-start(bf16[2,2,2,4,32,1024]{5,4,3,2,1,0:T(8,128)(2,1)} %get-tuple-element.96) | copy-start | bytes 6291460
  308.0 7.5 %copy-start.16 = (f32[256,1024]{1,0:T(8,128)S(1)}, f32[256,1024]{1,0:T(8,128)}, u32[]{:S(2)}) copy-start(f32[256,1024]{1,0:T(8,128)} %copy-done.15) | copy-start | bytes 3145732
  312.2 5.3 %copy-start.19 = (f32[256,1024]{1,0:T(8,128)S(1)}, f32[256,1024]{1,0:T(8,128)}, u32[]{:S(2)}) copy-start(f32[256,1024]{1,0:T(8,128)} %copy-done.18) | copy-start | bytes 3145732
  315.5 4.2 copy-start.52
  319.6 2.7 copy-start.11
  322.3 2.6 copy-start.50
  324.9 2.6 copy-start.24
  324.9 2.6 copy-start.30
  327.6 5.7 %copy-start.35 = (bf16[1024,1024]{1,0:T(8,128)(2,1)S(1)}, bf16[1024,1024]{1,0:T(8,128)(2,1)}, u32[]{:S(2)}) copy-start(bf16[1024,1024]{1,0:T(8,128)(2,1)} %get-tuple-element.110) | copy-start | bytes 6291460
  327.6 5.7 %copy-start.48 = (bf16[4,256,1024]{2,1,0:T(8,128)(2,1)S(1)}, bf16[4,256,1024]{2,1,0:T(8,128)(2,1)}, u32[]{:S(2)}) copy-start(bf16[4,256,1024]{2,1,0:T(8,128)(2,1)} %get-tuple-element.91) | copy-start | bytes 6291460
  333.3 3.9 copy-start.13
  340.9 5.8 %copy-start.14 = (bf16[1024,1024]{1,0:T(8,128)(2,1)S(1)}, bf16[1024,1024]{1,0:T(8,128)(2,1)}, u32[]{:S(2)}) copy-start(bf16[1024,1024]{1,0:T(8,128)(2,1)} %copy-done.12) | copy-start | bytes 6291460
  340.9 5.8 %copy-start.45 = (bf16[2,2,2,4,32,1024]{5,4,3,2,1,0:T(8,128)(2,1)S(1)}, bf16[2,2,2,4,32,1024]{5,4,3,2,1,0:T(8,128)(2,1)}, u32[]{:S(2)}) copy-start(bf16[2,2,2,4,32,1024]{5,4,3,2,1,0:T(8,128)(2,1)} %get-tuple-element.92) | copy-start | bytes 6291460
  346.8 2.4 copy-start.36
  346.8 2.4 copy-start.44
  352.9 144.4 %copy-start.17 = (f32[256,1024]{1,0:T(8,128)S(1)}, f32[256,1024]{1,0:T(8,128)}, u32[]{:S(2)}) copy-start(f32[256,1024]{1,0:T(8,128)} %copy-done.15) | copy-start | bytes 3145732
  (10 other events, 14.9 us)
Sparse Core Ops, SparseCore 0:
  156.9 76.5 all-gather.1
  248.1 69.9 reduce-scatter.2
  341.0 26.4 reduce-scatter.4

commit v5 on v4

--- a/solution.py
+++ b/solution.py
@@ -342,7 +342,7 @@
 
 
 def scatter_stages(
-    cube, here, full, variant, source, out, own, parts, send_sem, recv_sem, local_sem
+    cube, here, full, variant, source, out, own, parts, send_sem, recv_sem, local_sem, factors=None
 ):
     dp, seq = here.dp, here.seq
     n = cube.n_seq
@@ -360,8 +360,16 @@
     mine = {bit: here.bits[bit] for bit in range(1, cube.dp_bits)}
     settled = dims(mine, None) if full else ()
     lead = (slice(None),) * (cube.dp_bits - 1)
-    kept = source.at[lead + (here.bits[0],)] if full else source
-    local = pltpu.make_async_copy(kept, own, local_sem)
+    if factors is None:
+        kept = source.at[lead + (here.bits[0],)] if full else source
+        local = pltpu.make_async_copy(kept, own, local_sem)
+
+    def halves(core):
+        left, right = factors[:2]
+        for number, at in enumerate(itertools.product((0, 1), repeat=cube.dp_bits - 1)):
+            first = pl.multiple_of((2 * number + core) * (n * rows), 128)
+            block = left_outer(left[:, pl.ds(first, n * rows)], right.read())
+            yield at, block.reshape(n, rows, cols)
 
     def push(stage, what, device):
         copy = remote(what, parts[stage], send_sem.at[stage], recv_sem.at[stage], device)
@@ -405,14 +413,27 @@
             waits.append((passes, copy))
 
     def start():
+        if factors is not None:
+            _, _, ready, ring = factors
+            ready()
+            buffer = ring()
+            for at, block in halves(1 - here.bits[0]):
+                buffer[at] = block.astype(buffer.dtype)
+            push(0, buffer, (here.flips[0], seq))
+            ring(arrivals[0])
+            waits.pop()
+            return
         local.start()
         if full:
             push(0, source.at[lead + (1 - here.bits[0],)], (here.flips[0], seq))
 
     def after_dims(stage):
-        if stage == 0:
+        if stage == 0 and factors is None:
             local.wait()
         arrivals[stage].wait_recv()
+        if stage == 0 and factors is not None:
+            for at, block in halves(here.bits[0]):
+                own[at] = (block + own[at].astype(F32)).astype(own.dtype)
         closed = order[:stage]
         fixed = {bit: mine[bit] for bit in closed}
         open_bits = [bit for bit in reversed(range(1, cube.dp_bits)) if bit not in closed]
@@ -421,7 +442,8 @@
         for values in itertools.product((0, 1), repeat=len(open_bits)):
             to = dims({**fixed, **dict(zip(open_bits, values))}, None)
             pairs.append((own.at[to], parts[stage].at[values]))
-        add_rows(pairs, n, rows, cols)
+        if stage > 0 or factors is None:
+            add_rows(pairs, n, rows, cols)
         if stage < len(order):
             bit = order[stage]
             at = dims({**fixed, bit: 1 - mine[bit]}, slice(None)) + (pl.ds(0, n),)
@@ -481,43 +503,104 @@
     return stages, finish
 
 
-def scatter_kernel(cube, pieces, *refs):
+class Product:
+    def __init__(self, left, right, block):
+        self.left, self.right, self.dtype = left, right, jnp.dtype(BF)
+        self.shape = tuple(block)
+
+
+class Ring:
+    def __init__(self, buffers, depth):
+        self.buffers, self.depth, self.copies = buffers, depth, []
+
+    def __call__(self, copy=None):
+        if copy is not None:
+            self.copies.append(copy)
+            return None
+        turn = len(self.copies)
+        if turn >= self.depth:
+            self.copies[turn - self.depth].wait_send()
+        return self.buffers.at[turn % self.depth]
+
+    def finish(self):
+        for copy in self.copies[-self.depth :]:
+            copy.wait_send()
+
+
+RING = 6
+
+
+def scatter_kernel(cube, pieces, products, operands, *refs):
     count = 1 + max(piece[0] for piece in pieces)
-    ins, outs = refs[:count], refs[count : 2 * count]
-    refs = refs[2 * count :]
+    arrays = [index for index in range(count) if index not in products]
+    ins = dict(zip(arrays, refs))
+    refs = refs[len(arrays) :]
+    sources, refs = refs[:operands], refs[operands:]
+    outs, refs = refs[:count], refs[count:]
     send_sem, recv_sem, local_sem = refs[-3:]
+    refs = refs[:-3]
     here = Place(cube)
+    ring = None
+    if operands:
+        held, buffers, load_sem = refs[-2 - operands : -2], refs[-2], refs[-1]
+        loads = [
+            pltpu.make_async_copy(source, to, load_sem.at[turn])
+            for turn, (source, to) in enumerate(zip(sources, held))
+        ]
+        for copy in loads:
+            copy.start()
+        ring = Ring(buffers, RING)
+        waited = set()
+
+        def ready(places):
+            for place in places:
+                if place not in waited:
+                    loads[place].wait()
+                    waited.add(place)
+
     plans = []
     for index, (array, full, variant, col, cols) in enumerate(pieces):
-        held = 2 + (cube.dp_bits if full else 0)
         cut = (slice(None), pl.ds(col, cols))
+        if array in products:
+            places = products[array]
+            own, taken = refs[0], 1 + cube.dp_bits
+            parts, source = refs[:taken], None
+            left, right = held[places[0]], held[places[1]]
+            factors = (left, ColumnsOf(right, col, cols), functools.partial(ready, places), ring)
+        else:
+            taken = 2 + (cube.dp_bits if full else 0)
+            own, parts, factors = refs[0], refs[1:taken], None
+            source = ins[array].at[(slice(None),) * (cube.dp_bits * full + 1) + cut]
         plans.append(
             scatter_stages(
                 cube,
                 here,
                 full,
                 variant,
-                ins[array].at[(slice(None),) * (cube.dp_bits * full + 1) + cut],
+                source,
                 outs[array].at[cut],
-                refs[0],
-                refs[1:held],
+                own,
+                parts,
                 send_sem.at[index],
                 recv_sem.at[index],
                 local_sem.at[index],
+                factors,
             )
         )
-        refs = refs[held:]
+        refs = refs[taken:]
     meet(cube, here)
     in_slots([stages for stages, _ in plans], 4)
     for _, finish in plans:
         finish()
+    if ring is not None:
+        ring.finish()
 
 
 def scatter_shapes(cube, array, full, cols):
     block = (array.shape[-2], cols)
     shapes = []
     if full:
-        for stage in range(-1, cube.dp_bits):
+        for stage in range(0 if isinstance(array, Product) else -1, cube.dp_bits):
             lead = (2,) * (cube.dp_bits - 1 - max(stage, 0)) + (cube.n_seq,)
             shapes.append(lead + block)
     else:
@@ -533,6 +616,30 @@
     for array, full, _, _, cols in pieces:
         for shape in scatter_shapes(cube, arrays[array], full, cols):
             scratch.append(pltpu.VMEM(shape, arrays[array].dtype))
+    given, operands, products = [], [], {}
+    for index, array in enumerate(arrays):
+        if not isinstance(array, Product):
+            given.append(array)
+            continue
+        for factor in (array.left, array.right):
+            if not any(factor is one for one in operands):
+                operands.append(factor)
+        places = [
+            [factor is one for one in operands].index(True) for factor in (array.left, array.right)
+        ]
+        products[index] = tuple(places)
+    if operands:
+        scratch += [pltpu.VMEM(one.shape, one.dtype) for one in operands]
+        halves = {
+            scatter_shapes(cube, arrays[piece[0]], True, piece[4])[0]
+            for piece in pieces
+            if piece[0] in products
+        }
+        (half,) = halves
+        scratch += [
+            pltpu.VMEM((RING,) + half, BF),
+            pltpu.SemaphoreType.DMA((len(operands),)),
+        ]
     slots = 2 * cube.n_seq + cube.dp_bits
     scratch += [
         pltpu.SemaphoreType.DMA((len(pieces), slots)),
@@ -540,9 +647,9 @@
         pltpu.SemaphoreType.DMA((len(pieces),)),
     ]
     return pl.pallas_call(
-        functools.partial(scatter_kernel, cube, pieces),
+        functools.partial(scatter_kernel, cube, pieces, products, len(operands)),
         out_shape=outs,
-        in_specs=[pl.BlockSpec(memory_space=pl.ANY)] * len(arrays),
+        in_specs=[pl.BlockSpec(memory_space=pl.ANY)] * (len(given) + len(operands)),
         out_specs=[pl.BlockSpec(memory_space=pltpu.VMEM)] * len(arrays),
         scratch_shapes=scratch,
         compiler_params=pltpu.CompilerParams(
@@ -551,7 +658,7 @@
             vmem_limit_bytes=60 * 1024 * 1024,
         ),
         name="scatter_grads",
-    )(*arrays)
+    )(*given, *operands)
 
 
 def scatter_all(cube, arrays, kinds, collective_id):
@@ -571,6 +678,14 @@
             cube, [arrays[i] for i in group], [kinds[i] for i in group], collective_id + turn
         )
     return sums
+
+
+class ColumnsOf:
+    def __init__(self, ref, col, cols):
+        self.ref, self.at = ref, (slice(None), pl.ds(col, cols))
+
+    def read(self):
+        return self.ref[self.at]
 
 
 def hand_out_kernel(count, parts, *refs):
@@ -855,26 +970,29 @@
     grad_expanded = grad_act * slope
     g_expand_vec = jnp.sum(grad_expanded, axis=0)
     expand_rows = grad_expanded.astype(BF)
-    g_expand_mat = left_outer(stream_two, expand_rows)
-
-    def spread(grad, weight):
-        return grad.astype(BF).reshape(cube.lead(True) + block_shape(*weight.shape))
-
+
+    def gradient(left, right, weight):
+        block = block_shape(*weight.shape)
+        if block == weight.shape and cube.n_seq * block[0] % 128 == 0:
+            return Product(left, right, block)
+        return left_outer(left, right).astype(BF).reshape(cube.lead(True) + block)
+
+    g_expand_mat = gradient(stream_two, expand_rows, expand_weight)
     grad_two = grad_three + right_trans(expand_rows, expand_mat)
     g_shift_second = jnp.sum(grad_two, axis=0)
     g_gain_second = jnp.sum(grad_two * normed_two, axis=0)
     grad_second = layer_back(grad_two * gain_second, normed_two, inv_two)
     merge_rows = grad_second.astype(BF)
     g_merge_vec = jnp.sum(grad_second, axis=0)
-    g_merge_mat = left_outer(cross_outb, merge_rows)
+    g_merge_mat = gradient(cross_outb, merge_rows, merge_weight)
     grad_cross = right_trans(merge_rows, merge_mat).astype(BF)
     probe_rows, enc_key_rows, enc_value_rows = attend_call(
         True, None, [probe, enc_keys, enc_values, grad_cross, cross_logs]
     )
     g_probe_vec = jnp.sum(probe_rows.astype(F32), axis=0)
-    g_probe_mat = left_outer(stream_one, probe_rows)
-    g_lookup_mat = left_outer(enc_all, enc_key_rows)
-    g_content_mat = left_outer(enc_all, enc_value_rows)
+    g_probe_mat = gradient(stream_one, probe_rows, probe_weight)
+    g_lookup_mat = gradient(enc_all, enc_key_rows, lookup_weight)
+    g_content_mat = gradient(enc_all, enc_value_rows, content_weight)
     g_content_vec = jnp.sum(enc_value_rows.astype(F32), axis=0)
     enc_part = right_trans(enc_key_rows, lookup_mat) + right_trans(enc_value_rows, content_mat)
     grad_one = grad_second + right_trans(probe_rows, probe_mat)
@@ -883,16 +1001,16 @@
     grad_first = layer_back(grad_one * gain_first, normed_one, inv_one)
     out_rows = grad_first.astype(BF)
     g_out_vec = jnp.sum(grad_first, axis=0)
-    g_out_mat = left_outer(self_outb, out_rows)
+    g_out_mat = gradient(self_outb, out_rows, out_weight)
     grad_self = right_trans(out_rows, out_mat).astype(BF)
     query_rows, key_rows, value_rows = attend_call(
         True, ids, [queries, all_keys, all_values, grad_self, self_logs]
     )
     g_query_vec = jnp.sum(query_rows.astype(F32), axis=0)
     g_value_vec = jnp.sum(value_rows.astype(F32), axis=0)
-    g_query_mat = left_outer(flat, query_rows)
-    g_key_mat = left_outer(tok_all, key_rows)
-    g_value_mat = left_outer(tok_all, value_rows)
+    g_query_mat = gradient(flat, query_rows, query_weight)
+    g_key_mat = gradient(tok_all, key_rows, key_weight)
+    g_value_mat = gradient(tok_all, value_rows, value_weight)
     tok_part = right_trans(key_rows, key_mat) + right_trans(value_rows, value_mat)
     tok_own = grad_first + right_trans(query_rows, query_mat)
 
@@ -923,7 +1041,7 @@
             enc_part.astype(BF).reshape(cube.n_seq, enc_local, feat_width),
             tok_part.astype(BF).reshape(cube.n_seq, local_rows, feat_width),
         ]
-        + [spread(g, w) for g, w in zip(mats, shards)]
+        + mats
         + [vec_grads],
         [False, False] + [True] * (len(mats) + 1),
         1,

time: 520 us -> 498 us (0.958)
  matrix products: 119 us -> 87 us
  waiting for transfers between devices: 4.93 us -> 12.8 us
    dot_general x10 -> x1, matrix products: 34.8 us -> 5.62 us  [left_outer(): lax.dot_general(left_arg, right_arg, (((0,), (0,)), ((), ())), preferred_...]
    reduce_scatter x1, waiting for transfers between devices: 0.01 us -> 6.8 us  [local(): lax.psum_scatter(reduce_part, 'dp', scatter_dimension=0, tiled=True)]
  transfers between devices with their start and end apart: 3 -> 3, of which waited for: 1 -> 2; matrix products, arithmetic and copies ran while one was open for 23% -> 17% of each run, Pallas kernels for 40% -> 42%
where the time goes in v5:
time: 498 us; the launch traced here: 492 us
  Pallas kernels  354 us (71%)
  matrix products  87 us (17%)
  between operations  15.1 us (3%)
  waiting for transfers between devices  12.8 us (3%)
  local copies, waits for them, and re-layouts  12 us (2%)
  other arithmetic  10.9 us (2%)
    pallas_call x1, Pallas kernels, scatter_group(): pl.pallas_call(functools.partial(scatter_kernel, cube, pieces, products,...  147 us
    pallas_call x1, Pallas kernels, gather_all(): pl.pallas_call(functools.partial(gather_kernel, cube, pieces, casts), out...  146 us
    pallas_call x4, Pallas kernels, attend_call(): pl.pallas_call(functools.partial(attend_back_kernel if back else attend_k...  55.7 us
    dot_general x10, matrix products, matmul(): return jnp.dot(left_arg, right_arg, preferred_element_type=F32)  46 us
    dot_general x10, matrix products, right_trans(): lax.dot_general(left_arg, right_arg, (((1,), (1,)), ((), ())), preferred_...  35.3 us
  transfers between devices with their start and end apart: 3, of which 2 were waited for; matrix products, arithmetic and copies ran while one was open for 17% of the time, Pallas kernels for 42%

profile of v5, /device:TPU:0, one launch (start us, length us, event | category | flops | bytes accessed | tf_op | source)
XLA Modules:
  0.0 492.3 jit_solution(16844098060139643844)
XLA Ops:
  7.3 1.8 convert_element_type.93
  9.1 1.5 concatenate.20
  10.6 146.2 %gather_weights.1 = (bf16[4,256,1024]{2,1,0:T(8,128)(2,1)}, bf16[4,128,1024]{2,1,0:T(8,128)(2,1)}, bf16[2,2,2,4,32,1024]{5,4,3,2,1,0:T(8,128)(2,1)}, bf16[2,2,2,...) custom-call(bf16[256,1024]{1,0:T(8,128)(2,1)} %bitcast.110, ...), custom_call_target="tpu_custom_call" | custom-call | tf_op jit(solution)/shard_map/gather_weights/pallas_call | solution.py:303
  157.1 1.1 copy.67
  158.4 0.6 slice_reduce_fusion.1
  160.2 2.3 fusion.25.refs_2_
  162.6 4.2 convolution_convert_fusion.1.refs_3_
  166.9 2.3 add_convert_fusion.1.refs_4_
  169.3 14.7 %attend.2 = (bf16[256,1024]{1,0:T(8,128)(2,1)S(1)}, f32[8,2,256]{2,1,0:T(2,128)S(1)}) custom-call(s32[1024,2]{1,0:T(8,128)S(1)} %bitcast.101, s32[2,256]{1,0:T(2,128)S(1)} %pad_add_fusion.1.refs_1_, bf16[256,1024]{1,0:T(8,128)(2,1)S(1)} %fusion.25.refs_2_, bf16[1024,1024]{1,0:T(8,128)(2,1)S(1)} %convolution_convert_fusion.1.refs_3_, ...), custom_call_target="tpu_custom_call" | custom-call | flops 1073741824 | bytes 5242880 | tf_op jit(solution)/shard_map/attend/pallas_call | solution.py:824
  184.0 0.8 fusion.39
  185.5 0.4 copy-done.34
  185.8 0.7 fusion.23.refs_0_
  186.8 0.7 copy-done.43
  187.5 1.2 convolution_convert_fusion.2.refs_1_
  188.8 1.3 add_convert_fusion.3.refs_2_
  190.1 9.3 %attend.3 = (bf16[256,1024]{1,0:T(8,128)(2,1)S(1)}, f32[8,2,256]{2,1,0:T(2,128)S(1)}) custom-call(bf16[256,1024]{1,0:T(8,128)(2,1)S(1)} %fusion.23.refs_0_, bf16[512,1024]{1,0:T(8,128)(2,1)S(1)} %convolution_convert_fusion.2.refs_1_, bf16[512,1024]{1,0:T(8,128)(2,1)S(1)} %add_convert_fusion.3.refs_2_), custom_call_target="tpu_custom_call" | custom-call | flops 536870912 | bytes 3145728 | tf_op jit(solution)/shard_map/attend/pallas_call | solution.py:824
  199.4 0.8 copy-done.8
  200.2 2.4 fusion.40
  203.2 24.2 %fusion.2 = (bf16[256,4096]{1,0:T(8,128)(2,1)}, f32[256,4096]{1,0:T(8,128)}) fusion(f32[4096]{0:T(1024)S(1)} %slice_bitcast_fusion, bf16[256,1024]{1,0:T(8,128)(2,1)S(1)} %add_convert_fusion.5.refs_3_, bf16[1024,4096]{1,0:T(8,128)(2,1)S(1)} %bitcast.130), kind=kOutput, calls=%fused_computation.7 | convolution fusion | flops 2216689664 | bytes 15220736 | tf_op jit(solution)/shard_map/dot_general | solution.py:26
  227.4 5.9 %all-gather.2.cloned.1.call-done = bf16[4096,1024]{1,0:T(8,128)(2,1)} async-done(((bf16[128,1024]{1,0:T(8,128)(2,1)}), bf16[4096,1024]{1,0:T(8,128)(2,1)}) %all-gather.2.cloned.1.call-update) | async-done | bytes 8388624 | tf_op jit(solution)/shard_map/all_gather | solution.py:907
  233.3 6.5 %fusion.41 = (f32[256]{0:T(256)S(1)}, f32[256,1024]{1,0:T(8,128)S(1)}) fusion(f32[1024]{0:T(1024)S(1)} %add.208, bf16[256,4096]{1,0:T(8,128)(2,1)} %get-tuple-element.186, bf16[4096,1024]{1,0:T(8,128)(2,1)} %all-gather.2.cloned.1.call-done, bf16[256,1024]{1,0:T(8,128)(2,1)S(1)} %add_convert_fusion.5.refs_3_), kind=kOutput, calls=%fused_computation.125 | convolution fusion | flops 2148531968 | bytes 12063744 | tf_op jit(solution)/shard_map/dot_general | solution.py:26
  240.1 0.5 fusion.29
  240.7 1.3 fusion.34
  241.9 5.6 %convolution_convert_fusion = bf16[4096,1024]{1,0:T(8,128)(2,1)} fusion(bf16[256,4096]{1,0:T(8,128)(2,1)S(1)} %copy-done.25, f32[256,1024]{1,0:T(8,128)S(1)} %get-tuple-element.174), kind=kOutput, calls=%fused_computation | convolution fusion | flops 2151940096 | bytes 11534336 | tf_op jit(solution)/shard_map/dot_general | solution.py:30
  247.9 7.2 %fusion.38 = (f32[4096]{0:T(1024)S(1)}, bf16[256,4096]{1,0:T(8,128)(2,1)S(1)}) fusion(f32[256,4096]{1,0:T(8,128)} %get-tuple-element.187, bf16[4096,1024]{1,0:T(8,128)(2,1)} %all-gather.2.cloned.1.call-done, f32[256,1024]{1,0:T(8,128)S(1)} %get-tuple-element.174), kind=kOutput, calls=%fused_computation.122 | convolution fusion | flops 2159276032 | bytes 15745024 | tf_op jit(solution)/shard_map/dot_general | solution.py:36
  255.1 8.4 %multiply_reduce_fusion = (f32[1024]{0:T(1024)S(1)}, f32[256]{0:T(256)S(1)}, f32[256]{0:T(256)S(1)}, f32[1024]{0:T(1024)S(1)}, f32[256,1024]{1,0:T(8,128)S(1)}) fusion(f32[256,1024]{1,0:T(8,128)S(1)} %get-tuple-element.185, f32[256]{0:T(256)S(1)} %add_rsqrt_fusion.1, f32[256]{0:T(256)S(1)} %broadcast_multiply_fusion.7, f32[1024]{0:T(1024)S(1)} %mul.199, ...), kind=kOutput, calls=%fused_computation.63 | convolution fusion | flops 2150102528 | bytes 13647872 | tf_op jit(solution)/shard_map/dot_general | solution.py:36
  263.6 0.4 fusion.36
  264.0 0.8 copy-done.28
  264.8 0.5 copy-done.46
  265.3 0.7 convolution_convert_fusion.4.refs_3_
  266.1 11.8 %attend_back.2 = (bf16[256,1024]{1,0:T(8,128)(2,1)S(1)}, bf16[512,1024]{1,0:T(8,128)(2,1)S(1)}, bf16[512,1024]{1,0:T(8,128)(2,1)S(1)}) custom-call(bf16[256,1024]{1,0:T(8,128)(2,1)S(1)} %fusion.23.refs_0_, bf16[512,1024]{1,0:T(8,128)(2,1)S(1)} %copy-done.14, bf16[512,1024]{1,0:T(8,128)(2,1)S(1)} %copy-done.16, ...), custom_call_target="tpu_custom_call" | custom-call | flops 1879048192 | bytes 11010048 | tf_op jit(solution)/shard_map/attend_back/pallas_call | solution.py:824
  277.9 1.1 multiply_reduce_fusion.1
  279.1 0.4 fusion.37
  279.5 1.0 copy-done.21
  280.6 0.8 convolution_convert_fusion.3.refs_5_
  281.4 20.0 %attend_back.3 = (bf16[256,1024]{1,0:T(8,128)(2,1)S(1)}, bf16[1024,1024]{1,0:T(8,128)(2,1)S(1)}, bf16[1024,1024]{1,0:T(8,128)(2,1)}) custom-call(s32[1024,2]{1,0:T(8,128)S(1)} %bitcast.102, s32[2,256]{1,0:T(2,128)S(1)} %pad_add_fusion.1.refs_1_, bf16[256,1024]{1,0:T(8,128)(2,1)S(1)} %copy-done.12, bf16[1024,1024]{1,0:T(8,128)(2,1)} %copy-done.17, ...), custom_call_target="tpu_custom_call" | custom-call | flops 3758096384 | bytes 18350080 | tf_op jit(solution)/shard_map/attend_back/pallas_call | solution.py:824
  301.4 1.3 copy-done.4
  302.9 2.1 convert_reduce_fusion
  306.6 4.3 fusion.42
  310.9 6.8 %reduce-scatter.3.cloned.1.call-done = bf16[1,4,128,1024]{3,2,1,0:T(8,128)(2,1)} async-done(((bf16[8,4,128,1024]{3,2,1,0:T(8,128)(2,1)}), bf16[1,4,128,1024]{3,2,1,0:T(8,128)(2,1)}) %reduce-scatter.3.cloned.1.call-update) | async-done | bytes 1048592 | tf_op jit(solution)/shard_map/reduce_scatter | solution.py:963
  317.7 0.8 maximum_maximum_fusion.refs_2_
  318.5 5.0 %add_convert_fusion.2 = bf16[512,1024]{1,0:T(8,128)(2,1)} fusion(f32[512,1024]{1,0:T(8,128)} %fusion.42, bf16[512,1024]{1,0:T(8,128)(2,1)S(1)} %get-tuple-element.106.refs_11_, bf16[1024,1024]{1,0:T(8,128)(2,1)} %bitcast.135), kind=kOutput, calls=%fused_computation.30 | convolution fusion | flops 1074790400 | bytes 6291456 | tf_op jit(solution)/shard_map/dot_general | solution.py:36
  323.6 2.4 fusion.43
  326.0 3.7 add_convert_fusion
  329.7 147.2 %scatter_grads.1 = (f32[128,1024]{1,0:T(8,128)}, f32[256,1024]{1,0:T(8,128)}, f32[32,4096]{1,0:T(8,128)}, f32[32,1024]{1,0:T(8,128)}, f32[32,1024]{1,0:T(8,128)}...) custom-call(bf16[4,128,1024]{2,1,0:T(8,128)(2,1)} %bitcast.117, ...), custom_call_target="tpu_custom_call" | custom-call | tf_op jit(solution)/shard_map/scatter_grads/pallas_call | solution.py:649
  476.9 1.7 convolution_add_fusion.2.refs_12_
  478.6 5.1 %hand_out.1 = (f32[128,1024]{1,0:T(8,128)}, f32[32,4096]{1,0:T(8,128)}, f32[32,1024]{1,0:T(8,128)}, f32[32,1024]{1,0:T(8,128)}, f32[32,1024]{1,0:T(8,128)}, /*in...) custom-call(f32[128,1024]{1,0:T(8,128)} %get-tuple-element.112.refs_, ...), custom_call_target="tpu_custom_call" | custom-call | tf_op jit(solution)/shard_map/hand_out/pallas_call | solution.py:720
  483.7 1.8 bitcast_convert_fusion
  (160 shorter events, 5.8 us)
Async XLA Ops:
  7.2 153.0 %copy-start.33 = (bf16[1,256,1024]{2,1,0:T(8,128)(2,1)S(1)}, bf16[1,256,1024]{2,1,0:T(8,128)(2,1)}, u32[]{:S(2)}) copy-start(bf16[1,256,1024]{2,1,0:T(8,128)(2,1)} %param.29) | copy-start | bytes 1572868
  7.2 152.0 %copy-start.37 = (s32[1,1024]{1,0:T(1,128)S(1)}, s32[1,1024]{1,0:T(1,128)}, u32[]{:S(2)}) copy-start(s32[1,1024]{1,0:T(1,128)} %param.33) | copy-start | bytes 12292
  7.2 152.0 %copy-start.38 = (s32[1,1024]{1,0:T(1,128)S(1)}, s32[1,1024]{1,0:T(1,128)}, u32[]{:S(2)}) copy-start(s32[1,1024]{1,0:T(1,128)} %param.32) | copy-start | bytes 12292
  7.2 226.1 %all-gather.2.cloned.1.call-start = ((), (), s32[]{:S(2)}) async-start(), calls=%async_computation.2 | async-start | bytes 8650752 | tf_op jit(solution)/shard_map/all_gather | solution.py:907
  156.8 5.8 %copy-start.26 = (bf16[4,256,1024]{2,1,0:T(8,128)(2,1)S(1)}, bf16[4,256,1024]{2,1,0:T(8,128)(2,1)}, u32[]{:S(2)}) copy-start(bf16[4,256,1024]{2,1,0:T(8,128)(2,1)} %get-tuple-element.91) | copy-start | bytes 6291460
  156.8 160.9 %reduce-scatter.3.cloned.1.call-start = ((), (), s32[]{:S(2)}) async-start(), calls=%async_computation.3 | async-start | bytes 9437184 | tf_op jit(solution)/shard_map/reduce_scatter | solution.py:963
  159.5 9.8 %copy-start.9 = (s32[2,1024]{0,1:T(8,128)}, s32[2,1024]{0,1:T(8,128)S(1)}, u32[]{:S(2)}) copy-start(s32[2,1024]{0,1:T(8,128)S(1)} %copy.62) | copy-start | bytes 24580
  162.6 6.7 %copy-start.11 = (bf16[256,1024]{1,0:T(8,128)(2,1)}, bf16[256,1024]{1,0:T(8,128)(2,1)S(1)}, u32[]{:S(2)}) copy-start(bf16[256,1024]{1,0:T(8,128)(2,1)S(1)} %fusion.25.refs_2_) | copy-start | bytes 1572868
  162.6 4.3 copy-start.39
  166.8 2.4 copy-start.17
  169.2 15.7 %copy-start.18 = (bf16[1024,1024]{1,0:T(8,128)(2,1)}, bf16[1024,1024]{1,0:T(8,128)(2,1)S(1)}, u32[]{:S(2)}) copy-start(bf16[1024,1024]{1,0:T(8,128)(2,1)S(1)} %add_convert_fusion.1.refs_4_) | copy-start | bytes 6291460
  169.2 14.8 %copy-start.44 = (bf16[2,2,2,4,32,1024]{5,4,3,2,1,0:T(8,128)(2,1)S(1)}, bf16[2,2,2,4,32,1024]{5,4,3,2,1,0:T(8,128)(2,1)}, u32[]{:S(2)}) copy-start(bf16[2,2,2,4,32,1024]{5,4,3,2,1,0:T(8,128)(2,1)} %get-tuple-element.95) | copy-start | bytes 6291460
  184.0 2.5 copy-start.7
  184.0 1.8 copy-start.34
  184.9 3.9 copy-start.19
  184.9 1.9 copy-start.36
  184.9 2.6 copy-start.43
  185.4 13.9 %copy-start.30 = (bf16[256,1024]{1,0:T(8,128)(2,1)}, bf16[256,1024]{1,0:T(8,128)(2,1)S(1)}, u32[]{:S(2)}) copy-start(bf16[256,1024]{1,0:T(8,128)(2,1)S(1)} %add_convert_fusion.6.refs_7_) | copy-start | bytes 1572868
  186.5 2.3 copy-start.42
  188.8 10.6 %copy-start.13 = (bf16[512,1024]{1,0:T(8,128)(2,1)}, bf16[512,1024]{1,0:T(8,128)(2,1)S(1)}, u32[]{:S(2)}) copy-start(bf16[512,1024]{1,0:T(8,128)(2,1)S(1)} %convolution_convert_fusion.2.refs_1_) | copy-start | bytes 3145732
  188.8 14.4 %slice-start = ((s8[8388608]{0:T(1024)(128)(4,1)}), s8[4194304]{0:T(1024)(128)(4,1)S(1)}, s32[]{:S(2)}) async-start(s8[8388608]{0:T(1024)(128)(4,1)} %bitcast.128), calls=%async_computation.5 | async-start | bytes 8388608
  190.1 12.5 %copy-start.15 = (bf16[512,1024]{1,0:T(8,128)(2,1)}, bf16[512,1024]{1,0:T(8,128)(2,1)S(1)}, u32[]{:S(2)}) copy-start(bf16[512,1024]{1,0:T(8,128)(2,1)S(1)} %add_convert_fusion.3.refs_2_) | copy-start | bytes 3145732
  190.1 13.1 %slice-start.1 = ((s8[8388608]{0:T(1024)(128)(4,1)}), s8[4194304]{0:T(1024)(128)(4,1)S(1)}, s32[]{:S(2)}) async-start(s8[8388608]{0:T(1024)(128)(4,1)} %bitcast.128), calls=%async_computation.6 | async-start | bytes 8388608
  203.2 30.1 %copy-start.31 = (bf16[256,1024]{1,0:T(8,128)(2,1)}, bf16[256,1024]{1,0:T(8,128)(2,1)S(1)}, u32[]{:S(2)}) copy-start(bf16[256,1024]{1,0:T(8,128)(2,1)S(1)} %add_convert_fusion.5.refs_3_) | copy-start | bytes 1572868
  233.3 6.8 %copy-start.24 = (bf16[1,256,1024]{2,1,0:T(8,128)(2,1)S(1)}, bf16[1,256,1024]{2,1,0:T(8,128)(2,1)}, u32[]{:S(2)}) copy-start(bf16[1,256,1024]{2,1,0:T(8,128)(2,1)} %param.31) | copy-start | bytes 1572868
  239.8 2.1 copy-start.25
  247.6 236.2 %reduce-scatter.5.cloned.1.call-start = ((), (), s32[]{:S(2)}) async-start(), calls=%async_computation.4 | async-start | bytes 1310720 | tf_op jit(solution)/shard_map/reduce_scatter | solution.py:964
  255.1 8.4 %copy-start.27 = (bf16[256,4096]{1,0:T(8,128)(2,1)}, bf16[256,4096]{1,0:T(8,128)(2,1)S(1)}, u32[]{:S(2)}) copy-start(bf16[256,4096]{1,0:T(8,128)(2,1)S(1)} %get-tuple-element.180.refs_4_) | copy-start | bytes 6291460
  263.5 1.8 copy-start.46
  263.5 2.6 copy-start.14
  263.5 2.6 copy-start.16
  266.1 11.8 %copy-start.20 = (f32[256,1024]{1,0:T(8,128)S(1)}, f32[256,1024]{1,0:T(8,128)}, u32[]{:S(2)}) copy-start(f32[256,1024]{1,0:T(8,128)} %copy-done.19) | copy-start | bytes 3145732
  266.1 11.8 %copy-start.35 = (bf16[2,2,2,4,32,1024]{5,4,3,2,1,0:T(8,128)(2,1)S(1)}, bf16[2,2,2,4,32,1024]{5,4,3,2,1,0:T(8,128)(2,1)}, u32[]{:S(2)}) copy-start(bf16[2,2,2,4,32,1024]{5,4,3,2,1,0:T(8,128)(2,1)} %get-tuple-element.96) | copy-start | bytes 6291460
  277.9 27.5 %copy-start.2 = (bf16[256,1024]{1,0:T(8,128)(2,1)}, bf16[256,1024]{1,0:T(8,128)(2,1)S(1)}, u32[]{:S(2)}) copy-start(bf16[256,1024]{1,0:T(8,128)(2,1)S(1)} %get-tuple-element.107.refs_8_) | copy-start | bytes 1572868
  277.9 28.7 %copy-start.6 = (bf16[512,1024]{1,0:T(8,128)(2,1)}, bf16[512,1024]{1,0:T(8,128)(2,1)S(1)}, u32[]{:S(2)}) copy-start(bf16[512,1024]{1,0:T(8,128)(2,1)S(1)} %get-tuple-element.105.refs_10_) | copy-start | bytes 3145732
  277.9 40.6 %copy-start.3 = (bf16[512,1024]{1,0:T(8,128)(2,1)}, bf16[512,1024]{1,0:T(8,128)(2,1)S(1)}, u32[]{:S(2)}) copy-start(bf16[512,1024]{1,0:T(8,128)(2,1)S(1)} %get-tuple-element.106.refs_11_) | copy-start | bytes 3145732
  277.9 2.6 copy-start.45
  279.1 2.3 copy-start.10
  279.1 2.3 copy-start.12
  301.4 1.3 copy-start.4
  302.7 8.2 %copy-start = (bf16[256,1024]{1,0:T(8,128)(2,1)}, bf16[256,1024]{1,0:T(8,128)(2,1)S(1)}, u32[]{:S(2)}) copy-start(bf16[256,1024]{1,0:T(8,128)(2,1)S(1)} %get-tuple-element.111.refs_15_) | copy-start | bytes 1572868
  317.7 5.8 %copy-start.5 = (bf16[1024,1024]{1,0:T(8,128)(2,1)S(1)}, bf16[1024,1024]{1,0:T(8,128)(2,1)}, u32[]{:S(2)}) copy-start(bf16[1024,1024]{1,0:T(8,128)(2,1)} %copy-done.4) | copy-start | bytes 6291460
  317.7 5.8 %copy-start.41 = (bf16[2,2,2,4,32,1024]{5,4,3,2,1,0:T(8,128)(2,1)S(1)}, bf16[2,2,2,4,32,1024]{5,4,3,2,1,0:T(8,128)(2,1)}, u32[]{:S(2)}) copy-start(bf16[2,2,2,4,32,1024]{5,4,3,2,1,0:T(8,128)(2,1)} %get-tuple-element.92) | copy-start | bytes 6291460
  323.6 2.4 copy-start.23
  323.6 2.4 copy-start.40
  329.7 147.2 %copy-start.1 = (bf16[256,1024]{1,0:T(8,128)(2,1)S(1)}, bf16[256,1024]{1,0:T(8,128)(2,1)}, u32[]{:S(2)}) copy-start(bf16[256,1024]{1,0:T(8,128)(2,1)} %copy-done) | copy-start | bytes 1572868
  329.7 147.2 %copy-start.22 = (f32[256,1024]{1,0:T(8,128)S(1)}, f32[256,1024]{1,0:T(8,128)}, u32[]{:S(2)}) copy-start(f32[256,1024]{1,0:T(8,128)} %copy-done.21) | copy-start | bytes 3145732
  329.7 147.2 %copy-start.32 = (bf16[2,2,2,4,32,1024]{5,4,3,2,1,0:T(8,128)(2,1)S(1)}, bf16[2,2,2,4,32,1024]{5,4,3,2,1,0:T(8,128)(2,1)}, u32[]{:S(2)}) copy-start(bf16[2,2,2,4,32,1024]{5,4,3,2,1,0:T(8,128)(2,1)} %get-tuple-element.88) | copy-start | bytes 6291460
  (4 other events, 3.4 us)
Sparse Core Ops, SparseCore 0:
  156.9 76.3 all-gather.1
  247.7 69.9 reduce-scatter.2
  320.1 29.2 reduce-scatter.4

commit v6 on v5

--- a/solution.py
+++ b/solution.py
@@ -272,7 +272,7 @@
         finish()
 
 
-def cut_columns(kinds, arrays):
+def cut_columns(kinds, arrays, first, last):
     whole, along = [], []
     for index, (full, array) in enumerate(zip(kinds, arrays)):
         cols = array.shape[-1]
@@ -286,12 +286,13 @@
             else:
                 along.append((index, False, 0, width * i, width))
     placed = [((i + 0.5) / len(whole), 0, piece) for i, piece in enumerate(whole)]
-    placed += [((i + 0.5) / len(along), 1, piece) for i, piece in enumerate(along)]
+    reach = (last - first) / max(len(along), 1)
+    placed += [(first + (i + 0.5) * reach, 1, piece) for i, piece in enumerate(along)]
     return tuple(piece for _, _, piece in sorted(placed, key=lambda item: item[:2]))
 
 
 def gather_all(cube, arrays, kinds, casts, collective_id):
-    pieces = cut_columns(kinds, arrays)
+    pieces = cut_columns(kinds, arrays, 0.3, 1.0)
     outs = [
         jax.ShapeDtypeStruct(
             cube.lead(full) + array.shape, BF if index in casts else array.dtype
@@ -610,7 +611,7 @@
 
 
 def scatter_group(cube, arrays, kinds, collective_id):
-    pieces = cut_columns(kinds, arrays)
+    pieces = cut_columns(kinds, arrays, 0.0, 0.6)
     outs = [jax.ShapeDtypeStruct(array.shape[-2:], F32) for array in arrays]
     scratch = []
     for array, full, _, _, cols in pieces:
@@ -768,26 +769,34 @@
 
 def attend_back_kernel(masked, *refs):
     if masked:
-        key_ids, query_ids, query_ref, key_ref, value_ref, grad_ref, log_ref = refs[:7]
-        dq_ref, dk_ref, dv_ref, bias = refs[7:]
+        key_ids, query_ids, query_ref, key_ref, value_ref, grad_ref, got_ref, log_ref = refs[:8]
+        dq_ref, dk_ref, dv_ref, probs, slopes, bias = refs[8:]
         pl.when(pl.program_id(0) == 0)(lambda: write_bias(bias, key_ids[...], query_ids[...]))
     else:
-        query_ref, key_ref, value_ref, grad_ref, log_ref, dq_ref, dk_ref, dv_ref = refs
-    query, key, value, grad = query_ref[...], key_ref[...], value_ref[...], grad_ref[...]
-    key_t = key.T
+        query_ref, key_ref, value_ref, grad_ref, got_ref, log_ref = refs[:6]
+        dq_ref, dk_ref, dv_ref, probs, slopes = refs[6:]
+    query, grad = query_ref[...], grad_ref[...]
+    keys = key_ref.shape[0]
+    key_t = key_ref[...].T
+    both = (grad.astype(F32) * got_ref[...].astype(F32)).T
+    span = math.gcd(keys, 128)
     dq, dk, dv = [], None, None
     for head in range(2):
         query_head, grad_head = one_head(query, head), one_head(grad, head)
-        scores = right_trans(key, query_head)
-        if masked:
-            scores = scores + bias[...]
-        probs = jnp.exp(scores - log_ref[0, head : head + 1, :])
-        grad_probs = right_trans(value, grad_head)
-        delta = jnp.sum(probs * grad_probs, axis=0, keepdims=True)
-        grad_scores = (probs * (grad_probs - delta)).astype(BF)
-        dq.append(matmul(key_t[head * DH : (head + 1) * DH], grad_scores))
-        dk_head = matmul(grad_scores, query_head)
-        dv_head = matmul(probs.astype(BF), grad_head)
+        delta = jnp.sum(both[head * DH : (head + 1) * DH], axis=0, keepdims=True)
+        log = log_ref[0, head : head + 1, :]
+        for first in range(0, keys, span):
+            at = pl.ds(first, span)
+            scores = right_trans(key_ref[at, :], query_head)
+            if masked:
+                scores = scores + bias[at, :]
+            prob = jnp.exp(scores - log)
+            grad_probs = right_trans(value_ref[at, :], grad_head)
+            probs[at, :] = prob.astype(BF)
+            slopes[at, :] = (prob * (grad_probs - delta)).astype(BF)
+        dq.append(matmul(key_t[head * DH : (head + 1) * DH], slopes[...]))
+        dk_head = matmul(slopes[...], query_head)
+        dv_head = matmul(probs[...], grad_head)
         dk = dk_head if dk is None else dk + dk_head
         dv = dv_head if dv is None else dv + dv_head
     scale = DH ** (-0.5)
@@ -816,7 +825,7 @@
     query_shape = jax.ShapeDtypeStruct((rows, width), BF)
     key_shape = jax.ShapeDtypeStruct((keys, width), BF)
     if back:
-        in_specs += [by_query, logs]
+        in_specs += [by_query, by_query, logs]
         out_specs, out_shape = [by_query, by_key, by_key], [query_shape, key_shape, key_shape]
     else:
         out_specs, out_shape = [by_query, logs], [query_shape, log_shape]
@@ -827,7 +836,8 @@
         in_specs=in_specs,
         out_specs=out_specs,
         out_shape=out_shape,
-        scratch_shapes=[pltpu.VMEM((keys, rows), F32)] if masked else [],
+        scratch_shapes=[pltpu.VMEM((keys, rows), BF)] * (2 * back)
+        + [pltpu.VMEM((keys, rows), F32)] * masked,
         cost_estimate=pl.CostEstimate(
             flops=2 * products * rows * keys * width,
             bytes_accessed=2 * width * (rows + keys) * products,
@@ -961,8 +971,6 @@
     g_reduce_mat = left_outer(activated, reduce_rows).astype(BF)
     reduce_part = g_reduce_mat.reshape((cube.n_dp, cube.n_seq) + reduce_weight.shape)
     reduce_part = lax.psum_scatter(reduce_part, "dp", scatter_dimension=0, tiled=True)
-    reduce_part = lax.psum_scatter(reduce_part, "seq", scatter_dimension=1, tiled=True)
-    reduce_sum = reduce_part.astype(F32)
     grad_act = right_trans(reduce_rows, reduce_mat)
     slope = 0.5 * (
         1.0 + jax.scipy.special.erf(expanded * INV_ROOT_TWO)
@@ -987,7 +995,7 @@
     g_merge_mat = gradient(cross_outb, merge_rows, merge_weight)
     grad_cross = right_trans(merge_rows, merge_mat).astype(BF)
     probe_rows, enc_key_rows, enc_value_rows = attend_call(
-        True, None, [probe, enc_keys, enc_values, grad_cross, cross_logs]
+        True, None, [probe, enc_keys, enc_values, grad_cross, cross_outb, cross_logs]
     )
     g_probe_vec = jnp.sum(probe_rows.astype(F32), axis=0)
     g_probe_mat = gradient(stream_one, probe_rows, probe_weight)
@@ -1004,7 +1012,7 @@
     g_out_mat = gradient(self_outb, out_rows, out_weight)
     grad_self = right_trans(out_rows, out_mat).astype(BF)
     query_rows, key_rows, value_rows = attend_call(
-        True, ids, [queries, all_keys, all_values, grad_self, self_logs]
+        True, ids, [queries, all_keys, all_values, grad_self, self_outb, self_logs]
     )
     g_query_vec = jnp.sum(query_rows.astype(F32), axis=0)
     g_value_vec = jnp.sum(value_rows.astype(F32), axis=0)
@@ -1013,6 +1021,9 @@
     g_value_mat = gradient(tok_all, value_rows, value_weight)
     tok_part = right_trans(key_rows, key_mat) + right_trans(value_rows, value_mat)
     tok_own = grad_first + right_trans(query_rows, query_mat)
+    tok_part, reduce_part = lax.optimization_barrier((tok_part.astype(BF), reduce_part))
+    reduce_part = lax.psum_scatter(reduce_part, "seq", scatter_dimension=1, tiled=True)
+    reduce_sum = reduce_part.astype(F32)
 
     wide_grads = jnp.stack(
         [
@@ -1039,7 +1050,7 @@
         cube,
         [
             enc_part.astype(BF).reshape(cube.n_seq, enc_local, feat_width),
-            tok_part.astype(BF).reshape(cube.n_seq, local_rows, feat_width),
+            tok_part.reshape(cube.n_seq, local_rows, feat_width),
         ]
         + mats
         + [vec_grads],

time: 498 us -> 486 us (0.976)
  Pallas kernels: 354 us -> 337 us
  waiting for transfers between devices: 12.8 us -> 20.6 us
    pallas_call x1, Pallas kernels: 147 us -> 138 us  [scatter_group(): pl.pallas_call(functools.partial(scatter_kernel, cube, pieces, products,...]
    reduce_scatter x1, waiting for transfers between devices: 6.8 us -> 13.5 us  [local(): lax.psum_scatter(reduce_part, 'dp', scatter_dimension=0, tiled=True)]
    pallas_call x4, Pallas kernels: 55.7 us -> 50.7 us  [attend_call(): pl.pallas_call(functools.partial(attend_back_kernel if back else attend_k...]
  transfers between devices with their start and end apart: 3 -> 3, of which waited for: 2 -> 2; matrix products, arithmetic and copies ran while one was open for 17% -> 17% of each run, Pallas kernels for 42% -> 40%
where the time goes in v6:
time: 486 us; the launch traced here: 480 us
  Pallas kernels  337 us (69%)
  matrix products  83.1 us (17%)
  waiting for transfers between devices  20.6 us (4%)
  between operations  15.1 us (3%)
  local copies, waits for them, and re-layouts  12.1 us (2%)
  other arithmetic  11.9 us (2%)
    pallas_call x1, Pallas kernels, gather_all(): pl.pallas_call(functools.partial(gather_kernel, cube, pieces, casts), out...  143 us
    pallas_call x1, Pallas kernels, scatter_group(): pl.pallas_call(functools.partial(scatter_kernel, cube, pieces, products,...  138 us
    pallas_call x4, Pallas kernels, attend_call(): pl.pallas_call(functools.partial(attend_back_kernel if back else attend_k...  50.7 us
    dot_general x10, matrix products, matmul(): return jnp.dot(left_arg, right_arg, preferred_element_type=F32)  45.9 us
    dot_general x10, matrix products, right_trans(): lax.dot_general(left_arg, right_arg, (((1,), (1,)), ((), ())), preferred_...  31.7 us
    reduce_scatter x1, waiting for transfers between devices, local(): lax.psum_scatter(reduce_part, 'dp', scatter_dimension=0, tiled=True)  13.5 us
  transfers between devices with their start and end apart: 3, of which 2 were waited for; matrix products, arithmetic and copies ran while one was open for 17% of the time, Pallas kernels for 40%

profile of v6, /device:TPU:0, one launch (start us, length us, event | category | flops | bytes accessed | tf_op | source)
XLA Modules:
  0.0 480.1 jit_solution(4492449353609994294)
XLA Ops:
  7.3 1.8 convert_element_type.93
  9.1 1.5 concatenate.20
  10.6 143.0 %gather_weights.1 = (bf16[4,256,1024]{2,1,0:T(8,128)(2,1)}, bf16[4,128,1024]{2,1,0:T(8,128)(2,1)}, bf16[2,2,2,4,32,1024]{5,4,3,2,1,0:T(8,128)(2,1)}, bf16[2,2,2,...) custom-call(bf16[256,1024]{1,0:T(8,128)(2,1)} %bitcast.110, ...), custom_call_target="tpu_custom_call" | custom-call | tf_op jit(solution)/shard_map/gather_weights/pallas_call | solution.py:304
  154.0 1.1 copy.67
  155.2 0.6 slice_reduce_fusion.1
  157.1 2.3 fusion.25.refs_2_
  159.4 4.2 convolution_convert_fusion.1.refs_3_
  163.7 2.3 add_convert_fusion.1.refs_4_
  166.1 14.7 %attend.2 = (bf16[256,1024]{1,0:T(8,128)(2,1)S(1)}, f32[8,2,256]{2,1,0:T(2,128)S(1)}) custom-call(s32[1024,2]{1,0:T(8,128)S(1)} %bitcast.101, s32[2,256]{1,0:T(2,128)S(1)} %pad_add_fusion.1.refs_1_, bf16[256,1024]{1,0:T(8,128)(2,1)S(1)} %fusion.25.refs_2_, bf16[1024,1024]{1,0:T(8,128)(2,1)S(1)} %convolution_convert_fusion.1.refs_3_, ...), custom_call_target="tpu_custom_call" | custom-call | flops 1073741824 | bytes 5242880 | tf_op jit(solution)/shard_map/attend/pallas_call | solution.py:833
  180.9 0.8 fusion.39
  182.3 0.4 copy-done.34
  182.6 0.7 fusion.23.refs_0_
  183.6 0.7 copy-done.41
  184.3 1.2 convolution_convert_fusion.2.refs_1_
  185.6 1.3 add_convert_fusion.3.refs_2_
  186.9 9.3 %attend.3 = (bf16[256,1024]{1,0:T(8,128)(2,1)S(1)}, f32[8,2,256]{2,1,0:T(2,128)S(1)}) custom-call(bf16[256,1024]{1,0:T(8,128)(2,1)S(1)} %fusion.23.refs_0_, bf16[512,1024]{1,0:T(8,128)(2,1)S(1)} %convolution_convert_fusion.2.refs_1_, bf16[512,1024]{1,0:T(8,128)(2,1)S(1)} %add_convert_fusion.3.refs_2_), custom_call_target="tpu_custom_call" | custom-call | flops 536870912 | bytes 3145728 | tf_op jit(solution)/shard_map/attend/pallas_call | solution.py:833
  196.2 2.6 fusion.40
  199.5 23.8 %fusion.2 = (bf16[256,4096]{1,0:T(8,128)(2,1)}, f32[256,4096]{1,0:T(8,128)}) fusion(f32[4096]{0:T(1024)S(1)} %slice_bitcast_fusion, bf16[256,1024]{1,0:T(8,128)(2,1)S(1)} %add_convert_fusion.5.refs_3_, bf16[1024,4096]{1,0:T(8,128)(2,1)S(1)} %bitcast.130), kind=kOutput, calls=%fused_computation.7 | convolution fusion | flops 2216689664 | bytes 15220736 | tf_op jit(solution)/shard_map/dot_general | solution.py:26
  223.3 7.0 %all-gather.2.cloned.1.call-done = bf16[4096,1024]{1,0:T(8,128)(2,1)} async-done(((bf16[128,1024]{1,0:T(8,128)(2,1)}), bf16[4096,1024]{1,0:T(8,128)(2,1)}) %all-gather.2.cloned.1.call-update) | async-done | bytes 8388624 | tf_op jit(solution)/shard_map/all_gather | solution.py:917
  230.3 6.5 %fusion.41 = (f32[256]{0:T(256)S(1)}, f32[256,1024]{1,0:T(8,128)S(1)}) fusion(f32[1024]{0:T(1024)S(1)} %add.208, bf16[256,4096]{1,0:T(8,128)(2,1)} %get-tuple-element.190, bf16[4096,1024]{1,0:T(8,128)(2,1)} %all-gather.2.cloned.1.call-done, bf16[256,1024]{1,0:T(8,128)(2,1)S(1)} %add_convert_fusion.5.refs_3_), kind=kOutput, calls=%fused_computation.125 | convolution fusion | flops 2148531968 | bytes 12063744 | tf_op jit(solution)/shard_map/dot_general | solution.py:26
  237.1 0.5 fusion.29
  237.6 1.3 fusion.34
  238.9 5.6 %convolution_convert_fusion = bf16[4096,1024]{1,0:T(8,128)(2,1)} fusion(bf16[256,4096]{1,0:T(8,128)(2,1)S(1)} %copy-done.26, f32[256,1024]{1,0:T(8,128)S(1)} %get-tuple-element.178), kind=kOutput, calls=%fused_computation | convolution fusion | flops 2151940096 | bytes 11534336 | tf_op jit(solution)/shard_map/dot_general | solution.py:30
  244.6 1.1 copy-done.25
  245.7 7.3 %fusion.38 = (f32[4096]{0:T(1024)S(1)}, bf16[256,4096]{1,0:T(8,128)(2,1)S(1)}) fusion(f32[256,4096]{1,0:T(8,128)} %get-tuple-element.191, bf16[4096,1024]{1,0:T(8,128)(2,1)} %all-gather.2.cloned.1.call-done, f32[256,1024]{1,0:T(8,128)S(1)} %copy-done.25), kind=kOutput, calls=%fused_computation.122 | convolution fusion | flops 2159276032 | bytes 15745024 | tf_op jit(solution)/shard_map/dot_general | solution.py:36
  253.0 8.4 %multiply_reduce_fusion = (f32[1024]{0:T(1024)S(1)}, f32[256]{0:T(256)S(1)}, f32[256]{0:T(256)S(1)}, f32[1024]{0:T(1024)S(1)}, f32[256,1024]{1,0:T(8,128)S(1)}) fusion(f32[256,1024]{1,0:T(8,128)S(1)} %get-tuple-element.189, f32[256]{0:T(256)S(1)} %add_rsqrt_fusion.1, f32[256]{0:T(256)S(1)} %broadcast_multiply_fusion.7, f32[1024]{0:T(1024)S(1)} %mul.199, ...), kind=kOutput, calls=%fused_computation.63 | convolution fusion | flops 2150102528 | bytes 13647872 | tf_op jit(solution)/shard_map/dot_general | solution.py:36
  261.4 0.4 fusion.36
  261.9 0.8 copy-done.29
  262.7 0.5 copy-done.48
  263.1 0.7 convolution_convert_fusion.4.refs_3_
  263.9 10.9 %attend_back.2 = (bf16[256,1024]{1,0:T(8,128)(2,1)S(1)}, bf16[512,1024]{1,0:T(8,128)(2,1)S(1)}, bf16[512,1024]{1,0:T(8,128)(2,1)S(1)}) custom-call(bf16[256,1024]{1,0:T(8,128)(2,1)S(1)} %copy-done.13, bf16[512,1024]{1,0:T(8,128)(2,1)S(1)} %copy-done.15, bf16[512,1024]{1,0:T(8,128)(2,1)} %copy-done.16, ...), custom_call_target="tpu_custom_call" | custom-call | flops 1879048192 | bytes 11010048 | tf_op jit(solution)/shard_map/attend_back/pallas_call | solution.py:833
  274.9 1.1 multiply_reduce_fusion.1
  276.5 0.9 copy-done.47
  277.4 0.8 convolution_convert_fusion.3.refs_5_
  278.3 15.8 %attend_back.3 = (bf16[256,1024]{1,0:T(8,128)(2,1)S(1)}, bf16[1024,1024]{1,0:T(8,128)(2,1)S(1)}, bf16[1024,1024]{1,0:T(8,128)(2,1)}) custom-call(s32[1024,2]{1,0:T(8,128)S(1)} %bitcast.102, s32[2,256]{1,0:T(2,128)S(1)} %pad_add_fusion.1.refs_1_, bf16[256,1024]{1,0:T(8,128)(2,1)S(1)} %copy-done.11, bf16[1024,1024]{1,0:T(8,128)(2,1)} %copy-done.17, ...), custom_call_target="tpu_custom_call" | custom-call | flops 3758096384 | bytes 18350080 | tf_op jit(solution)/shard_map/attend_back/pallas_call | solution.py:833
  294.2 2.4 fusion.43
  296.7 0.6 copy-done.44
  297.4 3.7 add_convert_fusion
  301.1 13.5 %reduce-scatter.3.cloned.1.call-done = bf16[1,4,128,1024]{3,2,1,0:T(8,128)(2,1)} async-done(((bf16[8,4,128,1024]{3,2,1,0:T(8,128)(2,1)}), bf16[1,4,128,1024]{3,2,1,0:T(8,128)(2,1)}) %reduce-scatter.3.cloned.1.call-update) | async-done | bytes 1048592 | tf_op jit(solution)/shard_map/reduce_scatter | solution.py:973
  314.6 1.1 convert_reduce_fusion.2
  316.2 2.0 convert_reduce_fusion
  319.8 0.8 maximum_maximum_fusion.refs_2_
  320.6 3.7 convolution_add_fusion.2.refs_12_
  324.3 1.3 fusion.42
  325.9 2.3 add_convert_fusion.2
  328.1 138.1 %scatter_grads.1 = (f32[128,1024]{1,0:T(8,128)}, f32[256,1024]{1,0:T(8,128)}, f32[32,4096]{1,0:T(8,128)}, f32[32,1024]{1,0:T(8,128)}, f32[32,1024]{1,0:T(8,128)}...) custom-call(bf16[4,128,1024]{2,1,0:T(8,128)(2,1)} %bitcast.117, ...), custom_call_target="tpu_custom_call" | custom-call | tf_op jit(solution)/shard_map/scatter_grads/pallas_call | solution.py:650
  466.3 5.2 %hand_out.1 = (f32[128,1024]{1,0:T(8,128)}, f32[32,4096]{1,0:T(8,128)}, f32[32,1024]{1,0:T(8,128)}, f32[32,1024]{1,0:T(8,128)}, f32[32,1024]{1,0:T(8,128)}, /*in...) custom-call(f32[128,1024]{1,0:T(8,128)} %get-tuple-element.115.refs_, ...), custom_call_target="tpu_custom_call" | custom-call | tf_op jit(solution)/shard_map/hand_out/pallas_call | solution.py:721
  471.5 1.8 bitcast_convert_fusion
  (164 shorter events, 6.6 us)
Async XLA Ops:
  7.2 149.8 %copy-start.33 = (bf16[1,256,1024]{2,1,0:T(8,128)(2,1)S(1)}, bf16[1,256,1024]{2,1,0:T(8,128)(2,1)}, u32[]{:S(2)}) copy-start(bf16[1,256,1024]{2,1,0:T(8,128)(2,1)} %param.29) | copy-start | bytes 1572868
  7.2 148.8 %copy-start.38 = (s32[1,1024]{1,0:T(1,128)S(1)}, s32[1,1024]{1,0:T(1,128)}, u32[]{:S(2)}) copy-start(s32[1,1024]{1,0:T(1,128)} %param.32) | copy-start | bytes 12292
  7.2 148.8 %copy-start.37 = (s32[1,1024]{1,0:T(1,128)S(1)}, s32[1,1024]{1,0:T(1,128)}, u32[]{:S(2)}) copy-start(s32[1,1024]{1,0:T(1,128)} %param.33) | copy-start | bytes 12292
  7.2 223.0 %all-gather.2.cloned.1.call-start = ((), (), s32[]{:S(2)}) async-start(), calls=%async_computation.2 | async-start | bytes 8650752 | tf_op jit(solution)/shard_map/all_gather | solution.py:917
  153.6 5.8 %copy-start.27 = (bf16[4,256,1024]{2,1,0:T(8,128)(2,1)S(1)}, bf16[4,256,1024]{2,1,0:T(8,128)(2,1)}, u32[]{:S(2)}) copy-start(bf16[4,256,1024]{2,1,0:T(8,128)(2,1)} %get-tuple-element.93) | copy-start | bytes 6291460
  153.6 161.0 %reduce-scatter.3.cloned.1.call-start = ((), (), s32[]{:S(2)}) async-start(), calls=%async_computation.3 | async-start | bytes 9437184 | tf_op jit(solution)/shard_map/reduce_scatter | solution.py:973
  156.2 9.8 %copy-start.8 = (s32[2,1024]{0,1:T(8,128)}, s32[2,1024]{0,1:T(8,128)S(1)}, u32[]{:S(2)}) copy-start(s32[2,1024]{0,1:T(8,128)S(1)} %copy.62) | copy-start | bytes 24580
  159.4 6.7 %copy-start.10 = (bf16[256,1024]{1,0:T(8,128)(2,1)}, bf16[256,1024]{1,0:T(8,128)(2,1)S(1)}, u32[]{:S(2)}) copy-start(bf16[256,1024]{1,0:T(8,128)(2,1)S(1)} %fusion.25.refs_2_) | copy-start | bytes 1572868
  159.4 4.3 copy-start.43
  163.7 2.4 copy-start.17
  166.0 15.7 %copy-start.18 = (bf16[1024,1024]{1,0:T(8,128)(2,1)}, bf16[1024,1024]{1,0:T(8,128)(2,1)S(1)}, u32[]{:S(2)}) copy-start(bf16[1024,1024]{1,0:T(8,128)(2,1)S(1)} %add_convert_fusion.1.refs_4_) | copy-start | bytes 6291460
  166.0 14.8 %copy-start.46 = (bf16[2,2,2,4,32,1024]{5,4,3,2,1,0:T(8,128)(2,1)S(1)}, bf16[2,2,2,4,32,1024]{5,4,3,2,1,0:T(8,128)(2,1)}, u32[]{:S(2)}) copy-start(bf16[2,2,2,4,32,1024]{5,4,3,2,1,0:T(8,128)(2,1)} %get-tuple-element.97) | copy-start | bytes 6291460
  180.8 2.5 copy-start.5
  181.7 3.9 copy-start.19
  181.7 1.9 copy-start.36
  181.7 2.6 copy-start.41
  182.3 14.0 %copy-start.31 = (bf16[256,1024]{1,0:T(8,128)(2,1)}, bf16[256,1024]{1,0:T(8,128)(2,1)S(1)}, u32[]{:S(2)}) copy-start(bf16[256,1024]{1,0:T(8,128)(2,1)S(1)} %add_convert_fusion.6.refs_7_) | copy-start | bytes 1572868
  183.4 3.5 copy-start.12
  183.4 2.2 copy-start.39
  185.6 10.6 %copy-start.14 = (bf16[512,1024]{1,0:T(8,128)(2,1)}, bf16[512,1024]{1,0:T(8,128)(2,1)S(1)}, u32[]{:S(2)}) copy-start(bf16[512,1024]{1,0:T(8,128)(2,1)S(1)} %convolution_convert_fusion.2.refs_1_) | copy-start | bytes 3145732
  185.6 13.8 %slice-start = ((s8[8388608]{0:T(1024)(128)(4,1)}), s8[4194304]{0:T(1024)(128)(4,1)S(1)}, s32[]{:S(2)}) async-start(s8[8388608]{0:T(1024)(128)(4,1)} %bitcast.128), calls=%async_computation.5 | async-start | bytes 8388608
  186.9 11.9 %copy-start.16 = (bf16[512,1024]{1,0:T(8,128)(2,1)}, bf16[512,1024]{1,0:T(8,128)(2,1)S(1)}, u32[]{:S(2)}) copy-start(bf16[512,1024]{1,0:T(8,128)(2,1)S(1)} %add_convert_fusion.3.refs_2_) | copy-start | bytes 3145732
  186.9 12.6 %slice-start.1 = ((s8[8388608]{0:T(1024)(128)(4,1)}), s8[4194304]{0:T(1024)(128)(4,1)S(1)}, s32[]{:S(2)}) async-start(s8[8388608]{0:T(1024)(128)(4,1)} %bitcast.128), calls=%async_computation.6 | async-start | bytes 8388608
  196.2 67.7 %copy-start.7 = (bf16[256,1024]{1,0:T(8,128)(2,1)}, bf16[256,1024]{1,0:T(8,128)(2,1)S(1)}, u32[]{:S(2)}) copy-start(bf16[256,1024]{1,0:T(8,128)(2,1)S(1)} %get-tuple-element.102.refs_4_.refs_5_) | copy-start | bytes 1572868
  199.4 30.8 %copy-start.32 = (bf16[256,1024]{1,0:T(8,128)(2,1)}, bf16[256,1024]{1,0:T(8,128)(2,1)S(1)}, u32[]{:S(2)}) copy-start(bf16[256,1024]{1,0:T(8,128)(2,1)S(1)} %add_convert_fusion.5.refs_3_) | copy-start | bytes 1572868
  230.3 6.8 %copy-start.23 = (bf16[1,256,1024]{2,1,0:T(8,128)(2,1)S(1)}, bf16[1,256,1024]{2,1,0:T(8,128)(2,1)}, u32[]{:S(2)}) copy-start(bf16[1,256,1024]{2,1,0:T(8,128)(2,1)} %param.31) | copy-start | bytes 1572868
  236.8 2.1 copy-start.26
  238.9 5.6 %copy-start.24 = (f32[256,1024]{1,0:T(8,128)}, f32[256,1024]{1,0:T(8,128)S(1)}, u32[]{:S(2)}) copy-start(f32[256,1024]{1,0:T(8,128)S(1)} %get-tuple-element.178) | copy-start | bytes 3145732
  244.5 227.0 %reduce-scatter.5.cloned.1.call-start = ((), (), s32[]{:S(2)}) async-start(), calls=%async_computation.4 | async-start | bytes 1310720 | tf_op jit(solution)/shard_map/reduce_scatter | solution.py:1025
  253.0 8.4 %copy-start.28 = (bf16[256,4096]{1,0:T(8,128)(2,1)}, bf16[256,4096]{1,0:T(8,128)(2,1)S(1)}, u32[]{:S(2)}) copy-start(bf16[256,4096]{1,0:T(8,128)(2,1)S(1)} %get-tuple-element.184.refs_4_) | copy-start | bytes 6291460
  261.4 1.8 copy-start.48
  261.4 2.6 copy-start.13
  261.4 2.5 copy-start.15
  263.9 11.0 %copy-start.20 = (f32[256,1024]{1,0:T(8,128)S(1)}, f32[256,1024]{1,0:T(8,128)}, u32[]{:S(2)}) copy-start(f32[256,1024]{1,0:T(8,128)} %copy-done.19) | copy-start | bytes 3145732
  263.9 11.0 %copy-start.35 = (bf16[2,2,2,4,32,1024]{5,4,3,2,1,0:T(8,128)(2,1)S(1)}, bf16[2,2,2,4,32,1024]{5,4,3,2,1,0:T(8,128)(2,1)}, u32[]{:S(2)}) copy-start(bf16[2,2,2,4,32,1024]{5,4,3,2,1,0:T(8,128)(2,1)} %get-tuple-element.98) | copy-start | bytes 6291460
  274.8 43.7 %copy-start.1 = (bf16[256,1024]{1,0:T(8,128)(2,1)}, bf16[256,1024]{1,0:T(8,128)(2,1)S(1)}, u32[]{:S(2)}) copy-start(bf16[256,1024]{1,0:T(8,128)(2,1)S(1)} %get-tuple-element.109.refs_8_) | copy-start | bytes 1572868
  274.8 49.5 %copy-start.4 = (bf16[512,1024]{1,0:T(8,128)(2,1)}, bf16[512,1024]{1,0:T(8,128)(2,1)S(1)}, u32[]{:S(2)}) copy-start(bf16[512,1024]{1,0:T(8,128)(2,1)S(1)} %get-tuple-element.107.refs_10_) | copy-start | bytes 3145732
  274.8 50.8 %copy-start.2 = (bf16[512,1024]{1,0:T(8,128)(2,1)}, bf16[512,1024]{1,0:T(8,128)(2,1)S(1)}, u32[]{:S(2)}) copy-start(bf16[512,1024]{1,0:T(8,128)(2,1)S(1)} %get-tuple-element.108.refs_11_) | copy-start | bytes 3145732
  274.9 2.5 copy-start.47
  276.0 2.2 copy-start.6
  276.0 2.2 copy-start.9
  276.0 2.3 copy-start.11
  278.3 15.9 %copy-start.45 = (bf16[2,2,2,4,32,1024]{5,4,3,2,1,0:T(8,128)(2,1)S(1)}, bf16[2,2,2,4,32,1024]{5,4,3,2,1,0:T(8,128)(2,1)}, u32[]{:S(2)}) copy-start(bf16[2,2,2,4,32,1024]{5,4,3,2,1,0:T(8,128)(2,1)} %get-tuple-element.94) | copy-start | bytes 6291460
  294.2 2.4 copy-start.3
  294.2 26.4 %copy-start = (bf16[256,1024]{1,0:T(8,128)(2,1)}, bf16[256,1024]{1,0:T(8,128)(2,1)S(1)}, u32[]{:S(2)}) copy-start(bf16[256,1024]{1,0:T(8,128)(2,1)S(1)} %get-tuple-element.114.refs_15_) | copy-start | bytes 1572868
  294.2 2.5 copy-start.22
  294.2 3.1 copy-start.44
  319.7 4.6 copy-start.42
  (6 other events, 8.0 us)
Sparse Core Ops, SparseCore 0:
  153.7 76.4 all-gather.1
  244.6 69.9 reduce-scatter.2
  317.0 29.9 reduce-scatter.4

commit v7 on v6

--- a/solution.py
+++ b/solution.py
@@ -233,10 +233,13 @@
 
 def gather_kernel(cube, pieces, casts, *refs):
     count = 1 + max(piece[0] for piece in pieces)
-    ins, outs = list(refs[:count]), refs[count : 2 * count]
-    wide, stage = refs[2 * count : -4][: len(casts)], refs[2 * count : -4][len(casts) :]
-    send_sem, recv_sem, local_sem, cast_sem = refs[-4:]
+    ins, stays, outs, stays_out = list(refs[:count]), refs[count], refs[count + 1 : -6][:count], refs[2 * count + 1]
+    rest = refs[2 * count + 2 : -6]
+    wide, stage = rest[: len(casts)], rest[len(casts) :]
+    stays_wide, stays_narrow, send_sem, recv_sem, local_sem, cast_sem = refs[-6:]
     here = Place(cube)
+    stays_in = pltpu.make_async_copy(stays, stays_wide, cast_sem.at[len(casts)])
+    stays_back = pltpu.make_async_copy(stays_narrow, stays_out, cast_sem.at[len(casts) + 1])
     loads = [
         pltpu.make_async_copy(ins[array], held, cast_sem.at[turn])
         for turn, (array, held) in enumerate(zip(casts, wide))
@@ -266,10 +269,15 @@
         )
     for own, _, _ in plans:
         own.start()
+    stays_in.start()
     meet(cube, here)
     in_slots([stages for _, stages, _ in plans], 3)
+    stays_in.wait()
+    stays_narrow[...] = stays_wide[...].astype(BF)
+    stays_back.start()
     for _, _, finish in plans:
         finish()
+    stays_back.wait()
 
 
 def cut_columns(kinds, arrays, first, last):
@@ -291,7 +299,7 @@
     return tuple(piece for _, _, piece in sorted(placed, key=lambda item: item[:2]))
 
 
-def gather_all(cube, arrays, kinds, casts, collective_id):
+def gather_all(cube, arrays, kinds, casts, stays, collective_id):
     pieces = cut_columns(kinds, arrays, 0.3, 1.0)
     outs = [
         jax.ShapeDtypeStruct(
@@ -303,16 +311,17 @@
     anywhere = pl.BlockSpec(memory_space=pl.ANY)
     return pl.pallas_call(
         functools.partial(gather_kernel, cube, pieces, casts),
-        out_shape=outs,
-        in_specs=[anywhere] * len(arrays),
-        out_specs=[anywhere] * len(arrays),
+        out_shape=outs + [jax.ShapeDtypeStruct(stays.shape, BF)],
+        in_specs=[anywhere] * (len(arrays) + 1),
+        out_specs=[anywhere] * (len(arrays) + 1),
         scratch_shapes=[pltpu.VMEM(arrays[index].shape, F32) for index in casts]
         + [pltpu.VMEM(arrays[index].shape, BF) for index in casts]
+        + [pltpu.VMEM(stays.shape, F32), pltpu.VMEM(stays.shape, BF)]
         + [
             pltpu.SemaphoreType.DMA((len(pieces), slots)),
             pltpu.SemaphoreType.DMA((len(pieces), slots)),
             pltpu.SemaphoreType.DMA((len(pieces),)),
-            pltpu.SemaphoreType.DMA((len(casts),)),
+            pltpu.SemaphoreType.DMA((len(casts) + 2,)),
         ],
         compiler_params=pltpu.CompilerParams(
             collective_id=collective_id,
@@ -320,7 +329,7 @@
             vmem_limit_bytes=60 * 1024 * 1024,
         ),
         name="gather_weights",
-    )(*arrays)
+    )(*arrays, stays)
 
 
 def add_block(total, part):
@@ -690,9 +699,10 @@
 
 
 def hand_out_kernel(count, parts, *refs):
-    sums, vec, part_sum, part_own = refs[:count], refs[count], refs[count + 1], refs[count + 2]
-    refs = refs[count + 3 :]
-    outs, vec_outs, part_out = refs[:count], refs[count : count + len(parts)], refs[count + len(parts)]
+    sums, vec, part_sum, part_own, narrow = refs[:count], *refs[count : count + 4]
+    refs = refs[count + 4 :]
+    outs, vec_outs, refs = refs[:count], refs[count : count + len(parts)], refs[count + len(parts) :]
+    part_out, wide = refs[:2]
     held, sem = refs[-1 - count : -1], refs[-1]
     ins = [
         pltpu.make_async_copy(one, mid, sem.at[0, turn])
@@ -707,6 +717,7 @@
     for row, (size, out) in enumerate(zip(parts, vec_outs)):
         out[...] = vec[row, 0:size]
     part_out[...] = part_own[...] + part_sum[...]
+    wide[...] = narrow[...].astype(F32)
     for before, copy in zip(ins, copies):
         before.wait()
         copy.start()
@@ -714,7 +725,7 @@
         copy.wait()
 
 
-def hand_out(sums, vec, parts, part_sum, part_own):
+def hand_out(sums, vec, parts, part_sum, part_own, narrow):
     anywhere = pl.BlockSpec(memory_space=pl.ANY)
     inside = pl.BlockSpec(memory_space=pltpu.VMEM)
     count = len(sums)
@@ -722,14 +733,14 @@
         functools.partial(hand_out_kernel, count, parts),
         out_shape=[jax.ShapeDtypeStruct(one.shape, F32) for one in sums]
         + [jax.ShapeDtypeStruct((size,), F32) for size in parts]
-        + [jax.ShapeDtypeStruct(part_sum.shape, F32)],
-        in_specs=[anywhere] * count + [inside] * 3,
-        out_specs=[anywhere] * count + [inside] * (len(parts) + 1),
+        + [jax.ShapeDtypeStruct(part_sum.shape, F32), jax.ShapeDtypeStruct(narrow.shape, F32)],
+        in_specs=[anywhere] * count + [inside] * 4,
+        out_specs=[anywhere] * count + [inside] * (len(parts) + 2),
         scratch_shapes=[pltpu.VMEM(one.shape, F32) for one in sums]
         + [pltpu.SemaphoreType.DMA((2, count))],
         compiler_params=pltpu.CompilerParams(vmem_limit_bytes=60 * 1024 * 1024),
         name="hand_out",
-    )(*sums, vec, part_sum, part_own)
+    )(*sums, vec, part_sum, part_own, narrow)
 
 
 def write_bias(bias, key_ids, query_ids):
@@ -848,6 +859,81 @@
     )(*arrays)
 
 
+def close_kernel(steps, act_ref, weight_ref, stream_ref, cot_ref, vec_ref, *refs):
+    out_ref, grad_ref, rows_ref, sums_ref, weight_grad_ref, total = refs
+    step = pl.program_id(0)
+    span = act_ref.shape[1] // steps
+
+    def columns(index):
+        return act_ref[:, pl.ds(pl.multiple_of(index * span, span), span)]
+
+    @pl.when(step == 0)
+    def _():
+        total[...] = stream_ref[...].astype(F32) + vec_ref[0:1, :]
+
+    @pl.when(step < steps)
+    def _():
+        total[...] += matmul(columns(step), weight_ref[...])
+
+    @pl.when(step == steps - 1)
+    def _():
+        normed, inv_std = layer_stats(total[...])
+        gain = vec_ref[1:2, :]
+        out_ref[...] = (normed * gain + vec_ref[2:3, :]).astype(BF)
+        cot = cot_ref[...].astype(F32)
+        grad = layer_back(cot * gain, normed, inv_std)
+        grad_ref[...] = grad
+        rows_ref[...] = grad.astype(BF)
+        sums_ref[0:1, :] = jnp.sum(cot, axis=0, keepdims=True)
+        sums_ref[1:2, :] = jnp.sum(cot * normed, axis=0, keepdims=True)
+        sums_ref[2:3, :] = jnp.sum(grad, axis=0, keepdims=True)
+
+    @pl.when(step >= steps)
+    def _():
+        weight_grad_ref[...] = left_outer(columns(step - steps), rows_ref[...]).astype(BF)
+
+
+def close_layer(activated, weight, stream, cotangent, bias, gain, shift):
+    rows, hidden = activated.shape
+    width = stream.shape[1]
+    steps = 4
+    whole = lambda shape: pl.BlockSpec(shape, lambda i: (0, 0))
+    vecs = jnp.stack([bias, gain, shift])
+    return pl.pallas_call(
+        functools.partial(close_kernel, steps),
+        grid=(2 * steps,),
+        in_specs=[
+            whole((rows, hidden)),
+            pl.BlockSpec((hidden // steps, width), lambda i: (jnp.minimum(i, steps - 1), 0)),
+            whole((rows, width)),
+            whole((rows, width)),
+            whole((3, width)),
+        ],
+        out_specs=[
+            whole((rows, width)),
+            whole((rows, width)),
+            whole((rows, width)),
+            whole((3, width)),
+            pl.BlockSpec((hidden // steps, width), lambda i: (jnp.maximum(i - steps, 0), 0)),
+        ],
+        out_shape=[
+            jax.ShapeDtypeStruct((rows, width), BF),
+            jax.ShapeDtypeStruct((rows, width), F32),
+            jax.ShapeDtypeStruct((rows, width), BF),
+            jax.ShapeDtypeStruct((3, width), F32),
+            jax.ShapeDtypeStruct((hidden, width), BF),
+        ],
+        scratch_shapes=[pltpu.VMEM((rows, width), F32)],
+        cost_estimate=pl.CostEstimate(
+            flops=4 * rows * hidden * width,
+            bytes_accessed=4 * hidden * width + 12 * rows * width,
+            transcendentals=rows,
+        ),
+        compiler_params=pltpu.CompilerParams(vmem_limit_bytes=58 * 1024 * 1024),
+        name="close_layer",
+    )(activated, weight, stream, cotangent, vecs)
+
+
 WIDE = 13
 
 
@@ -911,9 +997,10 @@
         [flat, enc_flat] + blocks + [packed.reshape(vec_block)],
         kinds,
         tuple(range(2, 2 + len(blocks))),
+        reduce_weight,
         0,
     )
-    late, vec_all = lax.optimization_barrier((reduce_weight.astype(BF), gathered[11]))
+    late, vec_all = lax.optimization_barrier((gathered[12], gathered[11]))
     reduce_mat = lax.all_gather(late, ("dp", "seq"), axis=0, tiled=True)
     n_dev = cube.n_dev
     tok_all = gathered[0].reshape(cube.n_seq * local_rows, feat_width)
@@ -957,24 +1044,23 @@
     normed_two, inv_two = layer_stats(second_sum)
     stream_two = (normed_two * gain_second + shift_second).astype(BF)
     expanded = matmul(stream_two, expand_mat) + expand_vec
-    activated = jax.nn.gelu(expanded, approximate=False).astype(BF)
-    third_sum = stream_two.astype(F32) + matmul(activated, reduce_mat) + reduce_vec
-    normed_three, inv_three = layer_stats(third_sum)
-    output = (normed_three * gain_third + shift_third).astype(BF)
-
-    grad_output = cotangent.reshape(local_rows, feat_width).astype(F32)
-    g_shift_third = jnp.sum(grad_output, axis=0)
-    g_gain_third = jnp.sum(grad_output * normed_three, axis=0)
-    grad_three = layer_back(grad_output * gain_third, normed_three, inv_three)
-    reduce_rows = grad_three.astype(BF)
-    g_reduce_vec = jnp.sum(grad_three, axis=0)
-    g_reduce_mat = left_outer(activated, reduce_rows).astype(BF)
+    below = 0.5 * (1.0 + jax.scipy.special.erf(expanded * INV_ROOT_TWO))
+    activated = (expanded * below).astype(BF)
+    slope = below + expanded * DENSITY_CONST * jnp.exp(-0.5 * expanded * expanded)
+    slope, activated, reduce_mat = lax.optimization_barrier((slope, activated, reduce_mat))
+    output, grad_three, reduce_rows, third_sums, g_reduce_mat = close_layer(
+        activated,
+        reduce_mat,
+        stream_two,
+        cotangent.reshape(local_rows, feat_width),
+        reduce_vec,
+        gain_third,
+        shift_third,
+    )
+    g_shift_third, g_gain_third, g_reduce_vec = third_sums[0], third_sums[1], third_sums[2]
     reduce_part = g_reduce_mat.reshape((cube.n_dp, cube.n_seq) + reduce_weight.shape)
     reduce_part = lax.psum_scatter(reduce_part, "dp", scatter_dimension=0, tiled=True)
     grad_act = right_trans(reduce_rows, reduce_mat)
-    slope = 0.5 * (
-        1.0 + jax.scipy.special.erf(expanded * INV_ROOT_TWO)
-    ) + expanded * DENSITY_CONST * jnp.exp(-0.5 * expanded * expanded)
     grad_expanded = grad_act * slope
     g_expand_vec = jnp.sum(grad_expanded, axis=0)
     expand_rows = grad_expanded.astype(BF)
@@ -1021,9 +1107,8 @@
     g_value_mat = gradient(tok_all, value_rows, value_weight)
     tok_part = right_trans(key_rows, key_mat) + right_trans(value_rows, value_mat)
     tok_own = grad_first + right_trans(query_rows, query_mat)
-    tok_part, reduce_part = lax.optimization_barrier((tok_part.astype(BF), reduce_part))
-    reduce_part = lax.psum_scatter(reduce_part, "seq", scatter_dimension=1, tiled=True)
-    reduce_sum = reduce_part.astype(F32)
+    tok_part = tok_part.astype(BF)
+    enc_part = enc_part.astype(BF)
 
     wide_grads = jnp.stack(
         [
@@ -1046,10 +1131,14 @@
         expand_weight, merge_weight, probe_weight, lookup_weight, content_weight, out_weight,
         query_weight, key_weight, value_weight,
     ]
+    tok_part, enc_part, tok_own, vec_grads, reduce_part = lax.optimization_barrier(
+        (tok_part, enc_part, tok_own, vec_grads, reduce_part)
+    )
+    reduce_part = lax.psum_scatter(reduce_part, "seq", scatter_dimension=1, tiled=True)
     sums = scatter_all(
         cube,
         [
-            enc_part.astype(BF).reshape(cube.n_seq, enc_local, feat_width),
+            enc_part.reshape(cube.n_seq, enc_local, feat_width),
             tok_part.reshape(cube.n_seq, local_rows, feat_width),
         ]
         + mats
@@ -1058,18 +1147,22 @@
         1,
     )
     done = hand_out(
-        [sums[0]] + list(sums[2:11]), sums[11], (part,) * WIDE + (long_part,), sums[1], tok_own
+        [sums[0]] + list(sums[2:11]),
+        sums[11],
+        (part,) * WIDE + (long_part,),
+        sums[1],
+        tok_own,
+        reduce_part.reshape(reduce_weight.shape),
     )
     encoded_grad = done[0]
     (
         expand_sum, merge_sum, probe_sum, lookup_sum, content_sum, out_sum, query_sum, key_sum, value_sum,
     ) = [one.reshape(w.shape) for one, w in zip(done[1:10], shards)]
-    reduce_sum = reduce_sum.reshape(reduce_weight.shape)
     (
         query_vs, value_vs, out_vs, gain1_vs, shift1_vs, probe_vs, content_vs,
         merge_vs, gain2_vs, shift2_vs, reduce_vs, gain3_vs, shift3_vs, expand_vs,
     ) = done[10:24]
-    tokens_grad = done[24]
+    tokens_grad, reduce_sum = done[24:26]
     return (
         output[None],
         tokens_grad[None],

time: 486 us -> 476 us (0.979)
  matrix products: 83.1 us -> 50.1 us
  Pallas kernels: 337 us -> 356 us
  waiting for transfers between devices: 20.6 us -> 27.4 us
  other arithmetic: 11.9 us -> 5.71 us
    dot_general x10 -> x9, matrix products: 45.9 us -> 17.9 us  [matmul(): return jnp.dot(left_arg, right_arg, preferred_element_type=F32)]
    all_gather x1, waiting for transfers between devices: 6.98 us -> 27.3 us  [local(): reduce_mat = lax.all_gather(late, ('dp', 'seq'), axis=0, tiled=True)]
    reduce_scatter x1, waiting for transfers between devices: 13.5 us -> 0.01 us  [local(): lax.psum_scatter(reduce_part, 'dp', scatter_dimension=0, tiled=True)]
    pallas_call x0 -> x1, Pallas kernels: none -> 13.2 us  [close_layer(): pl.pallas_call(functools.partial(close_kernel, steps), grid=(2 * steps,),...]
    pallas_call x1, Pallas kernels: 138 us -> 144 us  [scatter_group(): pl.pallas_call(functools.partial(scatter_kernel, cube, pieces, products,...]
    dot_general x1 -> x0, matrix products: 5.6 us -> none  [left_outer(): lax.dot_general(left_arg, right_arg, (((0,), (0,)), ((), ())), preferred_...]
    unnamed x103 -> x107, local copies, waits for them, and re-layouts: 7.07 us -> 9.98 us
  transfers between devices with their start and end apart: 3 -> 3, of which waited for: 2 -> 1; matrix products, arithmetic and copies ran while one was open for 17% -> 13% of each run, Pallas kernels for 40% -> 41%
where the time goes in v7:
time: 476 us; the launch traced here: 470 us
  Pallas kernels  356 us (75%)
  matrix products  50.1 us (11%)
  waiting for transfers between devices  27.4 us (6%)
  local copies, waits for them, and re-layouts  15 us (3%)
  between operations  14.8 us (3%)
  other arithmetic  5.71 us (1%)
    pallas_call x1, Pallas kernels, scatter_group(): pl.pallas_call(functools.partial(scatter_kernel, cube, pieces, products,...  144 us
    pallas_call x1, Pallas kernels, gather_all(): pl.pallas_call(functools.partial(gather_kernel, cube, pieces, casts), out...  143 us
    pallas_call x4, Pallas kernels, attend_call(): pl.pallas_call(functools.partial(attend_back_kernel if back else attend_k...  50.5 us
    dot_general x10, matrix products, right_trans(): lax.dot_general(left_arg, right_arg, (((1,), (1,)), ((), ())), preferred_...  32.2 us
    all_gather x1, waiting for transfers between devices, local(): reduce_mat = lax.all_gather(late, ('dp', 'seq'), axis=0, tiled=True)  27.3 us
    dot_general x9, matrix products, matmul(): return jnp.dot(left_arg, right_arg, preferred_element_type=F32)  17.9 us
    pallas_call x1, Pallas kernels, close_layer(): pl.pallas_call(functools.partial(close_kernel, steps), grid=(2 * steps,),...  13.2 us
    unnamed x107, local copies, waits for them, and re-layouts  9.98 us
  transfers between devices with their start and end apart: 3, of which 1 were waited for; matrix products, arithmetic and copies ran while one was open for 13% of the time, Pallas kernels for 41%

profile of v7, /device:TPU:0, one launch (start us, length us, event | category | flops | bytes accessed | tf_op | source)
XLA Modules:
  0.0 470.1 jit_solution(2128616667794572292)
XLA Ops:
  7.3 1.5 concatenate.20
  8.7 143.1 %gather_weights.1 = (bf16[4,256,1024]{2,1,0:T(8,128)(2,1)}, bf16[4,128,1024]{2,1,0:T(8,128)(2,1)}, bf16[2,2,2,4,32,1024]{5,4,3,2,1,0:T(8,128)(2,1)}, bf16[2,2,2,...) custom-call(bf16[256,1024]{1,0:T(8,128)(2,1)} %bitcast.88, ...), custom_call_target="tpu_custom_call" | custom-call | tf_op jit(solution)/shard_map/gather_weights/pallas_call | solution.py:312
  151.8 0.4 reduce-scatter.3.cloned.1.call-start
  152.2 0.9 copy.76
  153.3 0.6 slice_reduce_fusion.2
  155.2 2.5 fusion.9.refs_2_
  157.7 2.3 convolution_convert_fusion.refs_3_
  160.0 2.3 add_convert_fusion.1.refs_4_
  162.4 14.9 %attend.2 = (bf16[256,1024]{1,0:T(8,128)(2,1)S(1)}, f32[8,2,256]{2,1,0:T(2,128)S(1)}) custom-call(s32[1024,2]{1,0:T(8,128)S(1)} %bitcast.79, s32[2,256]{1,0:T(2,128)S(1)} %pad_add_fusion.1.refs_1_, bf16[256,1024]{1,0:T(8,128)(2,1)S(1)} %fusion.9.refs_2_, bf16[1024,1024]{1,0:T(8,128)(2,1)S(1)} %convolution_convert_fusion.refs_3_, ...), custom_call_target="tpu_custom_call" | custom-call | flops 1073741824 | bytes 5242880 | tf_op jit(solution)/shard_map/attend/pallas_call | solution.py:844
  177.3 0.8 fusion.14
  178.8 1.6 copy-done.31
  180.3 0.7 fusion.7.refs_0_
  181.3 1.3 convolution_convert_fusion.1.refs_1_
  182.6 0.3 copy-done.41
  182.9 1.3 add_convert_fusion.3.refs_2_
  184.2 9.3 %attend.3 = (bf16[256,1024]{1,0:T(8,128)(2,1)S(1)}, f32[8,2,256]{2,1,0:T(2,128)S(1)}) custom-call(bf16[256,1024]{1,0:T(8,128)(2,1)S(1)} %fusion.7.refs_0_, bf16[512,1024]{1,0:T(8,128)(2,1)S(1)} %convolution_convert_fusion.1.refs_1_, bf16[512,1024]{1,0:T(8,128)(2,1)S(1)} %add_convert_fusion.3.refs_2_), custom_call_target="tpu_custom_call" | custom-call | flops 536870912 | bytes 3145728 | tf_op jit(solution)/shard_map/attend/pallas_call | solution.py:844
  193.5 0.7 pad_maximum_fusion.vec_ref
  194.2 0.8 fusion.15
  195.6 5.9 %multiply_convert_fusion = (bf16[256,4096]{1,0:T(8,128)(2,1)}, f32[256,4096]{1,0:T(8,128)}) fusion(f32[4096]{0:T(1024)S(1)} %slice_bitcast_fusion, bf16[256,1024]{1,0:T(8,128)(2,1)S(1)} %add_convert_fusion.4.stream_ref.refs_3_, bf16[1024,4096]{1,0:T(8,128)(2,1)S(1)} %bitcast.112), kind=kOutput, calls=%fused_computation.8 | convolution fusion | flops 2159017984 | bytes 15220736 | tf_op jit(solution)/shard_map/dot_general | solution.py:26
  201.5 27.3 %all-gather.2.cloned.1.call-done.weight_ref = bf16[4096,1024]{1,0:T(8,128)(2,1)} async-done(((bf16[128,1024]{1,0:T(8,128)(2,1)}), bf16[4096,1024]{1,0:T(8,128)(2,1)}) %all-gather.2.cloned.1.call-update) | async-done | bytes 8388624 | tf_op jit(solution)/shard_map/all_gather | solution.py:1004
  228.8 13.2 %close_layer.1 = (bf16[256,1024]{1,0:T(8,128)(2,1)}, f32[256,1024]{1,0:T(8,128)}, bf16[256,1024]{1,0:T(8,128)(2,1)}, f32[3,1024]{1,0:T(4,128)}, bf16[4096,1024]{1,0:T(8,128)(2,1)}) custom-call(bf16[256,4096]{1,0:T(8,128)(2,1)} %get-tuple-element.120.act_ref, bf16[4096,1024]{1,0:T(8,128)(2,1)} %all-gather.2.cloned.1.call-done.weight_ref, ...), custom_call_target="tpu_custom_call" | custom-call | flops 4294967296 | bytes 19922944 | tf_op jit(solution)/shard_map/close_layer/pallas_call | solution.py:902
  242.4 0.7 copy-done.50
  243.1 7.8 %fusion.13 = (f32[4096]{0:T(1024)S(1)}, bf16[256,4096]{1,0:T(8,128)(2,1)S(1)}) fusion(f32[256,4096]{1,0:T(8,128)} %get-tuple-element.125, bf16[256,1024]{1,0:T(8,128)(2,1)S(1)} %copy-done.50, bf16[4096,1024]{1,0:T(8,128)(2,1)} %all-gather.2.cloned.1.call-done.weight_ref), kind=kOutput, calls=%fused_computation.83 | convolution fusion | flops 2150625280 | bytes 15220736 | tf_op jit(solution)/shard_map/dot_general | solution.py:36
  250.9 8.3 %multiply_reduce_fusion = (f32[1024]{0:T(1024)S(1)}, f32[256]{0:T(256)S(1)}, f32[256]{0:T(256)S(1)}, f32[1024]{0:T(1024)S(1)}, f32[256,1024]{1,0:T(8,128)S(1)}) fusion(f32[256,1024]{1,0:T(8,128)S(1)} %get-tuple-element.214, f32[256]{0:T(256)S(1)} %add_rsqrt_fusion, f32[256]{0:T(256)S(1)} %broadcast_multiply_fusion.4, f32[1024]{0:T(1024)S(1)} %mul.152, ...), kind=kOutput, calls=%fused_computation.32 | convolution fusion | flops 2150102528 | bytes 13647872 | tf_op jit(solution)/shard_map/dot_general | solution.py:36
  259.3 0.4 fusion.11
  259.7 1.1 copy-done.48
  260.9 0.7 convolution_convert_fusion.3.refs_3_
  261.7 0.4 copy-done.14
  262.1 0.3 copy-done.16
  262.5 10.8 %attend_back.2 = (bf16[256,1024]{1,0:T(8,128)(2,1)S(1)}, bf16[512,1024]{1,0:T(8,128)(2,1)S(1)}, bf16[512,1024]{1,0:T(8,128)(2,1)S(1)}) custom-call(bf16[256,1024]{1,0:T(8,128)(2,1)S(1)} %copy-done.14, bf16[512,1024]{1,0:T(8,128)(2,1)S(1)} %copy-done.16, bf16[512,1024]{1,0:T(8,128)(2,1)} %copy-done.17, ...), custom_call_target="tpu_custom_call" | custom-call | flops 1879048192 | bytes 11010048 | tf_op jit(solution)/shard_map/attend_back/pallas_call | solution.py:844
  273.3 1.1 multiply_reduce_fusion.1
  274.5 0.3 fusion.12
  274.9 1.0 copy-done.22
  275.9 0.7 copy-done.46
  276.6 0.8 convolution_convert_fusion.2.refs_5_
  277.4 0.4 copy-done.7
  278.2 15.5 %attend_back.3 = (bf16[256,1024]{1,0:T(8,128)(2,1)S(1)}, bf16[1024,1024]{1,0:T(8,128)(2,1)S(1)}, bf16[1024,1024]{1,0:T(8,128)(2,1)}) custom-call(s32[1024,2]{1,0:T(8,128)S(1)} %bitcast.80, s32[2,256]{1,0:T(2,128)S(1)} %pad_add_fusion.1.refs_1_, bf16[256,1024]{1,0:T(8,128)(2,1)S(1)} %copy-done.12, bf16[1024,1024]{1,0:T(8,128)(2,1)} %copy-done.18, ...), custom_call_target="tpu_custom_call" | custom-call | flops 3758096384 | bytes 18350080 | tf_op jit(solution)/shard_map/attend_back/pallas_call | solution.py:844
  293.7 1.3 copy-done.3
  295.2 2.0 convert_reduce_fusion
  298.5 0.3 stack.56
  298.9 0.8 maximum_maximum_fusion.refs_2_
  299.7 3.8 convolution_add_fusion.2.refs_12_
  303.4 1.3 fusion.17
  305.1 2.3 add_convert_fusion.2
  307.4 2.4 fusion.16
  309.8 3.7 add_convert_fusion
  313.6 144.3 %scatter_grads.1 = (f32[128,1024]{1,0:T(8,128)}, f32[256,1024]{1,0:T(8,128)}, f32[32,4096]{1,0:T(8,128)}, f32[32,1024]{1,0:T(8,128)}, f32[32,1024]{1,0:T(8,128)}...) custom-call(bf16[4,128,1024]{2,1,0:T(8,128)(2,1)} %bitcast.95, ...), custom_call_target="tpu_custom_call" | custom-call | tf_op jit(solution)/shard_map/scatter_grads/pallas_call | solution.py:659
  458.0 5.4 %hand_out.1 = (f32[128,1024]{1,0:T(8,128)}, f32[32,4096]{1,0:T(8,128)}, f32[32,1024]{1,0:T(8,128)}, f32[32,1024]{1,0:T(8,128)}, f32[32,1024]{1,0:T(8,128)}, /*in...) custom-call(f32[128,1024]{1,0:T(8,128)} %get-tuple-element.139.refs_, ...), custom_call_target="tpu_custom_call" | custom-call | tf_op jit(solution)/shard_map/hand_out/pallas_call | solution.py:732
  (159 shorter events, 5.7 us)
Async XLA Ops:
  7.2 221.6 %all-gather.2.cloned.1.call-start = ((), (), s32[]{:S(2)}) async-start(), calls=%async_computation.2 | async-start | bytes 8650752 | tf_op jit(solution)/shard_map/all_gather | solution.py:1004
  8.7 145.3 %copy-start.35 = (s32[1,1024]{1,0:T(1,128)S(1)}, s32[1,1024]{1,0:T(1,128)}, u32[]{:S(2)}) copy-start(s32[1,1024]{1,0:T(1,128)} %param.33) | copy-start | bytes 12292
  8.7 145.3 %copy-start.36 = (s32[1,1024]{1,0:T(1,128)S(1)}, s32[1,1024]{1,0:T(1,128)}, u32[]{:S(2)}) copy-start(s32[1,1024]{1,0:T(1,128)} %param.32) | copy-start | bytes 12292
  8.7 146.4 %copy-start.30 = (bf16[1,256,1024]{2,1,0:T(8,128)(2,1)S(1)}, bf16[1,256,1024]{2,1,0:T(8,128)(2,1)}, u32[]{:S(2)}) copy-start(bf16[1,256,1024]{2,1,0:T(8,128)(2,1)} %param.29) | copy-start | bytes 1572868
  151.8 161.7 %reduce-scatter.3.cloned.1.call-start = ((), (), s32[]{:S(2)}) async-start(), calls=%async_computation.3 | async-start | bytes 9437184 | tf_op jit(solution)/shard_map/reduce_scatter | solution.py:1062
  154.3 8.1 %copy-start.9 = (s32[2,1024]{0,1:T(8,128)}, s32[2,1024]{0,1:T(8,128)S(1)}, u32[]{:S(2)}) copy-start(s32[2,1024]{0,1:T(8,128)S(1)} %copy.68) | copy-start | bytes 24580
  154.4 3.2 copy-start.24
  155.1 2.5 copy-start.39
  157.6 4.8 %copy-start.11 = (bf16[256,1024]{1,0:T(8,128)(2,1)}, bf16[256,1024]{1,0:T(8,128)(2,1)S(1)}, u32[]{:S(2)}) copy-start(bf16[256,1024]{1,0:T(8,128)(2,1)S(1)} %fusion.9.refs_2_) | copy-start | bytes 1572868
  157.7 2.4 copy-start.37
  160.0 2.4 copy-start.18
  162.4 15.0 %copy-start.19 = (bf16[1024,1024]{1,0:T(8,128)(2,1)}, bf16[1024,1024]{1,0:T(8,128)(2,1)S(1)}, u32[]{:S(2)}) copy-start(bf16[1024,1024]{1,0:T(8,128)(2,1)S(1)} %add_convert_fusion.1.refs_4_) | copy-start | bytes 6291460
  162.4 14.9 %copy-start.45 = (bf16[2,2,2,4,32,1024]{5,4,3,2,1,0:T(8,128)(2,1)S(1)}, bf16[2,2,2,4,32,1024]{5,4,3,2,1,0:T(8,128)(2,1)}, u32[]{:S(2)}) copy-start(bf16[2,2,2,4,32,1024]{5,4,3,2,1,0:T(8,128)(2,1)} %get-tuple-element.111) | copy-start | bytes 6291460
  178.2 2.9 copy-start.20
  178.2 2.2 copy-start.31
  178.7 15.4 %copy-start.28 = (bf16[256,1024]{1,0:T(8,128)(2,1)}, bf16[256,1024]{1,0:T(8,128)(2,1)S(1)}, u32[]{:S(2)}) copy-start(bf16[256,1024]{1,0:T(8,128)(2,1)S(1)} %add_convert_fusion.5.refs_7_) | copy-start | bytes 1572868
  178.7 2.4 copy-start.33
  178.7 2.5 copy-start.43
  181.1 3.1 copy-start.13
  181.3 1.6 copy-start.41
  182.6 1.6 copy-start.15
  182.9 11.3 %copy-start.47 = (bf16[2,2,2,4,32,1024]{5,4,3,2,1,0:T(8,128)(2,1)S(1)}, bf16[2,2,2,4,32,1024]{5,4,3,2,1,0:T(8,128)(2,1)}, u32[]{:S(2)}) copy-start(bf16[2,2,2,4,32,1024]{5,4,3,2,1,0:T(8,128)(2,1)} %get-tuple-element.117) | copy-start | bytes 6291460
  182.9 12.7 %slice-start = ((s8[8388608]{0:T(1024)(128)(4,1)}), s8[4194304]{0:T(1024)(128)(4,1)S(1)}, s32[]{:S(2)}) async-start(s8[8388608]{0:T(1024)(128)(4,1)} %bitcast.110), calls=%async_computation.5 | async-start | bytes 8388608
  184.2 10.8 %copy-start.17 = (bf16[512,1024]{1,0:T(8,128)(2,1)}, bf16[512,1024]{1,0:T(8,128)(2,1)S(1)}, u32[]{:S(2)}) copy-start(bf16[512,1024]{1,0:T(8,128)(2,1)S(1)} %add_convert_fusion.3.refs_2_) | copy-start | bytes 3145732
  184.2 11.4 %slice-start.1 = ((s8[8388608]{0:T(1024)(128)(4,1)}), s8[4194304]{0:T(1024)(128)(4,1)S(1)}, s32[]{:S(2)}) async-start(s8[8388608]{0:T(1024)(128)(4,1)} %bitcast.110), calls=%async_computation.6 | async-start | bytes 8388608
  193.5 68.2 %copy-start.8 = (bf16[256,1024]{1,0:T(8,128)(2,1)}, bf16[256,1024]{1,0:T(8,128)(2,1)S(1)}, u32[]{:S(2)}) copy-start(bf16[256,1024]{1,0:T(8,128)(2,1)S(1)} %get-tuple-element.116.refs_4_.refs_5_) | copy-start | bytes 1572868
  195.6 5.9 %copy-start.29 = (bf16[256,1024]{1,0:T(8,128)(2,1)}, bf16[256,1024]{1,0:T(8,128)(2,1)S(1)}, u32[]{:S(2)}) copy-start(bf16[256,1024]{1,0:T(8,128)(2,1)S(1)} %add_convert_fusion.4.stream_ref.refs_3_) | copy-start | bytes 1572868
  242.1 215.9 %reduce-scatter.5.cloned.1.call-start = ((), (), s32[]{:S(2)}) async-start(), calls=%async_computation.4 | async-start | bytes 1310720 | tf_op jit(solution)/shard_map/reduce_scatter | solution.py:1137
  243.1 7.8 %copy-start.49 = (f32[256,1024]{1,0:T(8,128)S(1)}, f32[256,1024]{1,0:T(8,128)}, u32[]{:S(2)}) copy-start(f32[256,1024]{1,0:T(8,128)} %get-tuple-element.123) | copy-start | bytes 3145732
  250.9 8.4 %copy-start.25 = (bf16[256,4096]{1,0:T(8,128)(2,1)}, bf16[256,4096]{1,0:T(8,128)(2,1)S(1)}, u32[]{:S(2)}) copy-start(bf16[256,4096]{1,0:T(8,128)(2,1)S(1)} %get-tuple-element.208.refs_4_) | copy-start | bytes 6291460
  259.3 1.6 copy-start.48
  260.9 1.6 copy-start.16
  262.4 10.9 %copy-start.21 = (f32[256,1024]{1,0:T(8,128)S(1)}, f32[256,1024]{1,0:T(8,128)}, u32[]{:S(2)}) copy-start(f32[256,1024]{1,0:T(8,128)} %copy-done.20) | copy-start | bytes 3145732
  262.4 10.9 %copy-start.32 = (bf16[2,2,2,4,32,1024]{5,4,3,2,1,0:T(8,128)(2,1)S(1)}, bf16[2,2,2,4,32,1024]{5,4,3,2,1,0:T(8,128)(2,1)}, u32[]{:S(2)}) copy-start(bf16[2,2,2,4,32,1024]{5,4,3,2,1,0:T(8,128)(2,1)} %get-tuple-element.112) | copy-start | bytes 6291460
  273.3 24.2 %copy-start.1 = (bf16[256,1024]{1,0:T(8,128)(2,1)}, bf16[256,1024]{1,0:T(8,128)(2,1)S(1)}, u32[]{:S(2)}) copy-start(bf16[256,1024]{1,0:T(8,128)(2,1)S(1)} %get-tuple-element.127.refs_8_) | copy-start | bytes 1572868
  273.3 30.1 %copy-start.5 = (bf16[512,1024]{1,0:T(8,128)(2,1)}, bf16[512,1024]{1,0:T(8,128)(2,1)S(1)}, u32[]{:S(2)}) copy-start(bf16[512,1024]{1,0:T(8,128)(2,1)S(1)} %get-tuple-element.131.refs_10_) | copy-start | bytes 3145732
  273.3 31.4 %copy-start.2 = (bf16[512,1024]{1,0:T(8,128)(2,1)}, bf16[512,1024]{1,0:T(8,128)(2,1)S(1)}, u32[]{:S(2)}) copy-start(bf16[512,1024]{1,0:T(8,128)(2,1)S(1)} %get-tuple-element.132.refs_11_) | copy-start | bytes 3145732
  274.5 2.1 copy-start.46
  276.6 1.4 copy-start.10
  276.6 1.6 copy-start.12
  295.0 4.7 copy-start
  295.0 3.2 copy-start.34
  299.7 3.8 copy-start.44
  303.4 1.6 copy-start.42
  305.1 2.3 copy-start.4
  305.1 2.4 copy-start.40
  307.4 2.4 copy-start.23
  307.4 2.4 copy-start.38
  (8 other events, 8.2 us)
Sparse Core Ops, SparseCore 0:
  152.0 76.7 all-gather.1
  242.2 69.8 reduce-scatter.2
  314.5 38.4 reduce-scatter.4

commit v8 on v7

--- a/solution.py
+++ b/solution.py
@@ -300,7 +300,7 @@
 
 
 def gather_all(cube, arrays, kinds, casts, stays, collective_id):
-    pieces = cut_columns(kinds, arrays, 0.3, 1.0)
+    pieces = cut_columns(kinds, arrays, 0.4, 1.0)
     outs = [
         jax.ShapeDtypeStruct(
             cube.lead(full) + array.shape, BF if index in casts else array.dtype
@@ -537,7 +537,7 @@
             copy.wait_send()
 
 
-RING = 6
+RING = 8
 
 
 def scatter_kernel(cube, pieces, products, operands, *refs):
@@ -599,7 +599,7 @@
         )
         refs = refs[taken:]
     meet(cube, here)
-    in_slots([stages for stages, _ in plans], 4)
+    in_slots([stages for stages, _ in plans], 6)
     for _, finish in plans:
         finish()
     if ring is not None:
@@ -620,7 +620,7 @@
 
 
 def scatter_group(cube, arrays, kinds, collective_id):
-    pieces = cut_columns(kinds, arrays, 0.0, 0.6)
+    pieces = cut_columns(kinds, arrays, 0.0, 0.7)
     outs = [jax.ShapeDtypeStruct(array.shape[-2:], F32) for array in arrays]
     scratch = []
     for array, full, _, _, cols in pieces:

time: 476 us -> 469 us (0.985)
  Pallas kernels: 356 us -> 347 us
    pallas_call x1, Pallas kernels: 144 us -> 137 us  [scatter_group(): pl.pallas_call(functools.partial(scatter_kernel, cube, pieces, products,...]
  transfers between devices with their start and end apart: 3 -> 3, of which waited for: 1 -> 1; matrix products, arithmetic and copies ran while one was open for 13% -> 13% of each run, Pallas kernels for 41% -> 40%
where the time goes in v8:
time: 469 us; the launch traced here: 463 us
  Pallas kernels  347 us (74%)
  matrix products  50.1 us (11%)
  waiting for transfers between devices  29 us (6%)
  local copies, waits for them, and re-layouts  15.1 us (3%)
  between operations  14.9 us (3%)
  other arithmetic  5.72 us (1%)
    pallas_call x1, Pallas kernels, gather_all(): pl.pallas_call(functools.partial(gather_kernel, cube, pieces, casts), out...  142 us
    pallas_call x1, Pallas kernels, scatter_group(): pl.pallas_call(functools.partial(scatter_kernel, cube, pieces, products,...  137 us
    pallas_call x4, Pallas kernels, attend_call(): pl.pallas_call(functools.partial(attend_back_kernel if back else attend_k...  50.2 us
    dot_general x10, matrix products, right_trans(): lax.dot_general(left_arg, right_arg, (((1,), (1,)), ((), ())), preferred_...  32.2 us
    all_gather x1, waiting for transfers between devices, local(): reduce_mat = lax.all_gather(late, ('dp', 'seq'), axis=0, tiled=True)  28.9 us
    dot_general x9, matrix products, matmul(): return jnp.dot(left_arg, right_arg, preferred_element_type=F32)  17.9 us
    pallas_call x1, Pallas kernels, close_layer(): pl.pallas_call(functools.partial(close_kernel, steps), grid=(2 * steps,),...  13.2 us
    unnamed x107, local copies, waits for them, and re-layouts  10.1 us
  transfers between devices with their start and end apart: 3, of which 1 were waited for; matrix products, arithmetic and copies ran while one was open for 13% of the time, Pallas kernels for 40%

profile of v8, /device:TPU:0, one launch (start us, length us, event | category | flops | bytes accessed | tf_op | source)
XLA Modules:
  0.0 462.9 jit_solution(18096066658176647365)
XLA Ops:
  7.3 1.5 concatenate.20
  8.7 141.6 %gather_weights.1 = (bf16[4,256,1024]{2,1,0:T(8,128)(2,1)}, bf16[4,128,1024]{2,1,0:T(8,128)(2,1)}, bf16[2,2,2,4,32,1024]{5,4,3,2,1,0:T(8,128)(2,1)}, bf16[2,2,2,...) custom-call(bf16[256,1024]{1,0:T(8,128)(2,1)} %bitcast.88, ...), custom_call_target="tpu_custom_call" | custom-call | tf_op jit(solution)/shard_map/gather_weights/pallas_call | solution.py:312
  150.3 0.6 reduce-scatter.3.cloned.1.call-start
  150.9 0.9 copy.76
  152.0 0.6 slice_reduce_fusion.2
  153.8 2.5 fusion.9.refs_2_
  156.4 2.3 convolution_convert_fusion.refs_3_
  158.7 2.3 add_convert_fusion.1.refs_4_
  161.1 14.5 %attend.2 = (bf16[256,1024]{1,0:T(8,128)(2,1)S(1)}, f32[8,2,256]{2,1,0:T(2,128)S(1)}) custom-call(s32[1024,2]{1,0:T(8,128)S(1)} %bitcast.79, s32[2,256]{1,0:T(2,128)S(1)} %pad_add_fusion.1.refs_1_, bf16[256,1024]{1,0:T(8,128)(2,1)S(1)} %fusion.9.refs_2_, bf16[1024,1024]{1,0:T(8,128)(2,1)S(1)} %convolution_convert_fusion.refs_3_, ...), custom_call_target="tpu_custom_call" | custom-call | flops 1073741824 | bytes 5242880 | tf_op jit(solution)/shard_map/attend/pallas_call | solution.py:844
  175.6 0.8 fusion.14
  177.0 1.8 copy-done.31
  178.8 0.7 fusion.7.refs_0_
  179.8 1.3 convolution_convert_fusion.1.refs_1_
  181.0 0.3 copy-done.41
  181.3 1.3 add_convert_fusion.3.refs_2_
  182.7 9.3 %attend.3 = (bf16[256,1024]{1,0:T(8,128)(2,1)S(1)}, f32[8,2,256]{2,1,0:T(2,128)S(1)}) custom-call(bf16[256,1024]{1,0:T(8,128)(2,1)S(1)} %fusion.7.refs_0_, bf16[512,1024]{1,0:T(8,128)(2,1)S(1)} %convolution_convert_fusion.1.refs_1_, bf16[512,1024]{1,0:T(8,128)(2,1)S(1)} %add_convert_fusion.3.refs_2_), custom_call_target="tpu_custom_call" | custom-call | flops 536870912 | bytes 3145728 | tf_op jit(solution)/shard_map/attend/pallas_call | solution.py:844
  191.9 0.7 pad_maximum_fusion.vec_ref
  192.6 0.8 fusion.15
  194.1 5.9 %multiply_convert_fusion = (bf16[256,4096]{1,0:T(8,128)(2,1)}, f32[256,4096]{1,0:T(8,128)}) fusion(f32[4096]{0:T(1024)S(1)} %slice_bitcast_fusion, bf16[256,1024]{1,0:T(8,128)(2,1)S(1)} %add_convert_fusion.4.stream_ref.refs_3_, bf16[1024,4096]{1,0:T(8,128)(2,1)S(1)} %bitcast.112), kind=kOutput, calls=%fused_computation.8 | convolution fusion | flops 2159017984 | bytes 15220736 | tf_op jit(solution)/shard_map/dot_general | solution.py:26
  200.0 28.9 %all-gather.2.cloned.1.call-done.weight_ref = bf16[4096,1024]{1,0:T(8,128)(2,1)} async-done(((bf16[128,1024]{1,0:T(8,128)(2,1)}), bf16[4096,1024]{1,0:T(8,128)(2,1)}) %all-gather.2.cloned.1.call-update) | async-done | bytes 8388624 | tf_op jit(solution)/shard_map/all_gather | solution.py:1004
  228.9 13.2 %close_layer.1 = (bf16[256,1024]{1,0:T(8,128)(2,1)}, f32[256,1024]{1,0:T(8,128)}, bf16[256,1024]{1,0:T(8,128)(2,1)}, f32[3,1024]{1,0:T(4,128)}, bf16[4096,1024]{1,0:T(8,128)(2,1)}) custom-call(bf16[256,4096]{1,0:T(8,128)(2,1)} %get-tuple-element.120.act_ref, bf16[4096,1024]{1,0:T(8,128)(2,1)} %all-gather.2.cloned.1.call-done.weight_ref, ...), custom_call_target="tpu_custom_call" | custom-call | flops 4294967296 | bytes 19922944 | tf_op jit(solution)/shard_map/close_layer/pallas_call | solution.py:902
  242.6 0.7 copy-done.50
  243.2 7.8 %fusion.13 = (f32[4096]{0:T(1024)S(1)}, bf16[256,4096]{1,0:T(8,128)(2,1)S(1)}) fusion(f32[256,4096]{1,0:T(8,128)} %get-tuple-element.125, bf16[256,1024]{1,0:T(8,128)(2,1)S(1)} %copy-done.50, bf16[4096,1024]{1,0:T(8,128)(2,1)} %all-gather.2.cloned.1.call-done.weight_ref), kind=kOutput, calls=%fused_computation.83 | convolution fusion | flops 2150625280 | bytes 15220736 | tf_op jit(solution)/shard_map/dot_general | solution.py:36
  251.0 8.3 %multiply_reduce_fusion = (f32[1024]{0:T(1024)S(1)}, f32[256]{0:T(256)S(1)}, f32[256]{0:T(256)S(1)}, f32[1024]{0:T(1024)S(1)}, f32[256,1024]{1,0:T(8,128)S(1)}) fusion(f32[256,1024]{1,0:T(8,128)S(1)} %get-tuple-element.214, f32[256]{0:T(256)S(1)} %add_rsqrt_fusion, f32[256]{0:T(256)S(1)} %broadcast_multiply_fusion.4, f32[1024]{0:T(1024)S(1)} %mul.152, ...), kind=kOutput, calls=%fused_computation.32 | convolution fusion | flops 2150102528 | bytes 13647872 | tf_op jit(solution)/shard_map/dot_general | solution.py:36
  259.4 0.4 fusion.11
  259.9 1.1 copy-done.48
  261.0 0.7 convolution_convert_fusion.3.refs_3_
  261.8 0.4 copy-done.14
  262.2 0.3 copy-done.16
  262.6 10.8 %attend_back.2 = (bf16[256,1024]{1,0:T(8,128)(2,1)S(1)}, bf16[512,1024]{1,0:T(8,128)(2,1)S(1)}, bf16[512,1024]{1,0:T(8,128)(2,1)S(1)}) custom-call(bf16[256,1024]{1,0:T(8,128)(2,1)S(1)} %copy-done.14, bf16[512,1024]{1,0:T(8,128)(2,1)S(1)} %copy-done.16, bf16[512,1024]{1,0:T(8,128)(2,1)} %copy-done.17, ...), custom_call_target="tpu_custom_call" | custom-call | flops 1879048192 | bytes 11010048 | tf_op jit(solution)/shard_map/attend_back/pallas_call | solution.py:844
  273.5 1.1 multiply_reduce_fusion.1
  274.6 0.3 fusion.12
  275.0 1.0 copy-done.22
  276.0 0.7 copy-done.46
  276.7 0.8 convolution_convert_fusion.2.refs_5_
  277.6 0.4 copy-done.7
  278.3 15.7 %attend_back.3 = (bf16[256,1024]{1,0:T(8,128)(2,1)S(1)}, bf16[1024,1024]{1,0:T(8,128)(2,1)S(1)}, bf16[1024,1024]{1,0:T(8,128)(2,1)}) custom-call(s32[1024,2]{1,0:T(8,128)S(1)} %bitcast.80, s32[2,256]{1,0:T(2,128)S(1)} %pad_add_fusion.1.refs_1_, bf16[256,1024]{1,0:T(8,128)(2,1)S(1)} %copy-done.12, bf16[1024,1024]{1,0:T(8,128)(2,1)} %copy-done.18, ...), custom_call_target="tpu_custom_call" | custom-call | flops 3758096384 | bytes 18350080 | tf_op jit(solution)/shard_map/attend_back/pallas_call | solution.py:844
  294.0 1.3 copy-done.3
  295.5 2.0 convert_reduce_fusion
  298.8 0.3 stack.56
  299.2 0.8 maximum_maximum_fusion.refs_2_
  300.0 3.8 convolution_add_fusion.2.refs_12_
  303.7 1.3 fusion.17
  305.3 2.3 add_convert_fusion.2
  307.8 2.4 fusion.16
  310.2 3.7 add_convert_fusion
  313.9 136.7 %scatter_grads.1 = (f32[128,1024]{1,0:T(8,128)}, f32[256,1024]{1,0:T(8,128)}, f32[32,4096]{1,0:T(8,128)}, f32[32,1024]{1,0:T(8,128)}, f32[32,1024]{1,0:T(8,128)}...) custom-call(bf16[4,128,1024]{2,1,0:T(8,128)(2,1)} %bitcast.95, ...), custom_call_target="tpu_custom_call" | custom-call | tf_op jit(solution)/shard_map/scatter_grads/pallas_call | solution.py:659
  450.7 5.4 %hand_out.1 = (f32[128,1024]{1,0:T(8,128)}, f32[32,4096]{1,0:T(8,128)}, f32[32,1024]{1,0:T(8,128)}, f32[32,1024]{1,0:T(8,128)}, f32[32,1024]{1,0:T(8,128)}, /*in...) custom-call(f32[128,1024]{1,0:T(8,128)} %get-tuple-element.139.refs_, ...), custom_call_target="tpu_custom_call" | custom-call | tf_op jit(solution)/shard_map/hand_out/pallas_call | solution.py:732
  (159 shorter events, 5.7 us)
Async XLA Ops:
  7.2 221.7 %all-gather.2.cloned.1.call-start = ((), (), s32[]{:S(2)}) async-start(), calls=%async_computation.2 | async-start | bytes 8650752 | tf_op jit(solution)/shard_map/all_gather | solution.py:1004
  8.7 144.0 %copy-start.35 = (s32[1,1024]{1,0:T(1,128)S(1)}, s32[1,1024]{1,0:T(1,128)}, u32[]{:S(2)}) copy-start(s32[1,1024]{1,0:T(1,128)} %param.33) | copy-start | bytes 12292
  8.7 144.0 %copy-start.36 = (s32[1,1024]{1,0:T(1,128)S(1)}, s32[1,1024]{1,0:T(1,128)}, u32[]{:S(2)}) copy-start(s32[1,1024]{1,0:T(1,128)} %param.32) | copy-start | bytes 12292
  8.7 145.1 %copy-start.30 = (bf16[1,256,1024]{2,1,0:T(8,128)(2,1)S(1)}, bf16[1,256,1024]{2,1,0:T(8,128)(2,1)}, u32[]{:S(2)}) copy-start(bf16[1,256,1024]{2,1,0:T(8,128)(2,1)} %param.29) | copy-start | bytes 1572868
  150.3 163.5 %reduce-scatter.3.cloned.1.call-start = ((), (), s32[]{:S(2)}) async-start(), calls=%async_computation.3 | async-start | bytes 9437184 | tf_op jit(solution)/shard_map/reduce_scatter | solution.py:1062
  153.0 8.1 %copy-start.9 = (s32[2,1024]{0,1:T(8,128)}, s32[2,1024]{0,1:T(8,128)S(1)}, u32[]{:S(2)}) copy-start(s32[2,1024]{0,1:T(8,128)S(1)} %copy.68) | copy-start | bytes 24580
  153.1 3.2 copy-start.24
  153.8 2.5 copy-start.39
  156.3 4.8 %copy-start.11 = (bf16[256,1024]{1,0:T(8,128)(2,1)}, bf16[256,1024]{1,0:T(8,128)(2,1)S(1)}, u32[]{:S(2)}) copy-start(bf16[256,1024]{1,0:T(8,128)(2,1)S(1)} %fusion.9.refs_2_) | copy-start | bytes 1572868
  156.4 2.4 copy-start.37
  158.7 2.4 copy-start.18
  161.1 14.5 %copy-start.19 = (bf16[1024,1024]{1,0:T(8,128)(2,1)}, bf16[1024,1024]{1,0:T(8,128)(2,1)S(1)}, u32[]{:S(2)}) copy-start(bf16[1024,1024]{1,0:T(8,128)(2,1)S(1)} %add_convert_fusion.1.refs_4_) | copy-start | bytes 6291460
  161.1 14.5 %copy-start.45 = (bf16[2,2,2,4,32,1024]{5,4,3,2,1,0:T(8,128)(2,1)S(1)}, bf16[2,2,2,4,32,1024]{5,4,3,2,1,0:T(8,128)(2,1)}, u32[]{:S(2)}) copy-start(bf16[2,2,2,4,32,1024]{5,4,3,2,1,0:T(8,128)(2,1)} %get-tuple-element.111) | copy-start | bytes 6291460
  176.4 3.1 copy-start.20
  176.5 2.3 copy-start.31
  177.0 15.6 %copy-start.28 = (bf16[256,1024]{1,0:T(8,128)(2,1)}, bf16[256,1024]{1,0:T(8,128)(2,1)S(1)}, u32[]{:S(2)}) copy-start(bf16[256,1024]{1,0:T(8,128)(2,1)S(1)} %add_convert_fusion.5.refs_7_) | copy-start | bytes 1572868
  177.0 2.5 copy-start.33
  177.0 2.7 copy-start.43
  179.5 3.1 copy-start.13
  179.7 1.6 copy-start.41
  181.0 1.6 copy-start.15
  181.3 11.3 %copy-start.47 = (bf16[2,2,2,4,32,1024]{5,4,3,2,1,0:T(8,128)(2,1)S(1)}, bf16[2,2,2,4,32,1024]{5,4,3,2,1,0:T(8,128)(2,1)}, u32[]{:S(2)}) copy-start(bf16[2,2,2,4,32,1024]{5,4,3,2,1,0:T(8,128)(2,1)} %get-tuple-element.117) | copy-start | bytes 6291460
  181.3 12.7 %slice-start = ((s8[8388608]{0:T(1024)(128)(4,1)}), s8[4194304]{0:T(1024)(128)(4,1)S(1)}, s32[]{:S(2)}) async-start(s8[8388608]{0:T(1024)(128)(4,1)} %bitcast.110), calls=%async_computation.5 | async-start | bytes 8388608
  182.6 10.8 %copy-start.17 = (bf16[512,1024]{1,0:T(8,128)(2,1)}, bf16[512,1024]{1,0:T(8,128)(2,1)S(1)}, u32[]{:S(2)}) copy-start(bf16[512,1024]{1,0:T(8,128)(2,1)S(1)} %add_convert_fusion.3.refs_2_) | copy-start | bytes 3145732
  182.6 11.4 %slice-start.1 = ((s8[8388608]{0:T(1024)(128)(4,1)}), s8[4194304]{0:T(1024)(128)(4,1)S(1)}, s32[]{:S(2)}) async-start(s8[8388608]{0:T(1024)(128)(4,1)} %bitcast.110), calls=%async_computation.6 | async-start | bytes 8388608
  191.9 69.9 %copy-start.8 = (bf16[256,1024]{1,0:T(8,128)(2,1)}, bf16[256,1024]{1,0:T(8,128)(2,1)S(1)}, u32[]{:S(2)}) copy-start(bf16[256,1024]{1,0:T(8,128)(2,1)S(1)} %get-tuple-element.116.refs_4_.refs_5_) | copy-start | bytes 1572868
  194.1 5.9 %copy-start.29 = (bf16[256,1024]{1,0:T(8,128)(2,1)}, bf16[256,1024]{1,0:T(8,128)(2,1)S(1)}, u32[]{:S(2)}) copy-start(bf16[256,1024]{1,0:T(8,128)(2,1)S(1)} %add_convert_fusion.4.stream_ref.refs_3_) | copy-start | bytes 1572868
  242.2 208.4 %reduce-scatter.5.cloned.1.call-start = ((), (), s32[]{:S(2)}) async-start(), calls=%async_computation.4 | async-start | bytes 1310720 | tf_op jit(solution)/shard_map/reduce_scatter | solution.py:1137
  243.2 7.8 %copy-start.49 = (f32[256,1024]{1,0:T(8,128)S(1)}, f32[256,1024]{1,0:T(8,128)}, u32[]{:S(2)}) copy-start(f32[256,1024]{1,0:T(8,128)} %get-tuple-element.123) | copy-start | bytes 3145732
  251.0 8.4 %copy-start.25 = (bf16[256,4096]{1,0:T(8,128)(2,1)}, bf16[256,4096]{1,0:T(8,128)(2,1)S(1)}, u32[]{:S(2)}) copy-start(bf16[256,4096]{1,0:T(8,128)(2,1)S(1)} %get-tuple-element.208.refs_4_) | copy-start | bytes 6291460
  259.4 1.6 copy-start.48
  261.0 1.6 copy-start.16
  262.6 10.9 %copy-start.21 = (f32[256,1024]{1,0:T(8,128)S(1)}, f32[256,1024]{1,0:T(8,128)}, u32[]{:S(2)}) copy-start(f32[256,1024]{1,0:T(8,128)} %copy-done.20) | copy-start | bytes 3145732
  262.6 10.9 %copy-start.32 = (bf16[2,2,2,4,32,1024]{5,4,3,2,1,0:T(8,128)(2,1)S(1)}, bf16[2,2,2,4,32,1024]{5,4,3,2,1,0:T(8,128)(2,1)}, u32[]{:S(2)}) copy-start(bf16[2,2,2,4,32,1024]{5,4,3,2,1,0:T(8,128)(2,1)} %get-tuple-element.112) | copy-start | bytes 6291460
  273.4 24.4 %copy-start.1 = (bf16[256,1024]{1,0:T(8,128)(2,1)}, bf16[256,1024]{1,0:T(8,128)(2,1)S(1)}, u32[]{:S(2)}) copy-start(bf16[256,1024]{1,0:T(8,128)(2,1)S(1)} %get-tuple-element.127.refs_8_) | copy-start | bytes 1572868
  273.4 30.3 %copy-start.5 = (bf16[512,1024]{1,0:T(8,128)(2,1)}, bf16[512,1024]{1,0:T(8,128)(2,1)S(1)}, u32[]{:S(2)}) copy-start(bf16[512,1024]{1,0:T(8,128)(2,1)S(1)} %get-tuple-element.131.refs_10_) | copy-start | bytes 3145732
  273.4 31.6 %copy-start.2 = (bf16[512,1024]{1,0:T(8,128)(2,1)}, bf16[512,1024]{1,0:T(8,128)(2,1)S(1)}, u32[]{:S(2)}) copy-start(bf16[512,1024]{1,0:T(8,128)(2,1)S(1)} %get-tuple-element.132.refs_11_) | copy-start | bytes 3145732
  274.6 2.1 copy-start.46
  276.7 1.4 copy-start.10
  276.7 1.5 copy-start.12
  295.3 4.7 %copy-start = (bf16[256,1024]{1,0:T(8,128)(2,1)}, bf16[256,1024]{1,0:T(8,128)(2,1)S(1)}, u32[]{:S(2)}) copy-start(bf16[256,1024]{1,0:T(8,128)(2,1)S(1)} %get-tuple-element.133.refs_15_) | copy-start | bytes 1572868
  295.3 3.2 copy-start.34
  300.0 3.8 copy-start.44
  303.7 1.6 copy-start.42
  305.3 2.3 copy-start.4
  305.3 2.4 copy-start.40
  307.8 2.4 copy-start.23
  307.8 2.4 copy-start.38
  (8 other events, 8.2 us)
Sparse Core Ops, SparseCore 0:
  150.5 78.4 all-gather.1
  242.3 69.8 reduce-scatter.2
  314.7 37.6 reduce-scatter.4
